TPU v7x, 32 devices: a whole 2x2x4 slice. The times are simulated.
32 devices in a mesh: groups: 2 (over y), ctx: 8 (over z, x), head: 2 (over core).
Axes of the slice: x: 2, y: 2, z: 4, core: 2. Of those that a mesh axis runs over, the one named last changes fastest.
Arguments:
- queries: bfloat16 [4096, 512], P(('groups', 'ctx'), 'head'), parts along dimension 0, may hold values from -5 to 5
- key_input: bfloat16 [4096, 128], P(('groups', 'ctx')), parts along dimension 0, may hold values from -5 to 5
- value_input: bfloat16 [4096, 128], P(('groups', 'ctx')), parts along dimension 0, may hold values from -2.5 to 2.5
- grad_out: bfloat16 [4096, 512], P(('groups', 'ctx'), 'head'), parts along dimension 0, may hold values from -1.5 to 1.5
- doc_lengths: int32 [32], P('groups'), parts along dimension 0, may hold values from 1 to 512, 2048 in all
- stretch_plan: int32 [32], P(('groups', 'ctx')), parts along dimension 0, may hold values from 0 to 15, as said below
Outputs:
- output: bfloat16 [4096, 512], P(('groups', 'ctx'), 'head'), parts along dimension 0
- query_grad: float32 [4096, 512], P(('groups', 'ctx'), 'head'), parts along dimension 0
- key_grad: float32 [4096, 128], P(('groups', 'ctx')), parts along dimension 0
- value_grad: float32 [4096, 128], P(('groups', 'ctx')), parts along dimension 0
There are 2 independent parts, one for each index of `groups`. A program takes and returns all parts, laid end to end along the dimension named above; each array names one. Nothing has to cross between parts.
Inputs may be any that keep to these rules, and one draw needn't show every extreme that they name: A permutation of the stretch numbers: slot j holds stretch stretch_plan[j], and |stretch_plan[j] - j| <= 4 for every slot, with equality for some slot.
All inputs are finite; a program needn't handle non-finite values.
Results may differ from a plain program's by a relative error of at most 0.025.
Values may be sent and summed in bfloat16 or wider, within the bound.
No kernel may reach another device: no remote copies, remote signals or barrier semaphores. Data moves between devices by JAX's collectives and lax.ppermute only.
A program may use at most 64 MiB of HBM per device.

v0:
```python
import math

import jax
import jax.numpy as jnp
from jax import lax
from jax.sharding import PartitionSpec as P

HOPS = 2
DOC_CAP = 4096


neg_large = -1e30


def shortened(value):
    return jax.tree.map(lambda a: a.astype(jnp.bfloat16) if a.dtype == jnp.float32 else a, value)


def from_behind(block, axis, distance):
    devices = range(lax.axis_size(axis))
    route = [((i - distance) % len(devices), i) for i in devices]
    return lax.ppermute(block, axis, route)


def shifted(value, axis, by):
    count = lax.axis_size(axis)
    pairs = [(i, i + by) for i in range(count) if 0 <= i + by < count]
    return lax.ppermute(value, axis, pairs)


def doc_numbers(bounds, places):
    return jnp.sum((bounds[None, :] <= places[:, None]).astype(jnp.int32), axis=1)


def per_device(queries, key_input, value_input, grad_out, doc_lengths, stretch_plan):
    tok_dev = key_input.shape[0]
    head_dim = key_input.shape[1]
    heads_here = queries.shape[1] // head_dim
    query_width = heads_here * head_dim
    stretch_rows = tok_dev // 2
    ctx_size = lax.axis_size("ctx")
    device_index = lax.axis_index("ctx")
    doc_max = min(DOC_CAP, tok_dev * ctx_size // 4)
    reach_blocks = doc_max // tok_dev
    visits = reach_blocks + 2 * HOPS + 1
    inv_root = 1.0 / math.sqrt(head_dim)
    bounds = jnp.cumsum(doc_lengths)

    def shift_blocks(block_pair, hops):
        return jax.tree.map(
            lambda part, own: part.astype(own.dtype),
            from_behind(shortened(block_pair), "ctx", hops),
            block_pair,
        )

    def shift_grads(grad_pair, hops):
        return from_behind(grad_pair, "ctx", hops)

    def first_blocks():
        return (key_input, value_input)

    def add_grads(moving, key_term, value_term):
        return (moving[0] + key_term, moving[1] + value_term)

    both_rows = jnp.concatenate([queries, grad_out], axis=1)
    pieces = []
    for offset in range(-HOPS, HOPS + 1):
        if offset == 0:
            pieces.append(both_rows)
        else:
            pieces.append(shifted(both_rows, "ctx", -offset))
    window = jnp.concatenate(pieces, axis=0)
    first_row = (device_index - HOPS) * tok_dev
    slot_rows = [
        lax.dynamic_slice_in_dim(
            window, stretch_plan[slot_index] * stretch_rows - first_row, stretch_rows, 0
        )
        for slot_index in range(2)
    ]
    local_rows = jnp.concatenate(slot_rows, axis=0)
    query_heads = local_rows[:, :query_width].reshape(tok_dev, heads_here, head_dim)
    grad_heads = local_rows[:, query_width:].reshape(tok_dev, heads_here, head_dim)
    stretch_offsets = jnp.arange(stretch_rows, dtype=jnp.int32)
    query_places = jnp.concatenate(
        [
            stretch_plan[0] * stretch_rows + stretch_offsets,
            stretch_plan[1] * stretch_rows + stretch_offsets,
        ]
    )
    query_docs = doc_numbers(bounds, query_places)
    key_offsets = jnp.arange(tok_dev, dtype=jnp.int32)

    def block_mask(source):
        key_places = source * tok_dev + key_offsets
        key_docs = doc_numbers(bounds, key_places)
        inside = (source >= 0) & (source < ctx_size)
        same_doc = (query_docs[:, None] == key_docs[None, :]) & (
            key_places[None, :] <= query_places[:, None]
        )
        return same_doc & inside

    def masked_scores(block_keys, allowed):
        products = (
            jnp.einsum("phd,td->pht", query_heads, block_keys, preferred_element_type=jnp.float32)
            * inv_root
        )
        return jnp.where(allowed[:, None, :], products, neg_large)

    def stats_terms(stats, block_pair, source):
        allowed = block_mask(source)
        row_top, row_total = stats
        scores = masked_scores(block_pair[0], allowed)
        new_top = jnp.maximum(row_top, jnp.max(scores, axis=2))
        exps = jnp.where(allowed[:, None, :], jnp.exp(scores - new_top[:, :, None]), 0.0)
        row_total = row_total * jnp.exp(row_top - new_top) + jnp.sum(exps, axis=2)
        return (new_top, row_total)

    stats = (
        jnp.full((tok_dev, heads_here), neg_large, jnp.float32),
        jnp.zeros((tok_dev, heads_here), jnp.float32),
    )

    def stats_step(carried, step_number):
        block_pair, stats = carried
        stats = stats_terms(stats, block_pair, device_index + HOPS - step_number)
        stored = None
        return ((shift_blocks(block_pair, 1), stats), stored)

    steps_all = jnp.arange(visits - 1, dtype=jnp.int32)
    start_block = shift_blocks(first_blocks(), -HOPS)
    (last_block, stats), stored = lax.scan(stats_step, (start_block, stats), steps_all)
    stats = stats_terms(stats, last_block, device_index + HOPS - (visits - 1))
    row_top, row_total = stats
    log_total = row_top + jnp.log(row_total)

    def value_terms(weighted, block_pair, source):
        allowed = block_mask(source)
        scores = masked_scores(block_pair[0], allowed)
        weights = jnp.where(allowed[:, None, :], jnp.exp(scores - log_total[:, :, None]), 0.0)
        return weighted + jnp.einsum(
            "pht,td->phd",
            weights.astype(jnp.bfloat16),
            block_pair[1],
            preferred_element_type=jnp.float32,
        )

    weighted = jnp.zeros((tok_dev, heads_here, head_dim), jnp.float32)

    def weighted_step(carried, step_number):
        block_pair, total = carried
        total = value_terms(total, block_pair, device_index + HOPS - step_number)
        return ((shift_blocks(block_pair, 1), total), None)

    second_block = shift_blocks(first_blocks(), -HOPS)
    (second_last, weighted), unused = lax.scan(weighted_step, (second_block, weighted), steps_all)
    weighted = value_terms(weighted, second_last, device_index + HOPS - (visits - 1))
    attended = weighted.astype(jnp.bfloat16)
    row_dots = jnp.sum(grad_heads.astype(jnp.float32) * attended.astype(jnp.float32), axis=2)

    def backward_terms(query_acc, block_pair, source):
        allowed = block_mask(source)
        backward_query_acc = query_acc
        scores = masked_scores(block_pair[0], allowed)
        weights = jnp.where(allowed[:, None, :], jnp.exp(scores - log_total[:, :, None]), 0.0)
        value_acc = jnp.einsum(
            "pht,phd->td",
            weights.astype(jnp.bfloat16),
            grad_heads,
            preferred_element_type=jnp.float32,
        )
        grad_weights = jnp.einsum(
            "phd,td->pht", grad_heads, block_pair[1], preferred_element_type=jnp.float32
        )
        grad_scores = (weights * (grad_weights - row_dots[:, :, None])).astype(jnp.bfloat16)
        backward_query_acc = backward_query_acc + jnp.einsum(
            "pht,td->phd", grad_scores, block_pair[0], preferred_element_type=jnp.float32
        )
        key_acc = jnp.einsum(
            "pht,phd->td", grad_scores, query_heads, preferred_element_type=jnp.float32
        )
        return (backward_query_acc, key_acc, value_acc)

    query_acc = jnp.zeros((tok_dev, heads_here, head_dim), jnp.float32)
    moving = (
        jnp.zeros((tok_dev, head_dim), jnp.float32),
        jnp.zeros((tok_dev, head_dim), jnp.float32),
    )

    def backward_step(carried, step_number):
        block_pair, query_acc, moving = carried
        query_acc, key_term, value_term = backward_terms(
            query_acc, block_pair, device_index + HOPS - step_number
        )
        moving = add_grads(moving, key_term, value_term)
        return ((shift_blocks(block_pair, 1), query_acc, shift_grads(moving, 1)), None)

    again_block = shift_blocks(first_blocks(), -HOPS)
    (final_block, query_acc, moving), unused = lax.scan(
        backward_step, (again_block, query_acc, moving), steps_all
    )
    query_acc, key_term, value_term = backward_terms(
        query_acc, final_block, device_index + HOPS - (visits - 1)
    )
    moving = add_grads(moving, key_term, value_term)
    moving = shift_grads(moving, -(reach_blocks + HOPS))
    key_sum, value_sum = lax.psum(moving, "head")
    output = attended.reshape(tok_dev, query_width)
    query_grad = (query_acc * inv_root).reshape(tok_dev, query_width)
    key_grad = key_sum * inv_root
    return (output, query_grad, key_grad, value_sum)


def solution(mesh):
    return jax.shard_map(
        per_device,
        mesh=mesh,
        in_specs=(
            P(("groups", "ctx"), "head"),
            P(("groups", "ctx"), None),
            P(("groups", "ctx"), None),
            P(("groups", "ctx"), "head"),
            P("groups"),
            P(("groups", "ctx")),
        ),
        out_specs=(
            P(("groups", "ctx"), "head"),
            P(("groups", "ctx"), "head"),
            P(("groups", "ctx"), None),
            P(("groups", "ctx"), None),
        ),
        check_vma=False,
    )
```

profile of v0, /device:TPU:1, one launch (start us, length us, event | category | flops | bytes accessed | tf_op | source)
XLA Modules:
  0.0 252.3 jit_solution(7476120381572225535)
XLA Ops:
  9.3 4.0 %collective-permute-start.9 = (bf16[256,512]{0,1:T(8,128)(2,1)S(1)}, bf16[256,512]{0,1:T(8,128)(2,1)S(1)}, u32[]{:S(2)}, u32[]{:S(2)}) collective-permute-start(bf16[256,512]{0,1:T(8,128)(2,1)S(1)} %pad_maximum_fusion), channel_id=1, source_target_pairs={{0,4},{2,6},{4,8},{6,10},{8,12},{10,14},{1,5},{3,7},{5,9},{7,11},{... | collective-permute-start | bytes 786440 | tf_op jit(solution)/shard_map/ppermute | solution.py:28
  13.3 3.1 %collective-permute-start.10 = (bf16[256,512]{0,1:T(8,128)(2,1)S(1)}, bf16[256,512]{0,1:T(8,128)(2,1)S(1)}, u32[]{:S(2)}, u32[]{:S(2)}) collective-permute-start(bf16[256,512]{0,1:T(8,128)(2,1)S(1)} %pad_maximum_fusion), channel_id=1, source_target_pairs={{0,2},{2,4},{4,6},{6,8},{8,10},{10,12},{12,14},{1,3},{3,5},{5,7},{... | collective-permute-start | bytes 786440 | tf_op jit(solution)/shard_map/ppermute | solution.py:28
  17.9 2.1 collective-permute-start.8
  26.6 5.1 %collective-permute-done.11 = bf16[256,512]{0,1:T(8,128)(2,1)S(1)} collective-permute-done((bf16[256,512]{0,1:T(8,128)(2,1)S(1)}, bf16[256,512]{0,1:T(8,128)(2,1)S(1)}, u32[]{:S(2)}, u32[]{:S(2)}) %collective-permute-start.11) | collective-permute-done | bytes 262176 | tf_op jit(solution)/shard_map/ppermute | solution.py:28
  31.7 5.6 %collective-permute-done.12 = bf16[256,512]{0,1:T(8,128)(2,1)S(1)} collective-permute-done((bf16[256,512]{0,1:T(8,128)(2,1)S(1)}, bf16[256,512]{0,1:T(8,128)(2,1)S(1)}, u32[]{:S(2)}, u32[]{:S(2)}) %collective-permute-start.12) | collective-permute-done | bytes 262176 | tf_op jit(solution)/shard_map/ppermute | solution.py:28
  37.6 35.5 %while.55 = (s32[]{:T(128)}, bf16[256,128]{1,0:T(8,128)(2,1)S(1)}, f32[256,2]{0,1:T(2,128)S(1)}, f32[256,2]{0,1:T(2,128)S(1)}, s32[256]{0:T(256)S(1)}, /*index=5...) while((s32[]{:T(128)}, bf16[256,128]{1,0:T(8,128)(2,1)S(1)}, ...), condition=%wide.region_6.7_spmd.clone, body=%wide.region_2.6_spmd.clone.sunk | while | flops 34617864 | bytes 1869110 | solution.py:131
  39.7 3.8 %collective-permute-done = bf16[256,128]{1,0:T(8,128)(2,1)S(1)} collective-permute-done((bf16[256,128]{1,0:T(8,128)(2,1)S(1)}, bf16[256,128]{1,0:T(8,128)(2,1)S(1)}, u32[]{:S(2)}, u32[]{:S(2)}) %collective-permute-start) | collective-permute-done | bytes 65568 | tf_op jit(solution)/shard_map/while/body/eval_jaxpr/ppermute | solution.py:22
  45.5 3.8 %collective-permute-done = bf16[256,128]{1,0:T(8,128)(2,1)S(1)} collective-permute-done((bf16[256,128]{1,0:T(8,128)(2,1)S(1)}, bf16[256,128]{1,0:T(8,128)(2,1)S(1)}, u32[]{:S(2)}, u32[]{:S(2)}) %collective-permute-start) | collective-permute-done | bytes 65568 | tf_op jit(solution)/shard_map/while/body/eval_jaxpr/ppermute | solution.py:22
  51.3 3.8 %collective-permute-done = bf16[256,128]{1,0:T(8,128)(2,1)S(1)} collective-permute-done((bf16[256,128]{1,0:T(8,128)(2,1)S(1)}, bf16[256,128]{1,0:T(8,128)(2,1)S(1)}, u32[]{:S(2)}, u32[]{:S(2)}) %collective-permute-start) | collective-permute-done | bytes 65568 | tf_op jit(solution)/shard_map/while/body/eval_jaxpr/ppermute | solution.py:22
  57.2 3.8 %collective-permute-done = bf16[256,128]{1,0:T(8,128)(2,1)S(1)} collective-permute-done((bf16[256,128]{1,0:T(8,128)(2,1)S(1)}, bf16[256,128]{1,0:T(8,128)(2,1)S(1)}, u32[]{:S(2)}, u32[]{:S(2)}) %collective-permute-start) | collective-permute-done | bytes 65568 | tf_op jit(solution)/shard_map/while/body/eval_jaxpr/ppermute | solution.py:22
  63.1 4.2 %collective-permute-done = bf16[256,128]{1,0:T(8,128)(2,1)S(1)} collective-permute-done((bf16[256,128]{1,0:T(8,128)(2,1)S(1)}, bf16[256,128]{1,0:T(8,128)(2,1)S(1)}, u32[]{:S(2)}, u32[]{:S(2)}) %collective-permute-start) | collective-permute-done | bytes 65568 | tf_op jit(solution)/shard_map/while/body/eval_jaxpr/ppermute | solution.py:22
  69.3 3.8 %collective-permute-done = bf16[256,128]{1,0:T(8,128)(2,1)S(1)} collective-permute-done((bf16[256,128]{1,0:T(8,128)(2,1)S(1)}, bf16[256,128]{1,0:T(8,128)(2,1)S(1)}, u32[]{:S(2)}, u32[]{:S(2)}) %collective-permute-start) | collective-permute-done | bytes 65568 | tf_op jit(solution)/shard_map/while/body/eval_jaxpr/ppermute | solution.py:22
  73.5 40.9 %while.56 = (s32[]{:T(128)}, bf16[256,128]{1,0:T(8,128)(2,1)S(1)}, bf16[256,128]{1,0:T(8,128)(2,1)S(1)}, f32[256,2,128]{2,0,1:T(8,128)S(1)}, s32[256]{0:T(256)S(...) while((s32[]{:T(128)}, bf16[256,128]{1,0:T(8,128)(2,1)S(1)}, ...), condition=%wide.region_12.13_spmd.clone, body=%wide.region_10.12_spmd.clone.sunk | while | flops 68169736 | bytes 1713509 | solution.py:155
  75.6 3.8 %collective-permute-done.1 = bf16[256,128]{1,0:T(8,128)(2,1)S(1)} collective-permute-done((bf16[256,128]{1,0:T(8,128)(2,1)S(1)}, bf16[256,128]{1,0:T(8,128)(2,1)S(1)}, u32[]{:S(2)}, u32[]{:S(2)}) %collective-permute-start.1) | collective-permute-done | bytes 65568 | tf_op jit(solution)/shard_map/while/body/eval_jaxpr/ppermute | solution.py:22
  82.1 3.8 %collective-permute-done.1 = bf16[256,128]{1,0:T(8,128)(2,1)S(1)} collective-permute-done((bf16[256,128]{1,0:T(8,128)(2,1)S(1)}, bf16[256,128]{1,0:T(8,128)(2,1)S(1)}, u32[]{:S(2)}, u32[]{:S(2)}) %collective-permute-start.1) | collective-permute-done | bytes 65568 | tf_op jit(solution)/shard_map/while/body/eval_jaxpr/ppermute | solution.py:22
  88.6 3.8 %collective-permute-done.1 = bf16[256,128]{1,0:T(8,128)(2,1)S(1)} collective-permute-done((bf16[256,128]{1,0:T(8,128)(2,1)S(1)}, bf16[256,128]{1,0:T(8,128)(2,1)S(1)}, u32[]{:S(2)}, u32[]{:S(2)}) %collective-permute-start.1) | collective-permute-done | bytes 65568 | tf_op jit(solution)/shard_map/while/body/eval_jaxpr/ppermute | solution.py:22
  95.2 3.8 %collective-permute-done.1 = bf16[256,128]{1,0:T(8,128)(2,1)S(1)} collective-permute-done((bf16[256,128]{1,0:T(8,128)(2,1)S(1)}, bf16[256,128]{1,0:T(8,128)(2,1)S(1)}, u32[]{:S(2)}, u32[]{:S(2)}) %collective-permute-start.1) | collective-permute-done | bytes 65568 | tf_op jit(solution)/shard_map/while/body/eval_jaxpr/ppermute | solution.py:22
  101.7 4.0 %collective-permute-done.1 = bf16[256,128]{1,0:T(8,128)(2,1)S(1)} collective-permute-done((bf16[256,128]{1,0:T(8,128)(2,1)S(1)}, bf16[256,128]{1,0:T(8,128)(2,1)S(1)}, u32[]{:S(2)}, u32[]{:S(2)}) %collective-permute-start.1) | collective-permute-done | bytes 65568 | tf_op jit(solution)/shard_map/while/body/eval_jaxpr/ppermute | solution.py:22
  108.4 4.8 %collective-permute-done.1 = bf16[256,128]{1,0:T(8,128)(2,1)S(1)} collective-permute-done((bf16[256,128]{1,0:T(8,128)(2,1)S(1)}, bf16[256,128]{1,0:T(8,128)(2,1)S(1)}, u32[]{:S(2)}, u32[]{:S(2)}) %collective-permute-start.1) | collective-permute-done | bytes 65568 | tf_op jit(solution)/shard_map/while/body/eval_jaxpr/ppermute | solution.py:22
  115.2 70.3 %while.57 = (s32[]{:T(128)}, bf16[256,128]{1,0:T(8,128)(2,1)S(1)}, bf16[256,128]{1,0:T(8,128)(2,1)S(1)}, f32[256,2,128]{2,0,1:T(8,128)S(1)}, f32[256,128]{1,0:T(...) while((s32[]{:T(128)}, bf16[256,128]{1,0:T(8,128)(2,1)S(1)}, ...), condition=%wide.region_16.17_spmd.clone, body=%wide.region_14.16_spmd.clone.sunk | while | flops 169291776 | bytes 6106581 | solution.py:198
  118.3 3.7 %collective-permute-done.3 = bf16[256,128]{1,0:T(8,128)(2,1)S(1)} collective-permute-done((bf16[256,128]{1,0:T(8,128)(2,1)S(1)}, bf16[256,128]{1,0:T(8,128)(2,1)S(1)}, u32[]{:S(2)}, u32[]{:S(2)}) %collective-permute-start.3) | collective-permute-done | bytes 65568 | tf_op jit(solution)/shard_map/while/body/eval_jaxpr/ppermute | solution.py:22
  128.7 3.1 %collective-permute-start.6 = (f32[256,128]{1,0:T(8,128)S(1)}, f32[256,128]{1,0:T(8,128)S(1)}, u32[]{:S(2)}, u32[]{:S(2)}) collective-permute-start(f32[256,128]{1,0:T(8,128)S(1)} %fusion.133), channel_id=1, source_target_pairs={{14,0},{0,2},{2,4},{4,6},{6,8},{8,10},{10,12},{12,14},{15,1},{1,3}... | collective-permute-start | bytes 393224 | tf_op jit(solution)/shard_map/while/body/eval_jaxpr/ppermute | solution.py:22
  132.5 2.5 collective-permute-done.5
  136.7 2.8 %collective-permute-start.4 = (bf16[256,128]{1,0:T(8,128)(2,1)S(1)}, bf16[256,128]{1,0:T(8,128)(2,1)S(1)}, u32[]{:S(2)}, u32[]{:S(2)}) collective-permute-start(bf16[256,128]{1,0:T(8,128)(2,1)S(1)} %copy.131), channel_id=1, source_target_pairs={{14,0},{0,2},{2,4},{4,6},{6,8},{8,10},{10,12},{12,14},{15,1},{1,3}... | collective-permute-start | bytes 196616 | tf_op jit(solution)/shard_map/while/body/eval_jaxpr/ppermute | solution.py:22
  145.3 3.1 %collective-permute-done.5 = f32[256,128]{1,0:T(8,128)S(1)} collective-permute-done((f32[256,128]{1,0:T(8,128)S(1)}, f32[256,128]{1,0:T(8,128)S(1)}, u32[]{:S(2)}, u32[]{:S(2)}) %collective-permute-start.5) | collective-permute-done | bytes 131104 | tf_op jit(solution)/shard_map/while/body/eval_jaxpr/ppermute | solution.py:22
  157.5 2.8 %collective-permute-done.5 = f32[256,128]{1,0:T(8,128)S(1)} collective-permute-done((f32[256,128]{1,0:T(8,128)S(1)}, f32[256,128]{1,0:T(8,128)S(1)}, u32[]{:S(2)}, u32[]{:S(2)}) %collective-permute-start.5) | collective-permute-done | bytes 131104 | tf_op jit(solution)/shard_map/while/body/eval_jaxpr/ppermute | solution.py:22
  164.8 2.9 %collective-permute-start.6 = (f32[256,128]{1,0:T(8,128)S(1)}, f32[256,128]{1,0:T(8,128)S(1)}, u32[]{:S(2)}, u32[]{:S(2)}) collective-permute-start(f32[256,128]{1,0:T(8,128)S(1)} %fusion.133), channel_id=1, source_target_pairs={{14,0},{0,2},{2,4},{4,6},{6,8},{8,10},{10,12},{12,14},{15,1},{1,3}... | collective-permute-start | bytes 393224 | tf_op jit(solution)/shard_map/while/body/eval_jaxpr/ppermute | solution.py:22
  168.3 3.2 %collective-permute-done.5 = f32[256,128]{1,0:T(8,128)S(1)} collective-permute-done((f32[256,128]{1,0:T(8,128)S(1)}, f32[256,128]{1,0:T(8,128)S(1)}, u32[]{:S(2)}, u32[]{:S(2)}) %collective-permute-start.5) | collective-permute-done | bytes 131104 | tf_op jit(solution)/shard_map/while/body/eval_jaxpr/ppermute | solution.py:22
  171.6 3.0 %collective-permute-done.6 = f32[256,128]{1,0:T(8,128)S(1)} collective-permute-done((f32[256,128]{1,0:T(8,128)S(1)}, f32[256,128]{1,0:T(8,128)S(1)}, u32[]{:S(2)}, u32[]{:S(2)}) %collective-permute-start.6) | collective-permute-done | bytes 131104 | tf_op jit(solution)/shard_map/while/body/eval_jaxpr/ppermute | solution.py:22
  181.9 2.2 collective-permute-done.5
  190.8 2.8 %collective-permute-done.13 = f32[256,128]{1,0:T(8,128)S(1)} collective-permute-done((f32[256,128]{1,0:T(8,128)S(1)}, f32[256,128]{1,0:T(8,128)S(1)}, u32[]{:S(2)}, u32[]{:S(2)}) %collective-permute-start.13) | collective-permute-done | bytes 131104 | tf_op jit(solution)/shard_map/ppermute | solution.py:22
  196.3 46.1 %all-reduce.3.cloned.1.call-done = (f32[256,128]{1,0:T(8,128)}, f32[256,128]{1,0:T(8,128)}) async-done(((f32[256,128]{1,0:T(8,128)}, f32[256,128]{1,0:T(8,128)}), (f32[256,128]{1,0:T(8,128)}, f32[256,128]{1,0:T(8,128)})) %all-reduce.3.cloned.1.call-update) | async-done | bytes 262160 | tf_op jit(solution)/shard_map/psum | solution.py:206
  (299 shorter events, 78.1 us)
Async XLA Ops:
  7.2 235.2 %all-reduce.3.cloned.1.call-start = ((), (), s32[]{:S(2)}) async-start(), calls=%async_computation | async-start | bytes 524288 | tf_op jit(solution)/shard_map/psum | solution.py:206
  9.3 17.2 %collective-permute-start.9 = (bf16[256,512]{0,1:T(8,128)(2,1)S(1)}, bf16[256,512]{0,1:T(8,128)(2,1)S(1)}, u32[]{:S(2)}, u32[]{:S(2)}) collective-permute-start(bf16[256,512]{0,1:T(8,128)(2,1)S(1)} %pad_maximum_fusion), channel_id=1, source_target_pairs={{0,4},{2,6},{4,8},{6,10},{8,12},{10,14},{1,5},{3,7},{5,9},{7,11},{... | collective-permute-start | bytes 786440 | tf_op jit(solution)/shard_map/ppermute | solution.py:28
  13.3 13.2 %collective-permute-start.10 = (bf16[256,512]{0,1:T(8,128)(2,1)S(1)}, bf16[256,512]{0,1:T(8,128)(2,1)S(1)}, u32[]{:S(2)}, u32[]{:S(2)}) collective-permute-start(bf16[256,512]{0,1:T(8,128)(2,1)S(1)} %pad_maximum_fusion), channel_id=1, source_target_pairs={{0,2},{2,4},{4,6},{6,8},{8,10},{10,12},{12,14},{1,3},{3,5},{5,7},{... | collective-permute-start | bytes 786440 | tf_op jit(solution)/shard_map/ppermute | solution.py:28
  16.4 8.7 %collective-permute-start.7 = (bf16[256,128]{1,0:T(8,128)(2,1)}, bf16[256,128]{1,0:T(8,128)(2,1)S(1)}, u32[]{:S(2)}, u32[]{:S(2)}) collective-permute-start(bf16[256,128]{1,0:T(8,128)(2,1)} %param.13), channel_id=1, source_target_pairs={{4,0},{6,2},{8,4},{10,6},{12,8},{14,10},{0,12},{2,14},{5,1},{7,3},... | collective-permute-start | bytes 196616 | tf_op jit(solution)/shard_map/ppermute | solution.py:22
  17.9 8.6 %collective-permute-start.8 = (bf16[256,128]{1,0:T(8,128)(2,1)}, bf16[256,128]{1,0:T(8,128)(2,1)S(1)}, u32[]{:S(2)}, u32[]{:S(2)}) collective-permute-start(bf16[256,128]{1,0:T(8,128)(2,1)} %param.14), channel_id=1, source_target_pairs={{4,0},{6,2},{8,4},{10,6},{12,8},{14,10},{0,12},{2,14},{5,1},{7,3},... | collective-permute-start | bytes 196616 | tf_op jit(solution)/shard_map/ppermute | solution.py:22
  23.8 7.9 %collective-permute-start.11 = (bf16[256,512]{0,1:T(8,128)(2,1)S(1)}, bf16[256,512]{0,1:T(8,128)(2,1)S(1)}, u32[]{:S(2)}, u32[]{:S(2)}) collective-permute-start(bf16[256,512]{0,1:T(8,128)(2,1)S(1)} %pad_maximum_fusion), channel_id=1, source_target_pairs={{2,0},{4,2},{6,4},{8,6},{10,8},{12,10},{14,12},{3,1},{5,3},{7,5},{... | collective-permute-start | bytes 786440 | tf_op jit(solution)/shard_map/ppermute | solution.py:28
  25.2 12.2 %collective-permute-start.12 = (bf16[256,512]{0,1:T(8,128)(2,1)S(1)}, bf16[256,512]{0,1:T(8,128)(2,1)S(1)}, u32[]{:S(2)}, u32[]{:S(2)}) collective-permute-start(bf16[256,512]{0,1:T(8,128)(2,1)S(1)} %pad_maximum_fusion), channel_id=1, source_target_pairs={{4,0},{6,2},{8,4},{10,6},{12,8},{14,10},{5,1},{7,3},{9,5},{11,7},{... | collective-permute-start | bytes 786440 | tf_op jit(solution)/shard_map/ppermute | solution.py:28
  80.1 6.5 %collective-permute-start.2 = (bf16[256,128]{1,0:T(8,128)(2,1)S(1)}, bf16[256,128]{1,0:T(8,128)(2,1)S(1)}, u32[]{:S(2)}, u32[]{:S(2)}) collective-permute-start(bf16[256,128]{1,0:T(8,128)(2,1)S(1)} %copy.117), channel_id=1, source_target_pairs={{14,0},{0,2},{2,4},{4,6},{6,8},{8,10},{10,12},{12,14},{15,1},{1,3}... | collective-permute-start | bytes 196616 | tf_op jit(solution)/shard_map/while/body/eval_jaxpr/ppermute | solution.py:22
  86.6 6.5 %collective-permute-start.2 = (bf16[256,128]{1,0:T(8,128)(2,1)S(1)}, bf16[256,128]{1,0:T(8,128)(2,1)S(1)}, u32[]{:S(2)}, u32[]{:S(2)}) collective-permute-start(bf16[256,128]{1,0:T(8,128)(2,1)S(1)} %copy.117), channel_id=1, source_target_pairs={{14,0},{0,2},{2,4},{4,6},{6,8},{8,10},{10,12},{12,14},{15,1},{1,3}... | collective-permute-start | bytes 196616 | tf_op jit(solution)/shard_map/while/body/eval_jaxpr/ppermute | solution.py:22
  93.1 6.5 %collective-permute-start.2 = (bf16[256,128]{1,0:T(8,128)(2,1)S(1)}, bf16[256,128]{1,0:T(8,128)(2,1)S(1)}, u32[]{:S(2)}, u32[]{:S(2)}) collective-permute-start(bf16[256,128]{1,0:T(8,128)(2,1)S(1)} %copy.117), channel_id=1, source_target_pairs={{14,0},{0,2},{2,4},{4,6},{6,8},{8,10},{10,12},{12,14},{15,1},{1,3}... | collective-permute-start | bytes 196616 | tf_op jit(solution)/shard_map/while/body/eval_jaxpr/ppermute | solution.py:22
  99.7 6.7 %collective-permute-start.2 = (bf16[256,128]{1,0:T(8,128)(2,1)S(1)}, bf16[256,128]{1,0:T(8,128)(2,1)S(1)}, u32[]{:S(2)}, u32[]{:S(2)}) collective-permute-start(bf16[256,128]{1,0:T(8,128)(2,1)S(1)} %copy.117), channel_id=1, source_target_pairs={{14,0},{0,2},{2,4},{4,6},{6,8},{8,10},{10,12},{12,14},{15,1},{1,3}... | collective-permute-start | bytes 196616 | tf_op jit(solution)/shard_map/while/body/eval_jaxpr/ppermute | solution.py:22
  106.4 6.8 %collective-permute-start.1 = (bf16[256,128]{1,0:T(8,128)(2,1)S(1)}, bf16[256,128]{1,0:T(8,128)(2,1)S(1)}, u32[]{:S(2)}, u32[]{:S(2)}) collective-permute-start(bf16[256,128]{1,0:T(8,128)(2,1)S(1)} %copy.116), channel_id=1, source_target_pairs={{14,0},{0,2},{2,4},{4,6},{6,8},{8,10},{10,12},{12,14},{15,1},{1,3}... | collective-permute-start | bytes 196616 | tf_op jit(solution)/shard_map/while/body/eval_jaxpr/ppermute | solution.py:22
  106.4 8.0 %collective-permute-start.2 = (bf16[256,128]{1,0:T(8,128)(2,1)S(1)}, bf16[256,128]{1,0:T(8,128)(2,1)S(1)}, u32[]{:S(2)}, u32[]{:S(2)}) collective-permute-start(bf16[256,128]{1,0:T(8,128)(2,1)S(1)} %copy.117), channel_id=1, source_target_pairs={{14,0},{0,2},{2,4},{4,6},{6,8},{8,10},{10,12},{12,14},{15,1},{1,3}... | collective-permute-start | bytes 196616 | tf_op jit(solution)/shard_map/while/body/eval_jaxpr/ppermute | solution.py:22
  115.2 6.9 %collective-permute-start.3 = (bf16[256,128]{1,0:T(8,128)(2,1)S(1)}, bf16[256,128]{1,0:T(8,128)(2,1)S(1)}, u32[]{:S(2)}, u32[]{:S(2)}) collective-permute-start(bf16[256,128]{1,0:T(8,128)(2,1)S(1)} %copy.130), channel_id=1, source_target_pairs={{14,0},{0,2},{2,4},{4,6},{6,8},{8,10},{10,12},{12,14},{15,1},{1,3}... | collective-permute-start | bytes 196616 | tf_op jit(solution)/shard_map/while/body/eval_jaxpr/ppermute | solution.py:22
  115.3 8.1 %collective-permute-start.4 = (bf16[256,128]{1,0:T(8,128)(2,1)S(1)}, bf16[256,128]{1,0:T(8,128)(2,1)S(1)}, u32[]{:S(2)}, u32[]{:S(2)}) collective-permute-start(bf16[256,128]{1,0:T(8,128)(2,1)S(1)} %copy.131), channel_id=1, source_target_pairs={{14,0},{0,2},{2,4},{4,6},{6,8},{8,10},{10,12},{12,14},{15,1},{1,3}... | collective-permute-start | bytes 196616 | tf_op jit(solution)/shard_map/while/body/eval_jaxpr/ppermute | solution.py:22
  117.7 6.9 %collective-permute-start.5 = (f32[256,128]{1,0:T(8,128)S(1)}, f32[256,128]{1,0:T(8,128)S(1)}, u32[]{:S(2)}, u32[]{:S(2)}) collective-permute-start(f32[256,128]{1,0:T(8,128)S(1)} %fusion.132), channel_id=1, source_target_pairs={{14,0},{0,2},{2,4},{4,6},{6,8},{8,10},{10,12},{12,14},{15,1},{1,3}... | collective-permute-start | bytes 393224 | tf_op jit(solution)/shard_map/while/body/eval_jaxpr/ppermute | solution.py:22
  118.0 7.9 %collective-permute-start.6 = (f32[256,128]{1,0:T(8,128)S(1)}, f32[256,128]{1,0:T(8,128)S(1)}, u32[]{:S(2)}, u32[]{:S(2)}) collective-permute-start(f32[256,128]{1,0:T(8,128)S(1)} %fusion.133), channel_id=1, source_target_pairs={{14,0},{0,2},{2,4},{4,6},{6,8},{8,10},{10,12},{12,14},{15,1},{1,3}... | collective-permute-start | bytes 393224 | tf_op jit(solution)/shard_map/while/body/eval_jaxpr/ppermute | solution.py:22
  128.4 6.6 %collective-permute-start.5 = (f32[256,128]{1,0:T(8,128)S(1)}, f32[256,128]{1,0:T(8,128)S(1)}, u32[]{:S(2)}, u32[]{:S(2)}) collective-permute-start(f32[256,128]{1,0:T(8,128)S(1)} %fusion.132), channel_id=1, source_target_pairs={{14,0},{0,2},{2,4},{4,6},{6,8},{8,10},{10,12},{12,14},{15,1},{1,3}... | collective-permute-start | bytes 393224 | tf_op jit(solution)/shard_map/while/body/eval_jaxpr/ppermute | solution.py:22
  128.7 7.6 %collective-permute-start.6 = (f32[256,128]{1,0:T(8,128)S(1)}, f32[256,128]{1,0:T(8,128)S(1)}, u32[]{:S(2)}, u32[]{:S(2)}) collective-permute-start(f32[256,128]{1,0:T(8,128)S(1)} %fusion.133), channel_id=1, source_target_pairs={{14,0},{0,2},{2,4},{4,6},{6,8},{8,10},{10,12},{12,14},{15,1},{1,3}... | collective-permute-start | bytes 393224 | tf_op jit(solution)/shard_map/while/body/eval_jaxpr/ppermute | solution.py:22
  136.3 8.9 %collective-permute-start.3 = (bf16[256,128]{1,0:T(8,128)(2,1)S(1)}, bf16[256,128]{1,0:T(8,128)(2,1)S(1)}, u32[]{:S(2)}, u32[]{:S(2)}) collective-permute-start(bf16[256,128]{1,0:T(8,128)(2,1)S(1)} %copy.130), channel_id=1, source_target_pairs={{14,0},{0,2},{2,4},{4,6},{6,8},{8,10},{10,12},{12,14},{15,1},{1,3}... | collective-permute-start | bytes 196616 | tf_op jit(solution)/shard_map/while/body/eval_jaxpr/ppermute | solution.py:22
  136.7 8.6 %collective-permute-start.4 = (bf16[256,128]{1,0:T(8,128)(2,1)S(1)}, bf16[256,128]{1,0:T(8,128)(2,1)S(1)}, u32[]{:S(2)}, u32[]{:S(2)}) collective-permute-start(bf16[256,128]{1,0:T(8,128)(2,1)S(1)} %copy.131), channel_id=1, source_target_pairs={{14,0},{0,2},{2,4},{4,6},{6,8},{8,10},{10,12},{12,14},{15,1},{1,3}... | collective-permute-start | bytes 196616 | tf_op jit(solution)/shard_map/while/body/eval_jaxpr/ppermute | solution.py:22
  141.9 6.6 %collective-permute-start.5 = (f32[256,128]{1,0:T(8,128)S(1)}, f32[256,128]{1,0:T(8,128)S(1)}, u32[]{:S(2)}, u32[]{:S(2)}) collective-permute-start(f32[256,128]{1,0:T(8,128)S(1)} %fusion.132), channel_id=1, source_target_pairs={{14,0},{0,2},{2,4},{4,6},{6,8},{8,10},{10,12},{12,14},{15,1},{1,3}... | collective-permute-start | bytes 393224 | tf_op jit(solution)/shard_map/while/body/eval_jaxpr/ppermute | solution.py:22
  143.4 6.6 %collective-permute-start.6 = (f32[256,128]{1,0:T(8,128)S(1)}, f32[256,128]{1,0:T(8,128)S(1)}, u32[]{:S(2)}, u32[]{:S(2)}) collective-permute-start(f32[256,128]{1,0:T(8,128)S(1)} %fusion.133), channel_id=1, source_target_pairs={{14,0},{0,2},{2,4},{4,6},{6,8},{8,10},{10,12},{12,14},{15,1},{1,3}... | collective-permute-start | bytes 393224 | tf_op jit(solution)/shard_map/while/body/eval_jaxpr/ppermute | solution.py:22
  150.0 6.9 %collective-permute-start.3 = (bf16[256,128]{1,0:T(8,128)(2,1)S(1)}, bf16[256,128]{1,0:T(8,128)(2,1)S(1)}, u32[]{:S(2)}, u32[]{:S(2)}) collective-permute-start(bf16[256,128]{1,0:T(8,128)(2,1)S(1)} %copy.130), channel_id=1, source_target_pairs={{14,0},{0,2},{2,4},{4,6},{6,8},{8,10},{10,12},{12,14},{15,1},{1,3}... | collective-permute-start | bytes 196616 | tf_op jit(solution)/shard_map/while/body/eval_jaxpr/ppermute | solution.py:22
  150.2 7.4 %collective-permute-start.4 = (bf16[256,128]{1,0:T(8,128)(2,1)S(1)}, bf16[256,128]{1,0:T(8,128)(2,1)S(1)}, u32[]{:S(2)}, u32[]{:S(2)}) collective-permute-start(bf16[256,128]{1,0:T(8,128)(2,1)S(1)} %copy.131), channel_id=1, source_target_pairs={{14,0},{0,2},{2,4},{4,6},{6,8},{8,10},{10,12},{12,14},{15,1},{1,3}... | collective-permute-start | bytes 196616 | tf_op jit(solution)/shard_map/while/body/eval_jaxpr/ppermute | solution.py:22
  153.8 6.6 %collective-permute-start.5 = (f32[256,128]{1,0:T(8,128)S(1)}, f32[256,128]{1,0:T(8,128)S(1)}, u32[]{:S(2)}, u32[]{:S(2)}) collective-permute-start(f32[256,128]{1,0:T(8,128)S(1)} %fusion.132), channel_id=1, source_target_pairs={{14,0},{0,2},{2,4},{4,6},{6,8},{8,10},{10,12},{12,14},{15,1},{1,3}... | collective-permute-start | bytes 393224 | tf_op jit(solution)/shard_map/while/body/eval_jaxpr/ppermute | solution.py:22
  154.2 7.6 %collective-permute-start.6 = (f32[256,128]{1,0:T(8,128)S(1)}, f32[256,128]{1,0:T(8,128)S(1)}, u32[]{:S(2)}, u32[]{:S(2)}) collective-permute-start(f32[256,128]{1,0:T(8,128)S(1)} %fusion.133), channel_id=1, source_target_pairs={{14,0},{0,2},{2,4},{4,6},{6,8},{8,10},{10,12},{12,14},{15,1},{1,3}... | collective-permute-start | bytes 393224 | tf_op jit(solution)/shard_map/while/body/eval_jaxpr/ppermute | solution.py:22
  164.2 7.4 %collective-permute-start.5 = (f32[256,128]{1,0:T(8,128)S(1)}, f32[256,128]{1,0:T(8,128)S(1)}, u32[]{:S(2)}, u32[]{:S(2)}) collective-permute-start(f32[256,128]{1,0:T(8,128)S(1)} %fusion.132), channel_id=1, source_target_pairs={{14,0},{0,2},{2,4},{4,6},{6,8},{8,10},{10,12},{12,14},{15,1},{1,3}... | collective-permute-start | bytes 393224 | tf_op jit(solution)/shard_map/while/body/eval_jaxpr/ppermute | solution.py:22
  164.8 9.7 %collective-permute-start.6 = (f32[256,128]{1,0:T(8,128)S(1)}, f32[256,128]{1,0:T(8,128)S(1)}, u32[]{:S(2)}, u32[]{:S(2)}) collective-permute-start(f32[256,128]{1,0:T(8,128)S(1)} %fusion.133), channel_id=1, source_target_pairs={{14,0},{0,2},{2,4},{4,6},{6,8},{8,10},{10,12},{12,14},{15,1},{1,3}... | collective-permute-start | bytes 393224 | tf_op jit(solution)/shard_map/while/body/eval_jaxpr/ppermute | solution.py:22
  174.6 7.3 %collective-permute-start.4 = (bf16[256,128]{1,0:T(8,128)(2,1)S(1)}, bf16[256,128]{1,0:T(8,128)(2,1)S(1)}, u32[]{:S(2)}, u32[]{:S(2)}) collective-permute-start(bf16[256,128]{1,0:T(8,128)(2,1)S(1)} %copy.131), channel_id=1, source_target_pairs={{14,0},{0,2},{2,4},{4,6},{6,8},{8,10},{10,12},{12,14},{15,1},{1,3}... | collective-permute-start | bytes 196616 | tf_op jit(solution)/shard_map/while/body/eval_jaxpr/ppermute | solution.py:22
  177.5 6.6 %collective-permute-start.5 = (f32[256,128]{1,0:T(8,128)S(1)}, f32[256,128]{1,0:T(8,128)S(1)}, u32[]{:S(2)}, u32[]{:S(2)}) collective-permute-start(f32[256,128]{1,0:T(8,128)S(1)} %fusion.132), channel_id=1, source_target_pairs={{14,0},{0,2},{2,4},{4,6},{6,8},{8,10},{10,12},{12,14},{15,1},{1,3}... | collective-permute-start | bytes 393224 | tf_op jit(solution)/shard_map/while/body/eval_jaxpr/ppermute | solution.py:22
  178.0 7.5 %collective-permute-start.6 = (f32[256,128]{1,0:T(8,128)S(1)}, f32[256,128]{1,0:T(8,128)S(1)}, u32[]{:S(2)}, u32[]{:S(2)}) collective-permute-start(f32[256,128]{1,0:T(8,128)S(1)} %fusion.133), channel_id=1, source_target_pairs={{14,0},{0,2},{2,4},{4,6},{6,8},{8,10},{10,12},{12,14},{15,1},{1,3}... | collective-permute-start | bytes 393224 | tf_op jit(solution)/shard_map/while/body/eval_jaxpr/ppermute | solution.py:22
  (21 other events, 116.6 us)
Sparse Core Ops, SparseCore 0:
  194.4 47.9 all-reduce.2
where the time goes:
time: 253 us; the launch traced here: 252 us
  waiting for transfers between devices  148 us (58%)
  starting transfers between devices  34.8 us (14%)
  local copies, waits for them, and re-layouts  19.8 us (8%)
  between operations  15.7 us (6%)
  matrix products  13.8 us (5%)
  loops' own time  13.3 us (5%)
  other arithmetic  7.43 us (3%)
    ppermute x46, waiting for transfers between devices, from_behind(): return lax.ppermute(block, axis, route)  90.8 us
    psum x1, waiting for transfers between devices, per_device(): key_sum, value_sum = lax.psum(moving, 'head')  46.1 us
    ppermute x46, starting transfers between devices, from_behind(): return lax.ppermute(block, axis, route)  25 us
    dynamic_slice x18, local copies, waits for them, and re-layouts, per_device(): lax.scan(stats_step, (start_block, stats), steps_all)  11.1 us
    ppermute x4, waiting for transfers between devices, shifted(): return lax.ppermute(value, axis, pairs)  10.7 us
    ppermute x4, starting transfers between devices, shifted(): return lax.ppermute(value, axis, pairs)  9.76 us
    unnamed x17, local copies, waits for them, and re-layouts  6.14 us
  transfers between devices with their start and end apart: 51, of which 43 were waited for; matrix products, arithmetic and copies ran while one was open for 13% of the time, Pallas kernels for 0%

commit v1 on v0

v1 whole, which is shorter than its diff:
```python
import math

import jax
import jax.numpy as jnp
from jax import lax
from jax.experimental import pallas as pl
from jax.experimental.pallas import tpu as pltpu
from jax.sharding import PartitionSpec as P

DOC_CAP = 4096
NEG = -1e30
CHUNK = 128

VMEM = pl.BlockSpec(memory_space=pltpu.VMEM)
SMEM = pl.BlockSpec(memory_space=pltpu.SMEM)


def nt(a, b):
    return lax.dot_general(a, b, (((1,), (1,)), ((), ())), preferred_element_type=jnp.float32)


def nn(a, b):
    return lax.dot_general(a, b, (((1,), (0,)), ((), ())), preferred_element_type=jnp.float32)


def tn(a, b):
    return lax.dot_general(a, b, (((0,), (0,)), ((), ())), preferred_element_type=jnp.float32)


def fold(a, op):
    rows = a.shape[0] // 8
    parts = a.reshape(rows, 8, a.shape[1])
    return op(parts, axis=0)


def swap_near(n):
    return [(i, i ^ 1) for i in range(n)]


def swap_near_odd(n):
    pairs = [(0, 0), (n - 1, n - 1)]
    for i in range(1, n - 1, 2):
        pairs += [(i, i + 1), (i + 1, i)]
    return pairs


def swap_far(n):
    return [(i, i ^ 2) for i in range(n)]


def swap_far_odd(n):
    pairs = [(0, 1), (1, 0), (n - 2, n - 1), (n - 1, n - 2)]
    for i in range(2, n - 2, 4):
        pairs += [(i, i + 2), (i + 2, i), (i + 1, i + 3), (i + 3, i + 1)]
    return pairs


def attend_kernel(rounds, tok, heads, head_dim):
    inv_root = 1.0 / math.sqrt(head_dim)
    per_block = tok // CHUNK
    width = heads * head_dim

    def kernel(lens, q_ref, g_ref, k_ref, v_ref, mine_ref, other_ref,
               od_ref, own_out, mine_out, other_out, w_ref):
        here = lax.axis_index("ctx")
        side = lax.axis_index("head")
        first = here * tok
        places = first + lax.broadcasted_iota(jnp.int32, (1, tok), 1)
        begin = jnp.zeros((1, tok), jnp.int32)
        bound = jnp.int32(0)
        for i in range(lens.shape[0]):
            bound = bound + lens[i]
            begin = jnp.where(places >= bound, bound, begin)

        def own_chunk(c):
            rows = pl.ds(c * CHUNK, CHUNK)
            return k_ref[rows, :], v_ref[rows, :]

        def far_chunk(ref, r, c):
            rows = pl.ds(c * CHUNK, CHUNK)
            return ref[r, rows, :head_dim], ref[r, rows, head_dim:]

        def each(body, carry):
            for c in range(per_block):
                carry = body(own_chunk(c), first + c * CHUNK, c,
                             (own_out, None, c), carry)
            for which, (ref, out) in enumerate(((mine_ref, mine_out), (other_ref, other_out))):
                def one(r, carry):
                    hop = 2 * r + 1 + (side if which == 0 else 1 - side)
                    base = first - hop * tok
                    for c in range(per_block):
                        slot = per_block * (1 + which * rounds + r) + c
                        carry = body(far_chunk(ref, r, c), base + c * CHUNK, slot,
                                     (out, r, c), carry)
                    return carry
                carry = one(0, carry) if rounds == 1 else lax.fori_loop(0, rounds, one, carry)
            return carry

        q = [q_ref[:, h * head_dim:(h + 1) * head_dim] for h in range(heads)]
        g = [g_ref[:, h * head_dim:(h + 1) * head_dim] for h in range(heads)]

        def scores(kv, base, slot, out, tops):
            at = base + lax.broadcasted_iota(jnp.int32, (CHUNK, tok), 0)
            allowed = (at >= begin) & (at <= places)
            result = []
            for h in range(heads):
                s = jnp.where(allowed, nt(kv[0], q[h]) * inv_root, NEG)
                w_ref[h, slot] = s
                result.append(jnp.maximum(tops[h], fold(s, jnp.max)))
            return tuple(result)

        tops = each(scores, tuple(jnp.full((8, tok), NEG, jnp.float32) for _ in range(heads)))
        tops = [jnp.max(t, axis=0, keepdims=True) for t in tops]

        def exps(kv, base, slot, out, totals):
            result = []
            for h in range(heads):
                e = jnp.exp(w_ref[h, slot] - tops[h])
                w_ref[h, slot] = e
                result.append(totals[h] + fold(e, jnp.sum))
            return tuple(result)

        totals = each(exps, tuple(jnp.zeros((8, tok), jnp.float32) for _ in range(heads)))
        scale = [1.0 / jnp.sum(t, axis=0, keepdims=True) for t in totals]

        def values(kv, base, slot, out, acc):
            result = []
            for h in range(heads):
                w = w_ref[h, slot] * scale[h]
                w_ref[h, slot] = w
                result.append(acc[h] + tn(kv[1], w.astype(jnp.bfloat16)))
            return tuple(result)

        acc = each(values, tuple(jnp.zeros((head_dim, tok), jnp.float32) for _ in range(heads)))
        dots = []
        for h in range(heads):
            attended = acc[h].T.astype(jnp.bfloat16)
            od_ref[:, h * head_dim:(h + 1) * head_dim] = attended
            product = g[h].astype(jnp.float32) * attended.astype(jnp.float32)
            dots.append(jnp.sum(product.T, axis=0, keepdims=True))

        def backward(kv, base, slot, out, acc):
            result = []
            key_term = value_term = None
            for h in range(heads):
                w = w_ref[h, slot]
                ds = (w * (nt(kv[1], g[h]) - dots[h])).astype(jnp.bfloat16)
                result.append(acc[h] + tn(kv[0], ds))
                dk = nn(ds, q[h])
                dv = nn(w.astype(jnp.bfloat16), g[h])
                key_term = dk if h == 0 else key_term + dk
                value_term = dv if h == 0 else value_term + dv
            ref, r, c = out
            rows = pl.ds(c * CHUNK, CHUNK)
            key_term = (key_term * inv_root).astype(ref.dtype)
            value_term = value_term.astype(ref.dtype)
            if r is None:
                ref[rows, :head_dim] = key_term
                ref[rows, head_dim:] = value_term
            else:
                ref[r, rows, :head_dim] = key_term
                ref[r, rows, head_dim:] = value_term
            return tuple(result)

        acc = each(backward, tuple(jnp.zeros((head_dim, tok), jnp.float32) for _ in range(heads)))
        for h in range(heads):
            od_ref[:, width + h * head_dim:width + (h + 1) * head_dim] = (
                (acc[h] * inv_root).T.astype(jnp.bfloat16))

    return kernel


def place_kernel(n, stretch, width):
    def kernel(plan, own, near, near_odd, far, far_odd, x_ref, y_ref,
               out_ref, dq_ref, dk_ref, dv_ref):
        here = lax.axis_index("ctx")
        odd = here % 2
        upper = (here // 2) % 2
        near_odd_src = jnp.clip(here + 2 * odd - 1, 0, n - 1)
        inner = (here >= 2) & (here < n - 2)
        far_odd_src = jnp.where(inner, here + 4 * upper - 2, here + 1 - 2 * odd)
        sources = ((own, here), (near, here + 1 - 2 * odd), (near_odd, near_odd_src),
                   (far, here + 2 - 4 * upper), (far_odd, far_odd_src))
        for slot in range(2):
            wanted = plan[slot]
            rows = pl.ds(pl.multiple_of((wanted % 2) * stretch, stretch), stretch)
            to = pl.ds(slot * stretch, stretch)
            for ref, source in sources:
                @pl.when(wanted // 2 == source)
                def _():
                    out_ref[to, :] = ref[rows, :width]
                    dq_ref[to, :] = ref[rows, width:].astype(jnp.float32)
        half = dk_ref.shape[1]
        dk_ref[...] = x_ref[:, :half] + y_ref[:, :half]
        dv_ref[...] = x_ref[:, half:] + y_ref[:, half:]

    return kernel


def per_device(queries, key_input, value_input, grad_out, doc_lengths, stretch_plan):
    tok, head_dim = key_input.shape
    width = queries.shape[1]
    heads = width // head_dim
    n = lax.axis_size("ctx")
    reach = min(DOC_CAP, tok * n // 4) // tok
    rounds = (reach + 1) // 2
    bf16, f32 = jnp.bfloat16, jnp.float32
    both = ("ctx", "head")
    cross = [(0, 1), (1, 0)]

    def hop_pairs(r, back):
        pairs = []
        for s in range(n):
            for h in range(2):
                to = s + 2 * r + 1 + h
                if to < n:
                    a, b = 2 * s + h, 2 * to + h
                    pairs.append((b, a) if back else (a, b))
        return pairs

    own_kv = jnp.concatenate([key_input, value_input], axis=1)
    mine = jnp.stack([lax.ppermute(own_kv, both, hop_pairs(r, False)) for r in range(rounds)])
    other = lax.ppermute(mine, "head", cross)

    blocks = 1 + 2 * rounds
    od, own_part, mine_part, other_part = pl.pallas_call(
        attend_kernel(rounds, tok, heads, head_dim),
        out_shape=(
            jax.ShapeDtypeStruct((tok, 2 * width), bf16),
            jax.ShapeDtypeStruct((tok, 2 * head_dim), f32),
            jax.ShapeDtypeStruct((rounds, tok, 2 * head_dim), bf16),
            jax.ShapeDtypeStruct((rounds, tok, 2 * head_dim), bf16),
        ),
        in_specs=[SMEM] + [VMEM] * 6,
        out_specs=(VMEM,) * 4,
        scratch_shapes=[pltpu.VMEM((heads, blocks * (tok // CHUNK), CHUNK, tok), f32)],
        compiler_params=pltpu.CompilerParams(vmem_limit_bytes=40 << 20),
        name="attend",
    )(doc_lengths, queries, grad_out, key_input, value_input, mine, other)

    partner = lax.ppermute(other_part, "head", cross)
    back = (mine_part.astype(f32) + partner.astype(f32)).astype(bf16)
    total = own_part
    for r in range(rounds):
        total = total + lax.ppermute(back[r], both, hop_pairs(r, True)).astype(f32)
    moved = [lax.ppermute(od, "ctx", pairs(n))
             for pairs in (swap_near, swap_near_odd, swap_far, swap_far_odd)]
    total_other = lax.ppermute(total, "head", cross)

    output, query_grad, key_grad, value_grad = pl.pallas_call(
        place_kernel(n, tok // 2, width),
        out_shape=(
            jax.ShapeDtypeStruct((tok, width), bf16),
            jax.ShapeDtypeStruct((tok, width), f32),
            jax.ShapeDtypeStruct((tok, head_dim), f32),
            jax.ShapeDtypeStruct((tok, head_dim), f32),
        ),
        in_specs=[SMEM] + [VMEM] * 7,
        out_specs=(VMEM,) * 4,
        name="place",
    )(stretch_plan, od, *moved, total, total_other)
    return (output, query_grad, key_grad, value_grad)


def solution(mesh):
    return jax.shard_map(
        per_device,
        mesh=mesh,
        in_specs=(
            P(("groups", "ctx"), "head"),
            P(("groups", "ctx"), None),
            P(("groups", "ctx"), None),
            P(("groups", "ctx"), "head"),
            P("groups"),
            P(("groups", "ctx")),
        ),
        out_specs=(
            P(("groups", "ctx"), "head"),
            P(("groups", "ctx"), "head"),
            P(("groups", "ctx"), None),
            P(("groups", "ctx"), None),
        ),
        check_vma=False,
    )
```

time: 253 us -> 43.9 us (0.17)
  the two profiles are of different devices: /device:TPU:1 before, /device:TPU:24 now
where the time goes in v1:
time: 43.9 us; the launch traced here: 43.7 us
  waiting for transfers between devices  22.6 us (51%)
  starting transfers between devices  11.3 us (26%)
  Pallas kernels  5.74 us (13%)
  local copies, waits for them, and re-layouts  2.28 us (5%)
  other arithmetic  0.99 us (2%)
  between operations  0.81 us (2%)
    ppermute x4, waiting for transfers between devices, per_device(): lax.ppermute(od, 'ctx', pairs(n))  14.8 us
    ppermute x4, starting transfers between devices, per_device(): lax.ppermute(od, 'ctx', pairs(n))  5.52 us
    ppermute x1, waiting for transfers between devices, per_device(): lax.ppermute(own_kv, both, hop_pairs(r, False))  4.65 us
    ppermute x1, starting transfers between devices, per_device(): lax.ppermute(own_kv, both, hop_pairs(r, False))  3.4 us
    pallas_call x1, Pallas kernels, per_device(): pl.pallas_call(attend_kernel(rounds, tok, heads, head_dim), out_shape=(ja...  3.36 us
    pallas_call x1, Pallas kernels, per_device(): pl.pallas_call(place_kernel(n, tok // 2, width), out_shape=(jax.ShapeDtyp...  2.38 us
    unnamed x24, local copies, waits for them, and re-layouts  2.28 us
    ppermute x1, starting transfers between devices, per_device(): total = total + lax.ppermute(back[r], both, hop_pairs(r, True)).astype(f32)  2.09 us
  transfers between devices with their start and end apart: 9, of which 6 were waited for; matrix products, arithmetic and copies ran while one was open for 0% of the time, Pallas kernels for 0%

profile of v1, /device:TPU:24, one launch (start us, length us, event | category | flops | bytes accessed | tf_op | source)
XLA Modules:
  0.0 43.7 jit_solution(6331743179003390619)
XLA Ops:
  0.6 0.0 copy-start.1
  0.6 0.0 copy-start
  0.7 0.0 copy-start.3
  0.7 0.9 %pad_maximum_fusion = bf16[256,256]{1,0:T(8,128)(2,1)S(1)} fusion(bf16[256,128]{1,0:T(8,128)(2,1)} %v_ref.1, bf16[256,128]{1,0:T(8,128)(2,1)} %k_ref.1), kind=kLoop, calls=%fused_computation.3 | loop fusion | flops 262144 | bytes 262144 | tf_op jit(solution)/shard_map/concatenate | solution.py:221
  1.6 0.0 copy-start.5
  1.6 3.4 %collective-permute-start = (bf16[256,256]{1,0:T(8,128)(2,1)S(1)}, bf16[256,256]{1,0:T(8,128)(2,1)S(1)}, u32[]{:S(2)}, u32[]{:S(2)}) collective-permute-start(bf16[256,256]{1,0:T(8,128)(2,1)S(1)} %pad_maximum_fusion), channel_id=1, source_target_pairs={{0,2},{1,5},{2,4},{3,7},{4,6},{5,9},{6,8},{7,11},{8,10},{9,13},{10... | collective-permute-start | bytes 393224 | tf_op jit(solution)/shard_map/ppermute | solution.py:222
  5.0 4.7 %collective-permute-done = bf16[256,256]{1,0:T(8,128)(2,1)S(1)} collective-permute-done((bf16[256,256]{1,0:T(8,128)(2,1)S(1)}, bf16[256,256]{1,0:T(8,128)(2,1)S(1)}, u32[]{:S(2)}, u32[]{:S(2)}) %collective-permute-start) | collective-permute-done | bytes 131104 | tf_op jit(solution)/shard_map/ppermute | solution.py:222
  9.7 0.0 collective-permute-start.1
  9.7 1.3 %collective-permute-done.1.other_ref = bf16[1,256,256]{2,1,0:T(8,128)(2,1)S(1)} collective-permute-done((bf16[1,256,256]{2,1,0:T(8,128)(2,1)S(1)}, bf16[1,256,256]{2,1,0:T(8,128)(2,1)S(1)}, u32[]{:S(2)}, u32[]{:S(2)}) %collective-permute-start.1) | collective-permute-done | bytes 131104 | tf_op jit(solution)/shard_map/ppermute | solution.py:223
  11.0 0.0 copy-done.1
  11.0 0.0 copy-done
  11.0 0.0 copy-done.3
  11.0 0.0 copy-start.4
  11.0 0.9 %copy-done.4 = bf16[256,256]{1,0:T(8,128)(2,1)S(1)} copy-done((bf16[256,256]{1,0:T(8,128)(2,1)S(1)}, bf16[256,256]{1,0:T(8,128)(2,1)}, u32[]{:S(2)}) %copy-start.4) | copy-done | bytes 131096
  11.9 3.4 %attend.1 = (bf16[256,512]{1,0:T(8,128)(2,1)S(1)}, f32[256,256]{1,0:T(8,128)S(1)}, bf16[1,256,256]{2,1,0:T(8,128)(2,1)S(1)}, bf16[1,256,256]{2,1,0:T(8,128)(2,1)S(1)}) custom-call(s32[16]{0:T(128)S(1)} %copy-done.5, bf16[256,256]{1,0:T(8,128)(2,1)S(1)} %copy-done.3, bf16[256,256]{1,0:T(8,128)(2,1)S(1)} %copy-done.4, bf16[256,128]{1,0:T(8,128)(2,1)S(1)} %copy-done, ...), custom_call_target="tpu_custom_call" | custom-call | tf_op jit(solution)/shard_map/attend/pallas_call | solution.py:226
  15.3 0.2 collective-permute-start.6
  15.5 1.2 %collective-permute-done.6 = bf16[1,256,256]{2,1,0:T(8,128)(2,1)S(1)} collective-permute-done((bf16[1,256,256]{2,1,0:T(8,128)(2,1)S(1)}, bf16[1,256,256]{2,1,0:T(8,128)(2,1)S(1)}, u32[]{:S(2)}, u32[]{:S(2)}) %collective-permute-start.6) | collective-permute-done | bytes 131104 | tf_op jit(solution)/shard_map/ppermute | solution.py:241
  16.8 2.1 %collective-permute-start.7 = (bf16[256,256]{1,0:T(8,128)(2,1)S(1)}, bf16[256,256]{1,0:T(8,128)(2,1)S(1)}, u32[]{:S(2)}, u32[]{:S(2)}) collective-permute-start(bf16[256,256]{1,0:T(8,128)(2,1)S(1)} %fusion), channel_id=1, source_target_pairs={{2,0},{5,1},{4,2},{7,3},{6,4},{9,5},{8,6},{11,7},{10,8},{13,9},{12... | collective-permute-start | bytes 393224 | tf_op jit(solution)/shard_map/ppermute | solution.py:245
  18.9 1.9 %collective-permute-start.5 = (bf16[256,512]{1,0:T(8,128)(2,1)S(1)}, bf16[256,512]{1,0:T(8,128)(2,1)S(1)}, u32[]{:S(2)}, u32[]{:S(2)}) collective-permute-start(bf16[256,512]{1,0:T(8,128)(2,1)S(1)} %get-tuple-element.8.own), channel_id=1, source_target_pairs={{0,2},{2,0},{12,14},{14,12},{4,8},{8,4},{6,10},{10,6},{1,3},{3,1},... | collective-permute-start | bytes 786440 | tf_op jit(solution)/shard_map/ppermute | solution.py:246
  20.8 0.0 collective-permute-start.4
  20.8 3.5 %collective-permute-start.3 = (bf16[256,512]{1,0:T(8,128)(2,1)S(1)}, bf16[256,512]{1,0:T(8,128)(2,1)S(1)}, u32[]{:S(2)}, u32[]{:S(2)}) collective-permute-start(bf16[256,512]{1,0:T(8,128)(2,1)S(1)} %get-tuple-element.8.own), channel_id=1, source_target_pairs={{0,0},{14,14},{2,4},{4,2},{6,8},{8,6},{10,12},{12,10},{1,1},{15,15... | collective-permute-start | bytes 786440 | tf_op jit(solution)/shard_map/ppermute | solution.py:246
  24.3 0.1 collective-permute-start.2
  24.4 0.6 %collective-permute-done.7 = bf16[256,256]{1,0:T(8,128)(2,1)S(1)} collective-permute-done((bf16[256,256]{1,0:T(8,128)(2,1)S(1)}, bf16[256,256]{1,0:T(8,128)(2,1)S(1)}, u32[]{:S(2)}, u32[]{:S(2)}) %collective-permute-start.7) | collective-permute-done | bytes 131104 | tf_op jit(solution)/shard_map/ppermute | solution.py:245
  25.0 0.1 collective-permute-start.8
  25.1 11.1 %collective-permute-done.5.far_odd = bf16[256,512]{1,0:T(8,128)(2,1)S(1)} collective-permute-done((bf16[256,512]{1,0:T(8,128)(2,1)S(1)}, bf16[256,512]{1,0:T(8,128)(2,1)S(1)}, u32[]{:S(2)}, u32[]{:S(2)}) %collective-permute-start.5) | collective-permute-done | bytes 262176 | tf_op jit(solution)/shard_map/ppermute | solution.py:246
  36.2 0.0 collective-permute-done.4.far
  36.2 0.0 collective-permute-done.3.near_odd
  36.2 3.7 %collective-permute-done.2.near = bf16[256,512]{1,0:T(8,128)(2,1)S(1)} collective-permute-done((bf16[256,512]{1,0:T(8,128)(2,1)S(1)}, bf16[256,512]{1,0:T(8,128)(2,1)S(1)}, u32[]{:S(2)}, u32[]{:S(2)}) %collective-permute-start.2) | collective-permute-done | bytes 262176 | tf_op jit(solution)/shard_map/ppermute | solution.py:246
  39.9 0.0 collective-permute-done.8.y_ref
  40.0 0.6 %copy-done.10 = bf16[256,512]{1,0:T(8,128)(2,1)} copy-done((bf16[256,512]{1,0:T(8,128)(2,1)}, bf16[256,512]{1,0:T(8,128)(2,1)S(1)}, u32[]{:S(2)}) %copy-start.10) | copy-done | bytes 262168
  40.6 0.7 %copy-done.11 = f32[256,256]{1,0:T(8,128)} copy-done((f32[256,256]{1,0:T(8,128)}, f32[256,256]{1,0:T(8,128)S(1)}, u32[]{:S(2)}) %copy-start.11) | copy-done | bytes 262168
  41.3 2.4 %place.1 = (bf16[256,256]{1,0:T(8,128)(2,1)}, f32[256,256]{1,0:T(8,128)}, f32[256,128]{1,0:T(8,128)}, f32[256,128]{1,0:T(8,128)}) custom-call(s32[2]{0:T(128)} %plan.1, bf16[256,512]{1,0:T(8,128)(2,1)} %copy-done.2, bf16[256,512]{1,0:T(8,128)(2,1)} %copy-done.10, bf16[256,512]{1,0:T(8,128)(2,1)} %copy-done.9, bf16[256,512]{1,0:T(8,128)(2,1)} %copy-done.8, ...), custom_call_target="tpu_custom_call" | custom-call | tf_op jit(solution)/shard_map/place/pallas_call | solution.py:250
  (15 shorter events, 0.1 us)
Async XLA Ops:
  0.6 10.4 %copy-start.1 = (bf16[256,128]{1,0:T(8,128)(2,1)S(1)}, bf16[256,128]{1,0:T(8,128)(2,1)}, u32[]{:S(2)}) copy-start(bf16[256,128]{1,0:T(8,128)(2,1)} %v_ref.1) | copy-start | bytes 196612
  0.6 10.4 %copy-start = (bf16[256,128]{1,0:T(8,128)(2,1)S(1)}, bf16[256,128]{1,0:T(8,128)(2,1)}, u32[]{:S(2)}) copy-start(bf16[256,128]{1,0:T(8,128)(2,1)} %k_ref.1) | copy-start | bytes 196612
  0.7 10.4 %copy-start.3 = (bf16[256,256]{1,0:T(8,128)(2,1)S(1)}, bf16[256,256]{1,0:T(8,128)(2,1)}, u32[]{:S(2)}) copy-start(bf16[256,256]{1,0:T(8,128)(2,1)} %q_ref.1) | copy-start | bytes 393220
  1.6 9.4 %copy-start.5 = (s32[16]{0:T(128)S(1)}, s32[16]{0:T(128)}, u32[]{:S(2)}) copy-start(s32[16]{0:T(128)} %lens.1) | copy-start | bytes 196
  1.6 8.1 %collective-permute-start = (bf16[256,256]{1,0:T(8,128)(2,1)S(1)}, bf16[256,256]{1,0:T(8,128)(2,1)S(1)}, u32[]{:S(2)}, u32[]{:S(2)}) collective-permute-start(bf16[256,256]{1,0:T(8,128)(2,1)S(1)} %pad_maximum_fusion), channel_id=1, source_target_pairs={{0,2},{1,5},{2,4},{3,7},{4,6},{5,9},{6,8},{7,11},{8,10},{9,13},{10... | collective-permute-start | bytes 393224 | tf_op jit(solution)/shard_map/ppermute | solution.py:222
  9.7 1.3 %collective-permute-start.1 = (bf16[1,256,256]{2,1,0:T(8,128)(2,1)S(1)}, bf16[1,256,256]{2,1,0:T(8,128)(2,1)S(1)}, u32[]{:S(2)}, u32[]{:S(2)}) collective-permute-start(bf16[1,256,256]{2,1,0:T(8,128)(2,1)S(1)} %bitcast.3), channel_id=1, source_target_pairs={{0,1},{1,0},{2,3},{3,2},{4,5},{5,4},{6,7},{7,6},{8,9},{9,8},{10,11... | collective-permute-start | bytes 393224 | tf_op jit(solution)/shard_map/ppermute | solution.py:223
  11.0 0.9 %copy-start.4 = (bf16[256,256]{1,0:T(8,128)(2,1)S(1)}, bf16[256,256]{1,0:T(8,128)(2,1)}, u32[]{:S(2)}) copy-start(bf16[256,256]{1,0:T(8,128)(2,1)} %g_ref.1) | copy-start | bytes 393220
  15.3 9.7 %copy-start.2 = (bf16[256,512]{1,0:T(8,128)(2,1)}, bf16[256,512]{1,0:T(8,128)(2,1)S(1)}, u32[]{:S(2)}) copy-start(bf16[256,512]{1,0:T(8,128)(2,1)S(1)} %get-tuple-element.8.own) | copy-start | bytes 786436
  15.3 1.4 %collective-permute-start.6 = (bf16[1,256,256]{2,1,0:T(8,128)(2,1)S(1)}, bf16[1,256,256]{2,1,0:T(8,128)(2,1)S(1)}, u32[]{:S(2)}, u32[]{:S(2)}) collective-permute-start(bf16[1,256,256]{2,1,0:T(8,128)(2,1)S(1)} %get-tuple-element.11), channel_id=1, source_target_pairs={{0,1},{1,0},{2,3},{3,2},{4,5},{5,4},{6,7},{7,6},{8,9},{9,8},{10,11... | collective-permute-start | bytes 393224 | tf_op jit(solution)/shard_map/ppermute | solution.py:241
  16.8 8.2 %collective-permute-start.7 = (bf16[256,256]{1,0:T(8,128)(2,1)S(1)}, bf16[256,256]{1,0:T(8,128)(2,1)S(1)}, u32[]{:S(2)}, u32[]{:S(2)}) collective-permute-start(bf16[256,256]{1,0:T(8,128)(2,1)S(1)} %fusion), channel_id=1, source_target_pairs={{2,0},{5,1},{4,2},{7,3},{6,4},{9,5},{8,6},{11,7},{10,8},{13,9},{12... | collective-permute-start | bytes 393224 | tf_op jit(solution)/shard_map/ppermute | solution.py:245
  18.9 17.3 %collective-permute-start.5 = (bf16[256,512]{1,0:T(8,128)(2,1)S(1)}, bf16[256,512]{1,0:T(8,128)(2,1)S(1)}, u32[]{:S(2)}, u32[]{:S(2)}) collective-permute-start(bf16[256,512]{1,0:T(8,128)(2,1)S(1)} %get-tuple-element.8.own), channel_id=1, source_target_pairs={{0,2},{2,0},{12,14},{14,12},{4,8},{8,4},{6,10},{10,6},{1,3},{3,1},... | collective-permute-start | bytes 786440 | tf_op jit(solution)/shard_map/ppermute | solution.py:246
  20.8 15.4 %collective-permute-start.4 = (bf16[256,512]{1,0:T(8,128)(2,1)S(1)}, bf16[256,512]{1,0:T(8,128)(2,1)S(1)}, u32[]{:S(2)}, u32[]{:S(2)}) collective-permute-start(bf16[256,512]{1,0:T(8,128)(2,1)S(1)} %get-tuple-element.8.own), channel_id=1, source_target_pairs={{0,4},{2,6},{4,0},{6,2},{8,12},{10,14},{12,8},{14,10},{1,5},{3,7},... | collective-permute-start | bytes 786440 | tf_op jit(solution)/shard_map/ppermute | solution.py:246
  20.8 15.4 %collective-permute-start.3 = (bf16[256,512]{1,0:T(8,128)(2,1)S(1)}, bf16[256,512]{1,0:T(8,128)(2,1)S(1)}, u32[]{:S(2)}, u32[]{:S(2)}) collective-permute-start(bf16[256,512]{1,0:T(8,128)(2,1)S(1)} %get-tuple-element.8.own), channel_id=1, source_target_pairs={{0,0},{14,14},{2,4},{4,2},{6,8},{8,6},{10,12},{12,10},{1,1},{15,15... | collective-permute-start | bytes 786440 | tf_op jit(solution)/shard_map/ppermute | solution.py:246
  24.3 15.6 %collective-permute-start.2 = (bf16[256,512]{1,0:T(8,128)(2,1)S(1)}, bf16[256,512]{1,0:T(8,128)(2,1)S(1)}, u32[]{:S(2)}, u32[]{:S(2)}) collective-permute-start(bf16[256,512]{1,0:T(8,128)(2,1)S(1)} %get-tuple-element.8.own), channel_id=1, source_target_pairs={{0,2},{2,0},{4,6},{6,4},{8,10},{10,8},{12,14},{14,12},{1,3},{3,1},... | collective-permute-start | bytes 786440 | tf_op jit(solution)/shard_map/ppermute | solution.py:246
  25.0 14.9 %copy-start.6 = (f32[256,256]{1,0:T(8,128)}, f32[256,256]{1,0:T(8,128)S(1)}, u32[]{:S(2)}) copy-start(f32[256,256]{1,0:T(8,128)S(1)} %convert_add_fusion.x_ref) | copy-start | bytes 786436
  25.0 14.9 %collective-permute-start.8 = (f32[256,256]{1,0:T(8,128)S(1)}, f32[256,256]{1,0:T(8,128)S(1)}, u32[]{:S(2)}, u32[]{:S(2)}) collective-permute-start(f32[256,256]{1,0:T(8,128)S(1)} %convert_add_fusion.x_ref), channel_id=1, source_target_pairs={{0,1},{1,0},{2,3},{3,2},{4,5},{5,4},{6,7},{7,6},{8,9},{9,8},{10,11... | collective-permute-start | bytes 786440 | tf_op jit(solution)/shard_map/ppermute | solution.py:248
  36.2 3.7 %copy-start.7 = (bf16[256,512]{1,0:T(8,128)(2,1)}, bf16[256,512]{1,0:T(8,128)(2,1)S(1)}, u32[]{:S(2)}) copy-start(bf16[256,512]{1,0:T(8,128)(2,1)S(1)} %collective-permute-done.5.far_odd) | copy-start | bytes 786436
  36.2 3.7 %copy-start.8 = (bf16[256,512]{1,0:T(8,128)(2,1)}, bf16[256,512]{1,0:T(8,128)(2,1)S(1)}, u32[]{:S(2)}) copy-start(bf16[256,512]{1,0:T(8,128)(2,1)S(1)} %collective-permute-done.4.far) | copy-start | bytes 786436
  36.2 3.7 %copy-start.9 = (bf16[256,512]{1,0:T(8,128)(2,1)}, bf16[256,512]{1,0:T(8,128)(2,1)S(1)}, u32[]{:S(2)}) copy-start(bf16[256,512]{1,0:T(8,128)(2,1)S(1)} %collective-permute-done.3.near_odd) | copy-start | bytes 786436
  39.9 0.7 %copy-start.10 = (bf16[256,512]{1,0:T(8,128)(2,1)}, bf16[256,512]{1,0:T(8,128)(2,1)S(1)}, u32[]{:S(2)}) copy-start(bf16[256,512]{1,0:T(8,128)(2,1)S(1)} %collective-permute-done.2.near) | copy-start | bytes 786436
  40.6 0.7 %copy-start.11 = (f32[256,256]{1,0:T(8,128)}, f32[256,256]{1,0:T(8,128)S(1)}, u32[]{:S(2)}) copy-start(f32[256,256]{1,0:T(8,128)S(1)} %collective-permute-done.8.y_ref) | copy-start | bytes 786436

commit v2 on v1

v2 whole, which is shorter than its diff:
```python
import math

import jax
import jax.numpy as jnp
from jax import lax
from jax.experimental import pallas as pl
from jax.experimental.pallas import tpu as pltpu
from jax.sharding import PartitionSpec as P

DOC_CAP = 4096
NEG = -1e30
LOG2E = 1.4426950408889634
CHUNK = 128

VMEM = pl.BlockSpec(memory_space=pltpu.VMEM)
SMEM = pl.BlockSpec(memory_space=pltpu.SMEM)


def nt(a, b):
    return lax.dot_general(a, b, (((1,), (1,)), ((), ())), preferred_element_type=jnp.float32)


def nn(a, b):
    return lax.dot_general(a, b, (((1,), (0,)), ((), ())), preferred_element_type=jnp.float32)


def tn(a, b):
    return lax.dot_general(a, b, (((0,), (0,)), ((), ())), preferred_element_type=jnp.float32)


def fold(a, op):
    rows = a.shape[0] // 8
    parts = a.reshape(rows, 8, a.shape[1])
    return op(parts, axis=0)


def up_down(z, flip):
    return z + 1 - 2 * ((z + flip) % 2)


def row_pairs(rows):
    pairs = ([], [])
    for z in range(rows):
        for x in range(2):
            for h in range(2):
                for way in range(2):
                    to = z + 1 - 2 * ((z + (h ^ way)) % 2)
                    other = (to, x) if 0 <= to < rows else (z, 1 - x)
                    node = 4 * z + 2 * x + h
                    pairs[way].append((node, 4 * other[0] + 2 * other[1] + h))
    return pairs


def pack_kernel(k_ref, v_ref, q_ref, g_ref, kv_ref, bundle_ref, sems):
    side = lax.axis_index("head")
    dim = k_ref.shape[1]
    width = q_ref.shape[1]
    half = bundle_ref.at[:, 2 * width:]
    moves = (
        (k_ref, kv_ref.at[:, :dim]),
        (v_ref, kv_ref.at[:, dim:]),
        (q_ref, bundle_ref.at[:, :width]),
        (g_ref, bundle_ref.at[:, width:2 * width]),
    )
    copies = [pltpu.make_async_copy(a, b, sems.at[i]) for i, (a, b) in enumerate(moves)]
    for copy in copies:
        copy.start()
    for copy in copies[:2]:
        copy.wait()

    @pl.when(side == 0)
    def _():
        half[...] = kv_ref[:, :dim]

    @pl.when(side == 1)
    def _():
        half[...] = kv_ref[:, dim:]

    for copy in copies[2:]:
        copy.wait()


def loop(count, body, carry):
    if count <= 8:
        for j in range(count):
            carry = body(j, carry)
        return carry
    return lax.fori_loop(0, count, body, carry)

def rows_at(c):
    start = c * CHUNK
    return pl.ds(start if isinstance(start, int) else pl.multiple_of(start, CHUNK), CHUNK)


def two_stretches(sizes, lens, z, column, kbuf, vbuf, q_all, g_all, w_ref, p_ref, d_ref,
                  od_ref, put=None):
    rounds, reach, tok, heads, head_dim = sizes
    inv_root = 1.0 / math.sqrt(head_dim)
    width = heads * head_dim
    lanes = heads * CHUNK
    span = 2 * reach + 2
    unrolled = span <= 8
    low = 4 * rounds + 2 * column - 2 * reach
    low_place = (2 * (z - rounds) * tok) + low * CHUNK
    q, g, places, begin = [], [], [], []
    for i in range(2):
        rows = slice(i * CHUNK, (i + 1) * CHUNK)
        q.append(jnp.concatenate(
            [q_all[rows, h * head_dim:(h + 1) * head_dim] for h in range(heads)], axis=0))
        g.append(jnp.concatenate(
            [g_all[rows, h * head_dim:(h + 1) * head_dim] for h in range(heads)], axis=0))
        lane = lax.broadcasted_iota(jnp.int32, (1, lanes), 1) % CHUNK
        place = (2 * z + column) * tok + i * CHUNK + lane
        start = jnp.zeros((1, lanes), jnp.int32)
        bound = jnp.int32(0)
        for m in range(lens.shape[0]):
            bound = bound + lens[m]
            start = jnp.where(place >= bound, bound, start)
        places.append(place)
        begin.append(start)

    def slots(j):
        if not unrolled:
            return (0, 1)
        return tuple(i for i in range(2) if i <= j <= 2 * reach + i)

    def of_slot(i):
        return slice(i * lanes, (i + 1) * lanes)

    def contract(buf, ref, i):
        if unrolled:
            rows = (2 * reach + 1) * CHUNK
            at = pl.ds(pl.multiple_of((low + i) * CHUNK, CHUNK), rows)
            return tn(buf[at, :], ref[i * CHUNK:i * CHUNK + rows, of_slot(i)])

        def add(j, acc):
            return acc + tn(buf[rows_at(low + j), :], ref[rows_at(j), of_slot(i)])

        return lax.fori_loop(0, span, add, jnp.zeros((head_dim, lanes), jnp.float32))

    def scores(j, tops):
        tops = list(tops)
        k = kbuf[rows_at(low + j), :]
        at = low_place + j * CHUNK + lax.broadcasted_iota(jnp.int32, (CHUNK, lanes), 0)
        for i in slots(j):
            allowed = at >= begin[i]
            if not unrolled or j == 2 * reach + i:
                allowed = allowed & (at <= places[i])
            s = jnp.where(allowed, nt(k, q[i]) * (inv_root * LOG2E), NEG)
            w_ref[i, j] = s
            tops[i] = jnp.maximum(tops[i], fold(s, jnp.max))
        return tuple(tops)

    full = lambda value: tuple(jnp.full((8, lanes), value, jnp.float32) for _ in range(2))
    tops = loop(span, scores, full(NEG))
    tops = [jnp.max(t, axis=0, keepdims=True) for t in tops]

    def exps(j, totals):
        totals = list(totals)
        for i in slots(j):
            e = jnp.exp2(w_ref[i, j] - tops[i])
            w_ref[i, j] = e
            p_ref[rows_at(j), of_slot(i)] = e.astype(jnp.bfloat16)
            totals[i] = totals[i] + fold(e, jnp.sum)
        return tuple(totals)

    totals = loop(span, exps, full(0.0))
    scale = [1.0 / jnp.sum(t, axis=0, keepdims=True) for t in totals]
    dots = []
    for i in range(2):
        attended = (contract(vbuf, p_ref, i) * scale[i]).T.astype(jnp.bfloat16)
        for h in range(heads):
            od_ref[i * CHUNK:(i + 1) * CHUNK, h * head_dim:(h + 1) * head_dim] = (
                attended[h * CHUNK:(h + 1) * CHUNK])
        product = g[i].astype(jnp.float32) * attended.astype(jnp.float32)
        dots.append(jnp.sum(product.T, axis=0, keepdims=True))

    def backward(j, carry):
        v = vbuf[rows_at(low + j), :]
        for i in range(2):
            if i in slots(j):
                w = w_ref[i, j] * scale[i]
                ds = (w * (nt(v, g[i]) - dots[i])).astype(jnp.bfloat16)
                d_ref[rows_at(j), of_slot(i)] = ds
                if put is not None:
                    p_ref[rows_at(j), of_slot(i)] = w.astype(jnp.bfloat16)
            elif put is not None:
                blank = jnp.zeros((CHUNK, lanes), jnp.bfloat16)
                d_ref[rows_at(j), of_slot(i)] = blank
                p_ref[rows_at(j), of_slot(i)] = blank
        return carry

    loop(span, backward, 0)
    if put is not None:
        q_both = jnp.concatenate(q, axis=0)
        g_both = jnp.concatenate(g, axis=0)

        def keys(b, carry):
            start = b * tok
            at = pl.ds(start if isinstance(start, int) else pl.multiple_of(start, tok), tok)
            put(reach - b, nn(d_ref[at, :], q_both) * inv_root, nn(p_ref[at, :], g_both))
            return carry

        loop(reach + 1, keys, 0)
    for i in range(2):
        grad = (contract(kbuf, d_ref, i) * inv_root).T.astype(jnp.bfloat16)
        for h in range(heads):
            at = width + h * head_dim
            od_ref[i * CHUNK:(i + 1) * CHUNK, at:at + head_dim] = (
                grad[h * CHUNK:(h + 1) * CHUNK])


def own_kernel(sizes):
    rounds, reach, tok, heads, head_dim = sizes

    def kernel(lens, k_ref, v_ref, q_ref, g_ref, mine_ref, other_ref, part_ref, cross_ref,
               od_ref, own_out, mine_out, other_out, kbuf, vbuf, w_ref, p_ref, d_ref, grads):
        here = lax.axis_index("ctx")
        side = lax.axis_index("head")
        z = here // 2
        x = here % 2
        half = part_ref.at[:, 2 * heads * head_dim:]

        for r in range(rounds):
            for ref, column in ((mine_ref, (x + side) % 2), (other_ref, (x + 1 - side) % 2)):
                at = pl.ds(pl.multiple_of((2 * (rounds - 1 - r) + column) * tok, tok), tok)
                kbuf[at, :] = ref[r, :, :head_dim]
                vbuf[at, :] = ref[r, :, head_dim:]
        own = pl.ds(pl.multiple_of((2 * rounds + x) * tok, tok), tok)
        kbuf[own, :] = k_ref[...]
        vbuf[own, :] = v_ref[...]
        next_to = pl.ds(pl.multiple_of((2 * rounds + 1 - x) * tok, tok), tok)

        @pl.when(side == 0)
        def _():
            kbuf[next_to, :] = half[...]
            vbuf[next_to, :] = cross_ref[...]

        @pl.when(side == 1)
        def _():
            vbuf[next_to, :] = half[...]
            kbuf[next_to, :] = cross_ref[...]

        def put(hop, dk, dv):
            def own_block():
                own_out[:, :head_dim] = dk
                own_out[:, head_dim:] = dv

            def far_block():
                grads[hop - 1, :, :head_dim] = dk.astype(grads.dtype)
                grads[hop - 1, :, head_dim:] = dv.astype(grads.dtype)

            if isinstance(hop, int):
                own_block() if hop == 0 else far_block()
            else:
                pl.when(hop == 0)(own_block)
                pl.when(hop > 0)(far_block)

        if reach < 2 * rounds:
            grads[reach] = jnp.zeros(grads.shape[1:], grads.dtype)
        two_stretches(sizes, lens, z, x, kbuf, vbuf, q_ref, g_ref, w_ref, p_ref, d_ref, od_ref, put)
        for r in range(rounds):
            mine_out[r] = grads[2 * r + side]
            other_out[r] = grads[2 * r + 1 - side]

    return kernel


def next_kernel(sizes):
    rounds, reach, tok, heads, head_dim = sizes
    width = heads * head_dim

    def kernel(lens, plan, kbuf, vbuf, qg_ref, own_od, od_ref, send_a, send_b, w_ref, p_ref, d_ref):
        here = lax.axis_index("ctx")
        side = lax.axis_index("head")
        z = here // 2
        x = here % 2
        od_ref[:tok, :] = own_od[...]
        two_stretches(sizes, lens, z, 1 - x, kbuf, vbuf, qg_ref.at[:, :width],
                      qg_ref.at[:, width:2 * width], w_ref, p_ref, d_ref, od_ref.at[tok:, :])
        for way, out in enumerate((send_a, send_b)):
            flip = (side + way) % 2
            for i in range(2):
                wanted = jnp.where(flip == 0, plan[i], plan[2 + i])
                at = row_of(wanted, x)
                out[i * CHUNK:(i + 1) * CHUNK, :] = od_ref[at, :]

    return kernel


def row_of(wanted, x):
    inner = wanted % 4
    return pl.ds(pl.multiple_of(((inner + 2 * x) % 4) * CHUNK, CHUNK), CHUNK)


def place_kernel(width):
    def kernel(plan, row_ref, a_ref, b_ref, s_ref, t_ref, out_ref, dq_ref, dk_ref, dv_ref):
        here = lax.axis_index("ctx")
        side = lax.axis_index("head")
        z = here // 2
        source_a = up_down(z, side)
        for slot in range(2):
            wanted = plan[slot]
            to = pl.ds(slot * CHUNK, CHUNK)
            inside = row_of(wanted, here % 2)

            def put(rows):
                out_ref[to, :] = rows[:, :width]
                dq_ref[to, :] = rows[:, width:].astype(jnp.float32)

            home = wanted // 4 == z
            from_a = wanted // 4 == source_a
            pl.when(home)(lambda: put(row_ref[inside, :]))
            pl.when(from_a)(lambda: put(a_ref[to, :]))
            pl.when(jnp.logical_not(home | from_a))(lambda: put(b_ref[to, :]))
        half = dk_ref.shape[1]
        dk_ref[...] = s_ref[:, :half] + t_ref[:, :half]
        dv_ref[...] = s_ref[:, half:] + t_ref[:, half:]

    return kernel


def per_device(queries, key_input, value_input, grad_out, doc_lengths, stretch_plan):
    tok, head_dim = key_input.shape
    width = queries.shape[1]
    heads = width // head_dim
    n = lax.axis_size("ctx")
    reach = min(DOC_CAP, tok * n // 4) // tok
    rounds = (reach + 1) // 2
    bf16, f32 = jnp.bfloat16, jnp.float32
    both = ("ctx", "head")
    cross = [(0, 1), (1, 0)]
    side = lax.axis_index("head")

    def fetch_pairs(r):
        pairs = []
        for s in range(n):
            for h in range(2):
                to = s // 2 + r + 1
                if to < n // 2:
                    pairs.append((2 * s + h, 2 * (2 * to + (s + h) % 2) + h))
        return pairs

    def back_pairs(r):
        pairs = []
        for s in range(n):
            for h in range(2):
                to = s - (2 * r + 1 + h)
                if to >= 0:
                    pairs.append((2 * s + h, 2 * to + h))
        return pairs

    own_kv, bundle = pl.pallas_call(
        pack_kernel,
        out_shape=(
            pltpu.VMEM((tok, 2 * head_dim), bf16),
            pltpu.VMEM((tok, 2 * width + head_dim), bf16),
        ),
        in_specs=[pl.BlockSpec(memory_space=pl.ANY)] * 4,
        out_specs=(VMEM,) * 2,
        scratch_shapes=[pltpu.SemaphoreType.DMA((4,))],
        name="pack",
    )(key_input, value_input, queries, grad_out)
    tie_a, tie_b = row_pairs(n // 2)
    part = lax.ppermute(bundle, "ctx", [(i, i ^ 1) for i in range(n)])
    mine = [lax.ppermute(own_kv, both, fetch_pairs(r)) for r in range(rounds)]
    plan_mine = lax.ppermute(stretch_plan, both, tie_a)
    *mine, part, plan_mine = lax.optimization_barrier((*mine, part, plan_mine))
    mine = jnp.stack(mine)
    other = lax.ppermute(mine, "head", cross)
    half_cross = lax.ppermute(part[:, 2 * width:], "head", cross)
    plan_other = lax.ppermute(plan_mine, "head", cross)
    plans = jnp.where(side == 0, jnp.concatenate([plan_mine, plan_other]),
                      jnp.concatenate([plan_other, plan_mine]))

    other, half_cross, plans = lax.optimization_barrier((other, half_cross, plans))
    sizes = (rounds, reach, tok, heads, head_dim)
    params = pltpu.CompilerParams(vmem_limit_bytes=40 << 20)
    span = 2 * reach + 2
    weights = pltpu.VMEM((span * CHUNK, 2 * heads * CHUNK), bf16)
    scores = [pltpu.VMEM((2, span, CHUNK, heads * CHUNK), f32), weights, weights]
    buffer = jax.ShapeDtypeStruct(((2 * rounds + 2) * tok, head_dim), bf16)
    rows = jax.ShapeDtypeStruct((tok, 2 * width), bf16)
    far = jax.ShapeDtypeStruct((rounds, tok, 2 * head_dim), bf16)
    od_own, own_part, mine_part, other_part, kbuf, vbuf = pl.pallas_call(
        own_kernel(sizes),
        out_shape=(rows, jax.ShapeDtypeStruct((tok, 2 * head_dim), f32), far, far, buffer, buffer),
        in_specs=[SMEM] + [VMEM] * 8,
        out_specs=(VMEM,) * 6,
        scratch_shapes=scores + [pltpu.VMEM((2 * rounds, tok, 2 * head_dim), bf16)],
        compiler_params=params,
        name="attend_own",
    )(doc_lengths, key_input, value_input, queries, grad_out, mine, other, part, half_cross)
    partner = lax.ppermute(other_part, "head", cross)
    od, send_a, send_b = pl.pallas_call(
        next_kernel(sizes),
        out_shape=(jax.ShapeDtypeStruct((2 * tok, 2 * width), bf16), rows, rows),
        in_specs=[SMEM, SMEM] + [VMEM] * 4,
        out_specs=(VMEM,) * 3,
        scratch_shapes=scores,
        compiler_params=params,
        name="attend_next",
    )(doc_lengths, plans, kbuf, vbuf, part, od_own)

    moved_a = lax.ppermute(send_a, both, tie_a)
    moved_b = lax.ppermute(send_b, both, tie_b)
    back = (mine_part.astype(f32) + partner.astype(f32)).astype(bf16)
    total = own_part
    for r in range(rounds):
        total = total + lax.ppermute(back[r], both, back_pairs(r)).astype(f32)
    total_other = lax.ppermute(total, "head", cross)

    output, query_grad, key_grad, value_grad = pl.pallas_call(
        place_kernel(width),
        out_shape=(
            jax.ShapeDtypeStruct((tok, width), bf16),
            jax.ShapeDtypeStruct((tok, width), f32),
            jax.ShapeDtypeStruct((tok, head_dim), f32),
            jax.ShapeDtypeStruct((tok, head_dim), f32),
        ),
        in_specs=[SMEM] + [VMEM] * 5,
        out_specs=(VMEM,) * 4,
        compiler_params=pltpu.CompilerParams(vmem_limit_bytes=32 << 20),
        name="place",
    )(stretch_plan, od, moved_a, moved_b, total, total_other)
    return (output, query_grad, key_grad, value_grad)


def solution(mesh):
    return jax.shard_map(
        per_device,
        mesh=mesh,
        in_specs=(
            P(("groups", "ctx"), "head"),
            P(("groups", "ctx"), None),
            P(("groups", "ctx"), None),
            P(("groups", "ctx"), "head"),
            P("groups"),
            P(("groups", "ctx")),
        ),
        out_specs=(
            P(("groups", "ctx"), "head"),
            P(("groups", "ctx"), "head"),
            P(("groups", "ctx"), None),
            P(("groups", "ctx"), None),
        ),
        check_vma=False,
    )
```

time: 43.9 us -> 34.3 us (0.78)
  the two profiles are of different devices: /device:TPU:24 before, /device:TPU:1 now
where the time goes in v2:
time: 34.3 us; the launch traced here: 33.8 us
  starting transfers between devices  16.4 us (48%)
  waiting for transfers between devices  9.19 us (27%)
  Pallas kernels  7.25 us (21%)
  between operations  0.77 us (2%)
    ppermute x1, waiting for transfers between devices, per_device(): moved_b = lax.ppermute(send_b, both, tie_b)  4.39 us
    ppermute x1, starting transfers between devices, per_device(): moved_b = lax.ppermute(send_b, both, tie_b)  3.57 us
    ppermute x1, starting transfers between devices, per_device(): mine = [lax.ppermute(own_kv, both, fetch_pairs(r)) for r in range(rounds)]  3.17 us
    ppermute x1, waiting for transfers between devices, per_device(): plan_mine = lax.ppermute(stretch_plan, both, tie_a)  2.97 us
    pallas_call x1, Pallas kernels, per_device(): pl.pallas_call(own_kernel(sizes), out_shape=(rows, jax.ShapeDtypeStruct((...  2.52 us
    pallas_call x1, Pallas kernels, per_device(): pl.pallas_call(next_kernel(sizes), out_shape=(jax.ShapeDtypeStruct((2 * t...  2.13 us
    ppermute x1, starting transfers between devices, per_device(): part = lax.ppermute(bundle, 'ctx', [(i, i ^ 1) for i in range(n)])  2.11 us
    ppermute x1, starting transfers between devices, per_device(): moved_a = lax.ppermute(send_a, both, tie_a)  1.53 us
  transfers between devices with their start and end apart: 11, of which 5 were waited for; matrix products, arithmetic and copies ran while one was open for 0% of the time, Pallas kernels for 6%

profile of v2, /device:TPU:1, one launch (start us, length us, event | category | flops | bytes accessed | tf_op | source)
XLA Modules:
  0.0 33.8 jit_solution(17016619410327975953)
XLA Ops:
  0.6 0.0 copy-start.5
  0.6 0.0 copy-start.1
  0.7 1.1 %pack.1 = (bf16[256,256]{1,0:T(8,128)(2,1)S(1)}, bf16[256,640]{1,0:T(8,128)(2,1)S(1)}) custom-call(bf16[256,128]{1,0:T(8,128)(2,1)} %k_ref.3, bf16[256,128]{1,0:T(8,128)(2,1)} %v_ref.3, bf16[256,256]{1,0:T(8,128)(2,1)} %q_ref.3, bf16[256,256]{1,0:T(8,128)(2,1)} %g_ref.3), custom_call_target="tpu_custom_call" | custom-call | tf_op jit(solution)/shard_map/pack/pallas_call | solution.py:353
  1.8 0.0 copy-start
  1.8 2.1 %collective-permute-start.1 = (bf16[256,640]{1,0:T(8,128)(2,1)S(1)}, bf16[256,640]{1,0:T(8,128)(2,1)S(1)}, u32[]{:S(2)}, u32[]{:S(2)}) collective-permute-start(bf16[256,640]{1,0:T(8,128)(2,1)S(1)} %get-tuple-element.22), channel_id=1, source_target_pairs={{0,2},{2,0},{4,6},{6,4},{8,10},{10,8},{12,14},{14,12},{1,3},{3,1},... | collective-permute-start | bytes 983048 | tf_op jit(solution)/shard_map/ppermute | solution.py:365
  3.9 3.2 %collective-permute-start = (bf16[256,256]{1,0:T(8,128)(2,1)S(1)}, bf16[256,256]{1,0:T(8,128)(2,1)S(1)}, u32[]{:S(2)}, u32[]{:S(2)}) collective-permute-start(bf16[256,256]{1,0:T(8,128)(2,1)S(1)} %get-tuple-element.21), channel_id=1, source_target_pairs={{0,4},{1,7},{2,6},{3,5},{4,8},{5,11},{6,10},{7,9},{8,12},{9,15},{1... | collective-permute-start | bytes 393224 | tf_op jit(solution)/shard_map/ppermute | solution.py:366
  7.1 1.3 %collective-permute-start.2 = (s32[2]{0:T(128)S(1)}, s32[2]{0:T(128)S(1)}, u32[]{:S(2)}, u32[]{:S(2)}) collective-permute-start(s32[2]{0:T(128)S(1)} %copy-done.5), channel_id=1, source_target_pairs={{0,4},{1,3},{2,6},{3,1},{4,0},{5,9},{6,2},{7,11},{8,12},{9,5},{10,... | collective-permute-start | bytes 32 | tf_op jit(solution)/shard_map/ppermute | solution.py:367
  8.4 3.0 %collective-permute-done.2 = s32[2]{0:T(128)S(1)} collective-permute-done((s32[2]{0:T(128)S(1)}, s32[2]{0:T(128)S(1)}, u32[]{:S(2)}, u32[]{:S(2)}) %collective-permute-start.2) | collective-permute-done | bytes 40 | tf_op jit(solution)/shard_map/ppermute | solution.py:367
  11.4 0.0 collective-permute-done
  11.4 0.0 collective-permute-done.1.part_ref.qg_ref
  11.4 1.2 %collective-permute-start.3 = (bf16[1,256,256]{2,1,0:T(8,128)(2,1)S(1)}, bf16[1,256,256]{2,1,0:T(8,128)(2,1)S(1)}, u32[]{:S(2)}, u32[]{:S(2)}) collective-permute-start(bf16[1,256,256]{2,1,0:T(8,128)(2,1)S(1)} %bitcast.3), channel_id=1, source_target_pairs={{0,1},{1,0},{2,3},{3,2},{4,5},{5,4},{6,7},{7,6},{8,9},{9,8},{10,11... | collective-permute-start | bytes 393224 | tf_op jit(solution)/shard_map/ppermute | solution.py:370
  12.6 0.0 collective-permute-start.5
  12.6 0.0 copy-start.4
  12.6 0.6 %collective-permute-start.4 = (bf16[256,128]{1,0:T(8,128)(2,1)S(1)}, bf16[256,128]{1,0:T(8,128)(2,1)S(1)}, u32[]{:S(2)}, u32[]{:S(2)}) collective-permute-start(bf16[256,128]{1,0:T(8,128)(2,1)S(1)} %slice.3), channel_id=1, source_target_pairs={{0,1},{1,0},{2,3},{3,2},{4,5},{5,4},{6,7},{7,6},{8,9},{9,8},{10,11... | collective-permute-start | bytes 196616 | tf_op jit(solution)/shard_map/ppermute | solution.py:371
  13.2 0.5 %collective-permute-done.5 = s32[2]{0:T(128)S(1)} collective-permute-done((s32[2]{0:T(128)S(1)}, s32[2]{0:T(128)S(1)}, u32[]{:S(2)}, u32[]{:S(2)}) %collective-permute-start.5) | collective-permute-done | bytes 40 | tf_op jit(solution)/shard_map/ppermute | solution.py:372
  13.7 0.1 broadcast_select_fusion.plan
  13.8 0.3 collective-permute-done.4.cross_ref
  14.1 0.0 collective-permute-done.3.other_ref
  14.1 0.0 copy-done.2
  14.1 2.5 %attend_own.1 = (bf16[256,512]{1,0:T(8,128)(2,1)S(1)}, f32[256,256]{1,0:T(8,128)S(1)}, bf16[1,256,256]{2,1,0:T(8,128)(2,1)S(1)}, bf16[1,256,256]{2,1,0:T(8,128)(...) custom-call(s32[16]{0:T(128)S(1)} %copy-done.4, bf16[256,128]{1,0:T(8,128)(2,1)S(1)} %copy-done.2, ...), custom_call_target="tpu_custom_call" | custom-call | tf_op jit(solution)/shard_map/attend_own/pallas_call | solution.py:385
  16.6 0.4 %collective-permute-start.8 = (bf16[1,256,256]{2,1,0:T(8,128)(2,1)S(1)}, bf16[1,256,256]{2,1,0:T(8,128)(2,1)S(1)}, u32[]{:S(2)}, u32[]{:S(2)}) collective-permute-start(bf16[1,256,256]{2,1,0:T(8,128)(2,1)S(1)} %get-tuple-element.37), channel_id=1, source_target_pairs={{0,1},{1,0},{2,3},{3,2},{4,5},{5,4},{6,7},{7,6},{8,9},{9,8},{10,11... | collective-permute-start | bytes 393224 | tf_op jit(solution)/shard_map/ppermute | solution.py:394
  17.1 1.0 %collective-permute-done.8 = bf16[1,256,256]{2,1,0:T(8,128)(2,1)S(1)} collective-permute-done((bf16[1,256,256]{2,1,0:T(8,128)(2,1)S(1)}, bf16[1,256,256]{2,1,0:T(8,128)(2,1)S(1)}, u32[]{:S(2)}, u32[]{:S(2)}) %collective-permute-start.8) | collective-permute-done | bytes 131104 | tf_op jit(solution)/shard_map/ppermute | solution.py:394
  18.1 1.3 %collective-permute-start.9 = (bf16[256,256]{1,0:T(8,128)(2,1)S(1)}, bf16[256,256]{1,0:T(8,128)(2,1)S(1)}, u32[]{:S(2)}, u32[]{:S(2)}) collective-permute-start(bf16[256,256]{1,0:T(8,128)(2,1)S(1)} %fusion), channel_id=1, source_target_pairs={{2,0},{4,2},{5,1},{6,4},{7,3},{8,6},{9,5},{10,8},{11,7},{12,10},{1... | collective-permute-start | bytes 393224 | tf_op jit(solution)/shard_map/ppermute | solution.py:410
  19.4 2.1 %attend_next.1 = (bf16[512,512]{1,0:T(8,128)(2,1)S(1)}, bf16[256,512]{1,0:T(8,128)(2,1)S(1)}, bf16[256,512]{1,0:T(8,128)(2,1)S(1)}) custom-call(s32[16]{0:T(128)S(1)} %copy-done.4, s32[4]{0:T(128)S(1)} %broadcast_select_fusion.plan, bf16[1024,128]{1,0:T(8,128)(2,1)S(1)} %get-tuple-element.29.kbuf, bf16[1024,128]{1,0:T(8,128)(2,1)S(1)} %get-tuple-element.30.vbuf, ...), custom_call_target="tpu_custom_call" | custom-call | tf_op jit(solution)/shard_map/attend_next/pallas_call | solution.py:395
  21.5 1.5 %collective-permute-start.6 = (bf16[256,512]{1,0:T(8,128)(2,1)S(1)}, bf16[256,512]{1,0:T(8,128)(2,1)S(1)}, u32[]{:S(2)}, u32[]{:S(2)}) collective-permute-start(bf16[256,512]{1,0:T(8,128)(2,1)S(1)} %get-tuple-element.33), channel_id=1, source_target_pairs={{0,4},{1,3},{2,6},{3,1},{4,0},{5,9},{6,2},{7,11},{8,12},{9,5},{10,... | collective-permute-start | bytes 786440 | tf_op jit(solution)/shard_map/ppermute | solution.py:405
  23.0 3.6 %collective-permute-start.7 = (bf16[256,512]{1,0:T(8,128)(2,1)S(1)}, bf16[256,512]{1,0:T(8,128)(2,1)S(1)}, u32[]{:S(2)}, u32[]{:S(2)}) collective-permute-start(bf16[256,512]{1,0:T(8,128)(2,1)S(1)} %get-tuple-element.34), channel_id=1, source_target_pairs={{0,2},{1,5},{2,0},{3,7},{4,8},{5,1},{6,10},{7,3},{8,4},{9,13},{10,... | collective-permute-start | bytes 786440 | tf_op jit(solution)/shard_map/ppermute | solution.py:406
  26.6 0.0 collective-permute-done.9
  26.6 1.3 %collective-permute-start.10 = (f32[256,256]{1,0:T(8,128)S(1)}, f32[256,256]{1,0:T(8,128)S(1)}, u32[]{:S(2)}, u32[]{:S(2)}) collective-permute-start(f32[256,256]{1,0:T(8,128)S(1)} %convert_add_fusion.s_ref), channel_id=1, source_target_pairs={{0,1},{1,0},{2,3},{3,2},{4,5},{5,4},{6,7},{7,6},{8,9},{9,8},{10,11... | collective-permute-start | bytes 786440 | tf_op jit(solution)/shard_map/ppermute | solution.py:411
  27.9 0.0 collective-permute-done.6.a_ref
  27.9 4.4 %collective-permute-done.7.b_ref = bf16[256,512]{1,0:T(8,128)(2,1)S(1)} collective-permute-done((bf16[256,512]{1,0:T(8,128)(2,1)S(1)}, bf16[256,512]{1,0:T(8,128)(2,1)S(1)}, u32[]{:S(2)}, u32[]{:S(2)}) %collective-permute-start.7) | collective-permute-done | bytes 262176 | tf_op jit(solution)/shard_map/ppermute | solution.py:406
  32.3 0.0 collective-permute-done.10.t_ref
  32.3 1.5 %place.1 = (bf16[256,256]{1,0:T(8,128)(2,1)}, f32[256,256]{1,0:T(8,128)}, f32[256,128]{1,0:T(8,128)}, f32[256,128]{1,0:T(8,128)}) custom-call(s32[2]{0:T(128)S(1)} %copy-done.5, bf16[512,512]{1,0:T(8,128)(2,1)S(1)} %get-tuple-element.32.row_ref, bf16[256,512]{1,0:T(8,128)(2,1)S(1)} %collective-permute-done.6.a_ref, ...), custom_call_target="tpu_custom_call" | custom-call | tf_op jit(solution)/shard_map/place/pallas_call | solution.py:413
  (10 shorter events, 0.1 us)
Async XLA Ops:
  0.6 6.5 %copy-start.5 = (s32[2]{0:T(128)S(1)}, s32[2]{0:T(128)}, u32[]{:S(2)}) copy-start(s32[2]{0:T(128)} %plan.1) | copy-start | bytes 28
  0.6 13.4 %copy-start.1 = (bf16[256,256]{1,0:T(8,128)(2,1)S(1)}, bf16[256,256]{1,0:T(8,128)(2,1)}, u32[]{:S(2)}) copy-start(bf16[256,256]{1,0:T(8,128)(2,1)} %g_ref.3) | copy-start | bytes 393220
  0.7 13.4 %copy-start.2 = (bf16[256,128]{1,0:T(8,128)(2,1)S(1)}, bf16[256,128]{1,0:T(8,128)(2,1)}, u32[]{:S(2)}) copy-start(bf16[256,128]{1,0:T(8,128)(2,1)} %k_ref.3) | copy-start | bytes 196612
  0.7 13.4 %copy-start.3 = (bf16[256,128]{1,0:T(8,128)(2,1)S(1)}, bf16[256,128]{1,0:T(8,128)(2,1)}, u32[]{:S(2)}) copy-start(bf16[256,128]{1,0:T(8,128)(2,1)} %v_ref.3) | copy-start | bytes 196612
  1.8 12.3 %copy-start = (bf16[256,256]{1,0:T(8,128)(2,1)S(1)}, bf16[256,256]{1,0:T(8,128)(2,1)}, u32[]{:S(2)}) copy-start(bf16[256,256]{1,0:T(8,128)(2,1)} %q_ref.3) | copy-start | bytes 393220
  1.8 9.5 %collective-permute-start.1 = (bf16[256,640]{1,0:T(8,128)(2,1)S(1)}, bf16[256,640]{1,0:T(8,128)(2,1)S(1)}, u32[]{:S(2)}, u32[]{:S(2)}) collective-permute-start(bf16[256,640]{1,0:T(8,128)(2,1)S(1)} %get-tuple-element.22), channel_id=1, source_target_pairs={{0,2},{2,0},{4,6},{6,4},{8,10},{10,8},{12,14},{14,12},{1,3},{3,1},... | collective-permute-start | bytes 983048 | tf_op jit(solution)/shard_map/ppermute | solution.py:365
  3.9 7.4 %collective-permute-start = (bf16[256,256]{1,0:T(8,128)(2,1)S(1)}, bf16[256,256]{1,0:T(8,128)(2,1)S(1)}, u32[]{:S(2)}, u32[]{:S(2)}) collective-permute-start(bf16[256,256]{1,0:T(8,128)(2,1)S(1)} %get-tuple-element.21), channel_id=1, source_target_pairs={{0,4},{1,7},{2,6},{3,5},{4,8},{5,11},{6,10},{7,9},{8,12},{9,15},{1... | collective-permute-start | bytes 393224 | tf_op jit(solution)/shard_map/ppermute | solution.py:366
  7.1 4.3 %collective-permute-start.2 = (s32[2]{0:T(128)S(1)}, s32[2]{0:T(128)S(1)}, u32[]{:S(2)}, u32[]{:S(2)}) collective-permute-start(s32[2]{0:T(128)S(1)} %copy-done.5), channel_id=1, source_target_pairs={{0,4},{1,3},{2,6},{3,1},{4,0},{5,9},{6,2},{7,11},{8,12},{9,5},{10,... | collective-permute-start | bytes 32 | tf_op jit(solution)/shard_map/ppermute | solution.py:367
  11.4 2.7 %collective-permute-start.3 = (bf16[1,256,256]{2,1,0:T(8,128)(2,1)S(1)}, bf16[1,256,256]{2,1,0:T(8,128)(2,1)S(1)}, u32[]{:S(2)}, u32[]{:S(2)}) collective-permute-start(bf16[1,256,256]{2,1,0:T(8,128)(2,1)S(1)} %bitcast.3), channel_id=1, source_target_pairs={{0,1},{1,0},{2,3},{3,2},{4,5},{5,4},{6,7},{7,6},{8,9},{9,8},{10,11... | collective-permute-start | bytes 393224 | tf_op jit(solution)/shard_map/ppermute | solution.py:370
  12.6 1.1 %collective-permute-start.5 = (s32[2]{0:T(128)S(1)}, s32[2]{0:T(128)S(1)}, u32[]{:S(2)}, u32[]{:S(2)}) collective-permute-start(s32[2]{0:T(128)S(1)} %collective-permute-done.2), channel_id=1, source_target_pairs={{0,1},{1,0},{2,3},{3,2},{4,5},{5,4},{6,7},{7,6},{8,9},{9,8},{10,11... | collective-permute-start | bytes 32 | tf_op jit(solution)/shard_map/ppermute | solution.py:372
  12.6 1.5 %copy-start.4 = (s32[16]{0:T(128)S(1)}, s32[16]{0:T(128)}, u32[]{:S(2)}) copy-start(s32[16]{0:T(128)} %lens.3) | copy-start | bytes 196
  12.6 1.5 %collective-permute-start.4 = (bf16[256,128]{1,0:T(8,128)(2,1)S(1)}, bf16[256,128]{1,0:T(8,128)(2,1)S(1)}, u32[]{:S(2)}, u32[]{:S(2)}) collective-permute-start(bf16[256,128]{1,0:T(8,128)(2,1)S(1)} %slice.3), channel_id=1, source_target_pairs={{0,1},{1,0},{2,3},{3,2},{4,5},{5,4},{6,7},{7,6},{8,9},{9,8},{10,11... | collective-permute-start | bytes 196616 | tf_op jit(solution)/shard_map/ppermute | solution.py:371
  16.6 1.4 %collective-permute-start.8 = (bf16[1,256,256]{2,1,0:T(8,128)(2,1)S(1)}, bf16[1,256,256]{2,1,0:T(8,128)(2,1)S(1)}, u32[]{:S(2)}, u32[]{:S(2)}) collective-permute-start(bf16[1,256,256]{2,1,0:T(8,128)(2,1)S(1)} %get-tuple-element.37), channel_id=1, source_target_pairs={{0,1},{1,0},{2,3},{3,2},{4,5},{5,4},{6,7},{7,6},{8,9},{9,8},{10,11... | collective-permute-start | bytes 393224 | tf_op jit(solution)/shard_map/ppermute | solution.py:394
  18.1 8.5 %collective-permute-start.9 = (bf16[256,256]{1,0:T(8,128)(2,1)S(1)}, bf16[256,256]{1,0:T(8,128)(2,1)S(1)}, u32[]{:S(2)}, u32[]{:S(2)}) collective-permute-start(bf16[256,256]{1,0:T(8,128)(2,1)S(1)} %fusion), channel_id=1, source_target_pairs={{2,0},{4,2},{5,1},{6,4},{7,3},{8,6},{9,5},{10,8},{11,7},{12,10},{1... | collective-permute-start | bytes 393224 | tf_op jit(solution)/shard_map/ppermute | solution.py:410
  21.5 6.4 %collective-permute-start.6 = (bf16[256,512]{1,0:T(8,128)(2,1)S(1)}, bf16[256,512]{1,0:T(8,128)(2,1)S(1)}, u32[]{:S(2)}, u32[]{:S(2)}) collective-permute-start(bf16[256,512]{1,0:T(8,128)(2,1)S(1)} %get-tuple-element.33), channel_id=1, source_target_pairs={{0,4},{1,3},{2,6},{3,1},{4,0},{5,9},{6,2},{7,11},{8,12},{9,5},{10,... | collective-permute-start | bytes 786440 | tf_op jit(solution)/shard_map/ppermute | solution.py:405
  23.0 9.3 %collective-permute-start.7 = (bf16[256,512]{1,0:T(8,128)(2,1)S(1)}, bf16[256,512]{1,0:T(8,128)(2,1)S(1)}, u32[]{:S(2)}, u32[]{:S(2)}) collective-permute-start(bf16[256,512]{1,0:T(8,128)(2,1)S(1)} %get-tuple-element.34), channel_id=1, source_target_pairs={{0,2},{1,5},{2,0},{3,7},{4,8},{5,1},{6,10},{7,3},{8,4},{9,13},{10,... | collective-permute-start | bytes 786440 | tf_op jit(solution)/shard_map/ppermute | solution.py:406
  26.6 5.7 %collective-permute-start.10 = (f32[256,256]{1,0:T(8,128)S(1)}, f32[256,256]{1,0:T(8,128)S(1)}, u32[]{:S(2)}, u32[]{:S(2)}) collective-permute-start(f32[256,256]{1,0:T(8,128)S(1)} %convert_add_fusion.s_ref), channel_id=1, source_target_pairs={{0,1},{1,0},{2,3},{3,2},{4,5},{5,4},{6,7},{7,6},{8,9},{9,8},{10,11... | collective-permute-start | bytes 786440 | tf_op jit(solution)/shard_map/ppermute | solution.py:411

commit v3 on v2

v3 whole, which is shorter than its diff:
```python
import math

import jax
import jax.numpy as jnp
from jax import lax
from jax.experimental import pallas as pl
from jax.experimental.pallas import tpu as pltpu
from jax.sharding import PartitionSpec as P

DOC_CAP = 4096
NEG = -1e30


LOG2E = 1.4426950408889634
CHUNK = 128

VMEM = pl.BlockSpec(memory_space=pltpu.VMEM)
SMEM = pl.BlockSpec(memory_space=pltpu.SMEM)


def nt(a, b):
    return lax.dot_general(a, b, (((1,), (1,)), ((), ())), preferred_element_type=jnp.float32)


def nn(a, b):
    return lax.dot_general(a, b, (((1,), (0,)), ((), ())), preferred_element_type=jnp.float32)


def tn(a, b):
    return lax.dot_general(a, b, (((0,), (0,)), ((), ())), preferred_element_type=jnp.float32)


def fold(a, op):
    rows = a.shape[0] // 8
    parts = a.reshape(rows, 8, a.shape[1])
    return op(parts, axis=0)


def scalars(ref, count):
    row = ref[...]
    lane = lax.broadcasted_iota(jnp.int32, row.shape, 1)
    return [jnp.sum(jnp.where(lane == i, row, 0)) for i in range(count)]


def up_down(z, flip):
    return z + 1 - 2 * ((z + flip) % 2)


def row_pairs(rows):
    pairs = ([], [])
    for z in range(rows):
        for x in range(2):
            for h in range(2):
                for way in range(2):
                    to = z + 1 - 2 * ((z + (h ^ way)) % 2)
                    other = (to, x) if 0 <= to < rows else (z, 1 - x)
                    node = 4 * z + 2 * x + h
                    pairs[way].append((node, 4 * other[0] + 2 * other[1] + h))
    return pairs


def pack_kernel(plan_ref, k_ref, v_ref, q_ref, g_ref, plan_out, kv_ref, half_ref, qg_ref, sems):
    side = lax.axis_index("head")
    dim = k_ref.shape[1]
    width = q_ref.shape[1]
    moves = (
        (k_ref, kv_ref.at[:, :dim]),
        (v_ref, kv_ref.at[:, dim:]),
        (q_ref, qg_ref.at[:, :width]),
        (g_ref, qg_ref.at[:, width:]),
        (plan_ref, plan_out),
    )
    copies = [pltpu.make_async_copy(a, b, sems.at[i]) for i, (a, b) in enumerate(moves)]
    for copy in copies:
        copy.start()
    for copy in copies[:2]:
        copy.wait()

    @pl.when(side == 0)
    def _():
        half_ref[...] = kv_ref[:, :dim]

    @pl.when(side == 1)
    def _():
        half_ref[...] = kv_ref[:, dim:]

    for copy in copies[2:]:
        copy.wait()


def loop(count, body, carry):
    if count <= 8:
        for j in range(count):
            carry = body(j, carry)
        return carry
    return lax.fori_loop(0, count, body, carry)

def rows_at(c):
    start = c * CHUNK
    return pl.ds(start if isinstance(start, int) else pl.multiple_of(start, CHUNK), CHUNK)


def contract(sizes, low, buf, ref, i):
    rounds, reach, tok, heads, head_dim = sizes
    lanes = heads * CHUNK
    span = 2 * reach + 2
    slot = slice(i * lanes, (i + 1) * lanes)
    if span <= 8:
        rows = (2 * reach + 1) * CHUNK
        at = pl.ds(pl.multiple_of((low + i) * CHUNK, CHUNK), rows)
        return tn(buf[at, :], ref[i * CHUNK:i * CHUNK + rows, slot])

    def add(j, acc):
        return acc + tn(buf[rows_at(low + j), :], ref[rows_at(j), slot])

    return lax.fori_loop(0, span, add, jnp.zeros((head_dim, lanes), jnp.float32))


def two_stretches(sizes, begin_ref, z, column, kbuf, vbuf, q_all, g_all, w_ref, p_ref, d_ref,
                  od_ref, blocks, put):
    rounds, reach, tok, heads, head_dim = sizes
    inv_root = 1.0 / math.sqrt(head_dim)
    width = heads * head_dim
    lanes = heads * CHUNK
    span = 2 * reach + 2
    unrolled = span <= 8
    low = 4 * rounds + 2 * column - 2 * reach
    low_place = (2 * (z - rounds) * tok) + low * CHUNK
    q, g, places, begin = [], [], [], []
    for i in range(2):
        rows = slice(i * CHUNK, (i + 1) * CHUNK)
        q.append(jnp.concatenate(
            [q_all[rows, h * head_dim:(h + 1) * head_dim] for h in range(heads)], axis=0))
        g.append(jnp.concatenate(
            [g_all[rows, h * head_dim:(h + 1) * head_dim] for h in range(heads)], axis=0))
        lane = lax.broadcasted_iota(jnp.int32, (1, lanes), 1) % CHUNK
        place = (2 * z + column) * tok + i * CHUNK + lane
        places.append(place)
        begin.append(begin_ref[i:i + 1, :])

    def slots(j):
        if not unrolled:
            return (0, 1)
        return tuple(i for i in range(2) if i <= j <= 2 * reach + i)

    def scores(j, tops):
        tops = list(tops)
        k = kbuf[rows_at(low + j), :]
        at = low_place + j * CHUNK + lax.broadcasted_iota(jnp.int32, (CHUNK, lanes), 0)
        for i in slots(j):
            allowed = at >= begin[i]
            if not unrolled or j == 2 * reach + i:
                allowed = allowed & (at <= places[i])
            s = jnp.where(allowed, nt(k, q[i]) * (inv_root * LOG2E), NEG)
            w_ref[i, j] = s
            tops[i] = jnp.maximum(tops[i], fold(s, jnp.max))
        return tuple(tops)

    full = lambda value: tuple(jnp.full((8, lanes), value, jnp.float32) for _ in range(2))
    tops = loop(span, scores, full(NEG))
    tops = [jnp.max(t, axis=0, keepdims=True) for t in tops]

    def exps(j, totals):
        totals = list(totals)
        for i in slots(j):
            e = jnp.exp2(w_ref[i, j] - tops[i])
            w_ref[i, j] = e
            p_ref[rows_at(j), slice(i * lanes, (i + 1) * lanes)] = e.astype(jnp.bfloat16)
            totals[i] = totals[i] + fold(e, jnp.sum)
        return tuple(totals)

    totals = loop(span, exps, full(0.0))
    scale = [1.0 / jnp.sum(t, axis=0, keepdims=True) for t in totals]
    dots = []
    for i in range(2):
        attended = (contract(sizes, low, vbuf, p_ref, i) * scale[i]).T.astype(jnp.bfloat16)
        for h in range(heads):
            od_ref[i * CHUNK:(i + 1) * CHUNK, h * head_dim:(h + 1) * head_dim] = (
                attended[h * CHUNK:(h + 1) * CHUNK])
        product = g[i].astype(jnp.float32) * attended.astype(jnp.float32)
        dots.append(jnp.sum(product.T, axis=0, keepdims=True))

    def backward(j, carry):
        v = vbuf[rows_at(low + j), :]
        for i in range(2):
            if i in slots(j):
                w = w_ref[i, j] * scale[i]
                ds = (w * (nt(v, g[i]) - dots[i])).astype(jnp.bfloat16)
                d_ref[rows_at(j), slice(i * lanes, (i + 1) * lanes)] = ds
                p_ref[rows_at(j), slice(i * lanes, (i + 1) * lanes)] = w.astype(jnp.bfloat16)
            else:
                blank = jnp.zeros((CHUNK, lanes), jnp.bfloat16)
                d_ref[rows_at(j), slice(i * lanes, (i + 1) * lanes)] = blank
                p_ref[rows_at(j), slice(i * lanes, (i + 1) * lanes)] = blank
        return carry

    loop(span, backward, 0)
    q_both = jnp.concatenate(q, axis=0)
    g_both = jnp.concatenate(g, axis=0)

    def keys(m, carry):
        first, count = blocks
        b = first + 2 * m
        start = b * tok
        at = pl.ds(start if isinstance(start, int) else pl.multiple_of(start, tok), tok)
        put(count - 1 - m, nn(d_ref[at, :], q_both) * inv_root, nn(p_ref[at, :], g_both))
        return carry

    loop(blocks[1], keys, 0)


def query_grads(sizes, column, kbuf, d_ref, od_ref):
    rounds, reach, tok, heads, head_dim = sizes
    inv_root = 1.0 / math.sqrt(head_dim)
    low = 4 * rounds + 2 * column - 2 * reach
    width = heads * head_dim
    for i in range(2):
        grad = (contract(sizes, low, kbuf, d_ref, i) * inv_root).T.astype(jnp.bfloat16)
        for h in range(heads):
            at = width + h * head_dim
            od_ref[i * CHUNK:(i + 1) * CHUNK, at:at + head_dim] = (
                grad[h * CHUNK:(h + 1) * CHUNK])


def own_kernel(sizes):
    rounds, reach, tok, heads, head_dim = sizes

    def kernel(begin_ref, k_ref, v_ref, q_ref, g_ref, mine_ref, other_ref, half_ref, cross_ref,
               att_ref, d_ref, kv_out, kbuf, vbuf, w_ref, p_ref):
        here = lax.axis_index("ctx")
        side = lax.axis_index("head")
        z = here // 2
        x = here % 2

        for r in range(rounds):
            for ref, column in ((mine_ref, (x + side) % 2), (other_ref, (x + 1 - side) % 2)):
                at = pl.ds(pl.multiple_of((2 * (rounds - 1 - r) + column) * tok, tok), tok)
                kbuf[at, :] = ref[r, :, :head_dim]
                vbuf[at, :] = ref[r, :, head_dim:]
        own = pl.ds(pl.multiple_of((2 * rounds + x) * tok, tok), tok)
        kbuf[own, :] = k_ref[...]
        vbuf[own, :] = v_ref[...]
        next_to = pl.ds(pl.multiple_of((2 * rounds + 1 - x) * tok, tok), tok)

        @pl.when(side == 0)
        def _():
            kbuf[next_to, :] = half_ref[...]
            vbuf[next_to, :] = cross_ref[...]

        @pl.when(side == 1)
        def _():
            vbuf[next_to, :] = half_ref[...]
            kbuf[next_to, :] = cross_ref[...]

        def put(r, dk, dv):
            kv_out[r, :, :head_dim] = dk
            kv_out[r, :, head_dim:] = dv

        two_stretches(sizes, begin_ref, z, x, kbuf, vbuf, q_ref, g_ref, w_ref, p_ref, d_ref,
                      att_ref, (0, rounds + 1), put)

    return kernel


def next_kernel(sizes):
    rounds, reach, tok, heads, head_dim = sizes
    width = heads * head_dim

    def kernel(begin_ref, kbuf, vbuf, qg_ref, own_kv, att_ref, d_ref, kv_out, far_out,
               w_ref, p_ref, sums):
        here = lax.axis_index("ctx")
        z = here // 2
        x = here % 2
        sums[...] = own_kv[...]

        def put(r, dk, dv):
            at = r + x
            sums[at, :, :head_dim] = sums[at, :, :head_dim] + dk
            sums[at, :, head_dim:] = sums[at, :, head_dim:] + dv

        two_stretches(sizes, begin_ref, z, 1 - x, kbuf, vbuf, qg_ref.at[:, :width],
                      qg_ref.at[:, width:], w_ref, p_ref, d_ref, att_ref, (1, rounds), put)
        kv_out[...] = sums[0]
        far_out[...] = sums[1:].astype(far_out.dtype)

    return kernel


def send_kernel(sizes):
    rounds, reach, tok, heads, head_dim = sizes
    width = heads * head_dim

    def kernel(plan_ref, kbuf, d_own, d_next, att_own, att_next, od_ref, send_a, send_b):
        here = lax.axis_index("ctx")
        side = lax.axis_index("head")
        x = here % 2
        plan = scalars(plan_ref, 4)
        for at, column, att, d_ref in ((0, x, att_own, d_own), (tok, 1 - x, att_next, d_next)):
            rows = od_ref.at[at:at + tok, :]
            rows[:, :width] = att[...]
            query_grads(sizes, column, kbuf, d_ref, rows)
        for way, out in enumerate((send_a, send_b)):
            flip = (side + way) % 2
            for i in range(2):
                wanted = jnp.where(flip == 0, plan[i], plan[2 + i])
                out[i * CHUNK:(i + 1) * CHUNK, :] = od_ref[row_of(wanted, x), :]

    return kernel


def row_of(wanted, x):
    inner = wanted % 4
    return pl.ds(pl.multiple_of(((inner + 2 * x) % 4) * CHUNK, CHUNK), CHUNK)


def place_kernel(width):
    def kernel(plan_ref, row_ref, a_ref, b_ref, s_ref, t_ref, out_ref, dq_ref, dk_ref, dv_ref):
        here = lax.axis_index("ctx")
        side = lax.axis_index("head")
        z = here // 2
        source_a = up_down(z, side)
        plan = scalars(plan_ref, 2)
        for slot in range(2):
            wanted = plan[slot]
            to = pl.ds(slot * CHUNK, CHUNK)
            inside = row_of(wanted, here % 2)

            def put(rows):
                out_ref[to, :] = rows[:, :width]
                dq_ref[to, :] = rows[:, width:].astype(jnp.float32)

            home = wanted // 4 == z
            from_a = wanted // 4 == source_a
            pl.when(home)(lambda: put(row_ref[inside, :]))
            pl.when(from_a)(lambda: put(a_ref[to, :]))
            pl.when(jnp.logical_not(home | from_a))(lambda: put(b_ref[to, :]))
        half = dk_ref.shape[1]
        dk_ref[...] = s_ref[:, :half] + t_ref[:, :half]
        dv_ref[...] = s_ref[:, half:] + t_ref[:, half:]

    return kernel


def per_device(queries, key_input, value_input, grad_out, doc_lengths, stretch_plan):
    tok, head_dim = key_input.shape
    width = queries.shape[1]
    heads = width // head_dim
    n = lax.axis_size("ctx")
    rounds = (min(DOC_CAP, tok * n // 4) // tok + 1) // 2
    reach = 2 * rounds
    bf16, f32 = jnp.bfloat16, jnp.float32
    both = ("ctx", "head")
    cross = [(0, 1), (1, 0)]
    side = lax.axis_index("head")

    here = lax.axis_index("ctx")
    order = jnp.arange(doc_lengths.shape[0], dtype=jnp.int32)
    bounds = jnp.sum(jnp.where(order[None, :] <= order[:, None], doc_lengths[None, :], 0), axis=1)

    def begins(device):
        places = device * tok + jnp.arange(tok, dtype=jnp.int32)
        starts = jnp.max(jnp.where(bounds[:, None] <= places[None, :], bounds[:, None], 0), axis=0)
        starts = starts.reshape(tok // CHUNK, 1, CHUNK)
        return jnp.broadcast_to(starts, (tok // CHUNK, heads, CHUNK)).reshape(tok // CHUNK, -1)

    def lanes_of(values):
        return jnp.pad(values, (0, 128 - values.shape[0])).reshape(1, 128)

    def fetch_pairs(r):
        pairs = []
        for s in range(n):
            for h in range(2):
                to = s // 2 + r + 1
                if to < n // 2:
                    pairs.append((2 * s + h, 2 * (2 * to + (s + h) % 2) + h))
        return pairs

    def back_pairs(r):
        return [(s, s - 2 * r) for s in range(2 * r, n)]

    plan_out, own_kv, half, queries_grads = pl.pallas_call(
        pack_kernel,
        out_shape=(
            pltpu.VMEM(stretch_plan.shape, jnp.int32),
            pltpu.VMEM((tok, 2 * head_dim), bf16),
            pltpu.VMEM((tok, head_dim), bf16),
            pltpu.VMEM((tok, 2 * width), bf16),
        ),
        in_specs=[pl.BlockSpec(memory_space=pl.ANY)] * 5,
        out_specs=(VMEM,) * 4,
        scratch_shapes=[pltpu.SemaphoreType.DMA((5,))],
        name="pack",
    )(stretch_plan, key_input, value_input, queries, grad_out)
    tie_a, tie_b = row_pairs(n // 2)
    near = [(i, i ^ 1) for i in range(n)]
    part = lax.ppermute(queries_grads, "ctx", near)
    half_next = lax.ppermute(half, "ctx", near)
    mine = [lax.ppermute(own_kv, both, fetch_pairs(r)) for r in range(rounds)]
    mine = jnp.stack(mine)
    other = lax.ppermute(mine, "head", cross)
    half_cross = lax.ppermute(half_next, "head", cross)
    sizes = (rounds, reach, tok, heads, head_dim)
    params = pltpu.CompilerParams(vmem_limit_bytes=40 << 20)
    span = 2 * reach + 2
    weights = pltpu.VMEM((span * CHUNK, 2 * heads * CHUNK), bf16)
    scores = pltpu.VMEM((2, span, CHUNK, heads * CHUNK), f32)
    buffer = jax.ShapeDtypeStruct(((2 * rounds + 2) * tok, head_dim), bf16)
    rows = jax.ShapeDtypeStruct((tok, 2 * width), bf16)
    attended = jax.ShapeDtypeStruct((tok, width), bf16)
    grads = jax.ShapeDtypeStruct((span * CHUNK, 2 * heads * CHUNK), bf16)
    key_sums = jax.ShapeDtypeStruct((rounds + 1, tok, 2 * head_dim), f32)
    att_own, d_own, kv_own, kbuf, vbuf = pl.pallas_call(
        own_kernel(sizes),
        out_shape=(attended, grads, key_sums, buffer, buffer),
        in_specs=[VMEM] * 9,
        out_specs=(VMEM,) * 5,
        scratch_shapes=[scores, weights],
        compiler_params=params,
        name="attend_own",
    )(begins(here), key_input, value_input, queries, grad_out, mine, other, half_next,
      half_cross)
    kv_own, stretch_here = lax.optimization_barrier((kv_own, plan_out))
    plan_mine = lax.ppermute(stretch_here, both, tie_a)
    plan_other = lax.ppermute(plan_mine, "head", cross)
    plans = jnp.where(side == 0, jnp.concatenate([plan_mine, plan_other]),
                      jnp.concatenate([plan_other, plan_mine]))
    att_next, d_next, kv_sum, far = pl.pallas_call(
        next_kernel(sizes),
        out_shape=(
            attended, grads, jax.ShapeDtypeStruct((tok, 2 * head_dim), f32),
            jax.ShapeDtypeStruct((rounds, tok, 2 * head_dim), bf16),
        ),
        in_specs=[VMEM] * 5,
        out_specs=(VMEM,) * 4,
        scratch_shapes=[scores, weights, pltpu.VMEM((rounds + 1, tok, 2 * head_dim), f32)],
        compiler_params=params,
        name="attend_next",
    )(begins(here ^ 1), kbuf, vbuf, part, kv_own)
    od, send_a, send_b = pl.pallas_call(
        send_kernel(sizes),
        out_shape=(jax.ShapeDtypeStruct((2 * tok, 2 * width), bf16), rows, rows),
        in_specs=[VMEM] * 6,
        out_specs=(VMEM,) * 3,
        compiler_params=params,
        name="send_rows",
    )(lanes_of(plans), kbuf, d_own, d_next, att_own, att_next)

    moved_a = lax.ppermute(send_a, both, tie_a)
    moved_b = lax.ppermute(send_b, both, tie_b)
    total = kv_sum
    for r in range(rounds):
        total = total + lax.ppermute(far[r], "ctx", back_pairs(r + 1)).astype(f32)
    total_other = lax.ppermute(total, "head", cross)

    output, query_grad, key_grad, value_grad = pl.pallas_call(
        place_kernel(width),
        out_shape=(
            jax.ShapeDtypeStruct((tok, width), bf16),
            jax.ShapeDtypeStruct((tok, width), f32),
            jax.ShapeDtypeStruct((tok, head_dim), f32),
            jax.ShapeDtypeStruct((tok, head_dim), f32),
        ),
        in_specs=[VMEM] * 6,
        out_specs=(VMEM,) * 4,
        compiler_params=pltpu.CompilerParams(vmem_limit_bytes=32 << 20),
        name="place",
    )(lanes_of(stretch_plan), od, moved_a, moved_b, total, total_other)
    return (output, query_grad, key_grad, value_grad)


def solution(mesh):
    return jax.shard_map(
        per_device,
        mesh=mesh,
        in_specs=(
            P(("groups", "ctx"), "head"),
            P(("groups", "ctx"), None),
            P(("groups", "ctx"), None),
            P(("groups", "ctx"), "head"),
            P("groups"),
            P(("groups", "ctx")),
        ),
        out_specs=(
            P(("groups", "ctx"), "head"),
            P(("groups", "ctx"), "head"),
            P(("groups", "ctx"), None),
            P(("groups", "ctx"), None),
        ),
        check_vma=False,
    )
```

time: 34.3 us -> 31.6 us (0.921)
  waiting for transfers between devices: 9.19 us -> 6.47 us
  Pallas kernels: 7.25 us -> 5.8 us
  local copies, waits for them, and re-layouts: 0.03 us -> 1.01 us
  starting transfers between devices: 16.4 us -> 16.9 us
    ppermute x5, waiting for transfers between devices: 4.25 us -> 0.01 us  [the longest x1 0.01 us: per_device(): part = lax.ppermute(queries_grads, 'ctx', near)]
    ppermute x1, starting transfers between devices: 0.01 us -> 1.76 us  [per_device(): plan_other = lax.ppermute(plan_mine, 'head', cross)]
    pallas_call x3 -> x4, Pallas kernels: 5.77 us -> 4.75 us  [the longest x1 1.6 us: per_device(): pl.pallas_call(own_kernel(sizes), out_shape=(attended, grads, key_sums, b...]
    ppermute x1, waiting for transfers between devices: 0.01 us -> 0.97 us  [per_device(): other = lax.ppermute(mine, 'head', cross)]
    unnamed x12 -> x16, local copies, waits for them, and re-layouts: 0.03 us -> 1 us
    ppermute x1, starting transfers between devices: 1.27 us -> 0.31 us  [per_device(): total_other = lax.ppermute(total, 'head', cross)]
    ppermute x5, starting transfers between devices: 5.66 us -> 6.52 us  [the longest x1 2.11 us: per_device(): half_next = lax.ppermute(half, 'ctx', near)]
    ppermute x1, waiting for transfers between devices: 0.01 us -> 0.71 us  [per_device(): moved_a = lax.ppermute(send_a, both, tie_a)]
  transfers between devices with their start and end apart: 11 -> 11, of which waited for: 5 -> 4; matrix products, arithmetic and copies ran while one was open for 0% -> 1% of each run, Pallas kernels for 6% -> 12%
where the time goes in v3:
time: 31.6 us; the launch traced here: 31.2 us
  starting transfers between devices  16.9 us (53%)
  waiting for transfers between devices  6.47 us (20%)
  Pallas kernels  5.8 us (18%)
  local copies, waits for them, and re-layouts  1.01 us (3%)
  between operations  0.75 us (2%)
    ppermute x1, waiting for transfers between devices, per_device(): moved_b = lax.ppermute(send_b, both, tie_b)  3.95 us
    ppermute x1, starting transfers between devices, per_device(): mine = [lax.ppermute(own_kv, both, fetch_pairs(r)) for r in range(rounds)]  3.17 us
    ppermute x1, starting transfers between devices, per_device(): moved_b = lax.ppermute(send_b, both, tie_b)  2.98 us
    ppermute x1, starting transfers between devices, per_device(): half_next = lax.ppermute(half, 'ctx', near)  2.11 us
    ppermute x1, starting transfers between devices, per_device(): plan_other = lax.ppermute(plan_mine, 'head', cross)  1.76 us
    pallas_call x1, Pallas kernels, per_device(): pl.pallas_call(own_kernel(sizes), out_shape=(attended, grads, key_sums, b...  1.6 us
    pallas_call x1, Pallas kernels, per_device(): pl.pallas_call(next_kernel(sizes), out_shape=(attended, grads, jax.ShapeD...  1.47 us
    ppermute x1, starting transfers between devices, per_device(): total = total + lax.ppermute(far[r], 'ctx', back_pairs(r + 1)).astype(f32)  1.29 us
  transfers between devices with their start and end apart: 11, of which 4 were waited for; matrix products, arithmetic and copies ran while one was open for 1% of the time, Pallas kernels for 12%

profile of v3, /device:TPU:1, one launch (start us, length us, event | category | flops | bytes accessed | tf_op | source)
XLA Modules:
  0.0 31.2 jit_solution(181051801818077833)
XLA Ops:
  0.7 1.1 %pack.1 = (s32[2]{0:T(128)S(1)}, bf16[256,256]{1,0:T(8,128)(2,1)S(1)}, bf16[256,128]{1,0:T(8,128)(2,1)S(1)}, bf16[256,512]{1,0:T(8,128)(2,1)S(1)}) custom-call(s32[2]{0:T(128)} %plan_ref.1, bf16[256,128]{1,0:T(8,128)(2,1)} %k_ref.3, bf16[256,128]{1,0:T(8,128)(2,1)} %v_ref.3, bf16[256,256]{1,0:T(8,128)(2,1)} %q_ref.3, bf16[256,256]{1,0:T(8,128)(2,1)} %g_ref.3), custom_call_target="tpu_custom_call" | custom-call | tf_op jit(solution)/shard_map/pack/pallas_call | solution.py:381
  1.8 2.1 %collective-permute-start.2 = (bf16[256,128]{1,0:T(8,128)(2,1)S(1)}, bf16[256,128]{1,0:T(8,128)(2,1)S(1)}, u32[]{:S(2)}, u32[]{:S(2)}) collective-permute-start(bf16[256,128]{1,0:T(8,128)(2,1)S(1)} %get-tuple-element.23), channel_id=1, source_target_pairs={{0,2},{2,0},{4,6},{6,4},{8,10},{10,8},{12,14},{14,12},{1,3},{3,1},... | collective-permute-start | bytes 196616 | tf_op jit(solution)/shard_map/ppermute | solution.py:397
  3.9 3.2 %collective-permute-start = (bf16[256,256]{1,0:T(8,128)(2,1)S(1)}, bf16[256,256]{1,0:T(8,128)(2,1)S(1)}, u32[]{:S(2)}, u32[]{:S(2)}) collective-permute-start(bf16[256,256]{1,0:T(8,128)(2,1)S(1)} %get-tuple-element.22), channel_id=1, source_target_pairs={{0,4},{1,7},{2,6},{3,5},{4,8},{5,11},{6,10},{7,9},{8,12},{9,15},{1... | collective-permute-start | bytes 393224 | tf_op jit(solution)/shard_map/ppermute | solution.py:398
  7.1 1.3 %collective-permute-start.6 = (bf16[256,512]{1,0:T(8,128)(2,1)S(1)}, bf16[256,512]{1,0:T(8,128)(2,1)S(1)}, u32[]{:S(2)}, u32[]{:S(2)}) collective-permute-start(bf16[256,512]{1,0:T(8,128)(2,1)S(1)} %get-tuple-element.30), channel_id=1, source_target_pairs={{0,2},{2,0},{4,6},{6,4},{8,10},{10,8},{12,14},{14,12},{1,3},{3,1},... | collective-permute-start | bytes 786440 | tf_op jit(solution)/shard_map/ppermute | solution.py:396
  8.4 0.7 %copy-done.5 = s32[16]{0:T(128)S(1)} copy-done((s32[16]{0:T(128)S(1)}, s32[16]{0:T(128)}, u32[]{:S(2)}) %copy-start.5) | copy-done | bytes 88
  9.0 0.1 select_reduce_fusion.2
  9.2 0.1 select_reduce_fusion
  9.2 0.0 collective-permute-done.2.half_ref
  9.3 0.7 %collective-permute-start.3 = (bf16[256,128]{1,0:T(8,128)(2,1)S(1)}, bf16[256,128]{1,0:T(8,128)(2,1)S(1)}, u32[]{:S(2)}, u32[]{:S(2)}) collective-permute-start(bf16[256,128]{1,0:T(8,128)(2,1)S(1)} %collective-permute-done.2.half_ref), channel_id=1, source_target_pairs={{0,1},{1,0},{2,3},{3,2},{4,5},{5,4},{6,7},{7,6},{8,9},{9,8},{10,11... | collective-permute-start | bytes 196616 | tf_op jit(solution)/shard_map/ppermute | solution.py:401
  9.9 0.0 collective-permute-done
  9.9 0.9 %collective-permute-start.1 = (bf16[1,256,256]{2,1,0:T(8,128)(2,1)S(1)}, bf16[1,256,256]{2,1,0:T(8,128)(2,1)S(1)}, u32[]{:S(2)}, u32[]{:S(2)}) collective-permute-start(bf16[1,256,256]{2,1,0:T(8,128)(2,1)S(1)} %bitcast.18), channel_id=1, source_target_pairs={{0,1},{1,0},{2,3},{3,2},{4,5},{5,4},{6,7},{7,6},{8,9},{9,8},{10,11... | collective-permute-start | bytes 393224 | tf_op jit(solution)/shard_map/ppermute | solution.py:400
  10.9 0.0 collective-permute-done.3.cross_ref
  10.9 1.0 %collective-permute-done.1.other_ref = bf16[1,256,256]{2,1,0:T(8,128)(2,1)S(1)} collective-permute-done((bf16[1,256,256]{2,1,0:T(8,128)(2,1)S(1)}, bf16[1,256,256]{2,1,0:T(8,128)(2,1)S(1)}, u32[]{:S(2)}, u32[]{:S(2)}) %collective-permute-start.1) | collective-permute-done | bytes 131104 | tf_op jit(solution)/shard_map/ppermute | solution.py:400
  11.9 1.6 %attend_own.1 = (bf16[256,256]{1,0:T(8,128)(2,1)S(1)}, bf16[768,512]{1,0:T(8,128)(2,1)S(1)}, f32[2,256,256]{2,1,0:T(8,128)S(1)}, bf16[1024,128]{1,0:T(8,128)(2,1)S(1)}, bf16[1024,128]{1,0:T(8,128)(2,1)S(1)}) custom-call(s32[2,256]{1,0:T(2,128)S(1)} %bitcast.21, bf16[256,128]{1,0:T(8,128)(2,1)S(1)} %copy-done.2, bf16[256,128]{1,0:T(8,128)(2,1)S(1)} %copy-done.3, ...), custom_call_target="tpu_custom_call" | custom-call | tf_op jit(solution)/shard_map/attend_own/pallas_call | solution.py:412
  13.5 1.2 %collective-permute-start.4 = (s32[2]{0:T(128)S(1)}, s32[2]{0:T(128)S(1)}, u32[]{:S(2)}, u32[]{:S(2)}) collective-permute-start(s32[2]{0:T(128)S(1)} %get-tuple-element.26), channel_id=1, source_target_pairs={{0,4},{1,3},{2,6},{3,1},{4,0},{5,9},{6,2},{7,11},{8,12},{9,5},{10,... | collective-permute-start | bytes 32 | tf_op jit(solution)/shard_map/ppermute | solution.py:423
  14.7 0.0 collective-permute-done.6.qg_ref
  14.7 1.5 %attend_next.1 = (bf16[256,256]{1,0:T(8,128)(2,1)S(1)}, bf16[768,512]{1,0:T(8,128)(2,1)S(1)}, f32[256,256]{1,0:T(8,128)S(1)}, bf16[1,256,256]{2,1,0:T(8,128)(2,1)S(1)}) custom-call(s32[2,256]{1,0:T(2,128)S(1)} %bitcast.20, bf16[1024,128]{1,0:T(8,128)(2,1)S(1)} %get-tuple-element.27.kbuf, bf16[1024,128]{1,0:T(8,128)(2,1)S(1)} %get-tuple-element.29.vbuf, ...), custom_call_target="tpu_custom_call" | custom-call | tf_op jit(solution)/shard_map/attend_next/pallas_call | solution.py:427
  16.1 1.3 %collective-permute-start.9 = (bf16[256,256]{1,0:T(8,128)(2,1)S(1)}, bf16[256,256]{1,0:T(8,128)(2,1)S(1)}, u32[]{:S(2)}, u32[]{:S(2)}) collective-permute-start(bf16[256,256]{1,0:T(8,128)(2,1)S(1)} %bitcast.22), channel_id=1, source_target_pairs={{4,0},{6,2},{8,4},{10,6},{12,8},{14,10},{5,1},{7,3},{9,5},{11,7},{... | collective-permute-start | bytes 393224 | tf_op jit(solution)/shard_map/ppermute | solution.py:452
  17.4 0.0 collective-permute-done.4
  17.4 1.8 %collective-permute-start.5 = (s32[2]{0:T(128)S(1)}, s32[2]{0:T(128)S(1)}, u32[]{:S(2)}, u32[]{:S(2)}) collective-permute-start(s32[2]{0:T(128)S(1)} %collective-permute-done.4), channel_id=1, source_target_pairs={{0,1},{1,0},{2,3},{3,2},{4,5},{5,4},{6,7},{7,6},{8,9},{9,8},{10,11... | collective-permute-start | bytes 32 | tf_op jit(solution)/shard_map/ppermute | solution.py:424
  19.2 0.8 %collective-permute-done.5 = s32[2]{0:T(128)S(1)} collective-permute-done((s32[2]{0:T(128)S(1)}, s32[2]{0:T(128)S(1)}, u32[]{:S(2)}, u32[]{:S(2)}) %collective-permute-start.5) | collective-permute-done | bytes 40 | tf_op jit(solution)/shard_map/ppermute | solution.py:424
  20.0 0.1 broadcast_select_fusion
  20.1 0.5 %send_rows.1 = (bf16[512,512]{1,0:T(8,128)(2,1)S(1)}, bf16[256,512]{1,0:T(8,128)(2,1)S(1)}, bf16[256,512]{1,0:T(8,128)(2,1)S(1)}) custom-call(s32[1,128]{1,0:T(1,128)S(1)} %pad_bitcast_fusion.plan_ref, bf16[1024,128]{1,0:T(8,128)(2,1)S(1)} %get-tuple-element.27.kbuf, bf16[768,512]{1,0:T(8,128)(2,1)S(1)} %get-tuple-element.28.d_own, ...), custom_call_target="tpu_custom_call" | custom-call | tf_op jit(solution)/shard_map/send_rows/pallas_call | solution.py:439
  20.6 1.2 %collective-permute-start.7 = (bf16[256,512]{1,0:T(8,128)(2,1)S(1)}, bf16[256,512]{1,0:T(8,128)(2,1)S(1)}, u32[]{:S(2)}, u32[]{:S(2)}) collective-permute-start(bf16[256,512]{1,0:T(8,128)(2,1)S(1)} %get-tuple-element.36), channel_id=1, source_target_pairs={{0,4},{1,3},{2,6},{3,1},{4,0},{5,9},{6,2},{7,11},{8,12},{9,5},{10,... | collective-permute-start | bytes 786440 | tf_op jit(solution)/shard_map/ppermute | solution.py:448
  21.9 3.0 %collective-permute-start.8 = (bf16[256,512]{1,0:T(8,128)(2,1)S(1)}, bf16[256,512]{1,0:T(8,128)(2,1)S(1)}, u32[]{:S(2)}, u32[]{:S(2)}) collective-permute-start(bf16[256,512]{1,0:T(8,128)(2,1)S(1)} %get-tuple-element.37), channel_id=1, source_target_pairs={{0,2},{1,5},{2,0},{3,7},{4,8},{5,1},{6,10},{7,3},{8,4},{9,13},{10,... | collective-permute-start | bytes 786440 | tf_op jit(solution)/shard_map/ppermute | solution.py:449
  24.9 0.0 collective-permute-done.9
  24.9 0.3 collective-permute-start.10
  25.2 0.3 %copy-done.4 = s32[2]{0:T(128)S(1)} copy-done((s32[2]{0:T(128)S(1)}, s32[2]{0:T(128)}, u32[]{:S(2)}) %copy-start.4) | copy-done | bytes 32
  25.5 0.7 %collective-permute-done.7.a_ref = bf16[256,512]{1,0:T(8,128)(2,1)S(1)} collective-permute-done((bf16[256,512]{1,0:T(8,128)(2,1)S(1)}, bf16[256,512]{1,0:T(8,128)(2,1)S(1)}, u32[]{:S(2)}, u32[]{:S(2)}) %collective-permute-start.7) | collective-permute-done | bytes 262176 | tf_op jit(solution)/shard_map/ppermute | solution.py:448
  26.2 3.9 %collective-permute-done.8.b_ref = bf16[256,512]{1,0:T(8,128)(2,1)S(1)} collective-permute-done((bf16[256,512]{1,0:T(8,128)(2,1)S(1)}, bf16[256,512]{1,0:T(8,128)(2,1)S(1)}, u32[]{:S(2)}, u32[]{:S(2)}) %collective-permute-start.8) | collective-permute-done | bytes 262176 | tf_op jit(solution)/shard_map/ppermute | solution.py:449
  30.2 0.0 collective-permute-done.10.t_ref
  30.2 1.1 %place.1 = (bf16[256,256]{1,0:T(8,128)(2,1)}, f32[256,256]{1,0:T(8,128)}, f32[256,128]{1,0:T(8,128)}, f32[256,128]{1,0:T(8,128)}) custom-call(s32[1,128]{1,0:T(1,128)S(1)} %pad_bitcast_fusion.1.plan_ref, bf16[512,512]{1,0:T(8,128)(2,1)S(1)} %get-tuple-element.35.row_ref, bf16[256,512]{1,0:T(8,128)(2,1)S(1)} %collective-permute-done.7.a_ref, ...), custom_call_target="tpu_custom_call" | custom-call | tf_op jit(solution)/shard_map/place/pallas_call | solution.py:455
  (18 shorter events, 0.1 us)
Async XLA Ops:
  0.6 11.2 %copy-start.1 = (bf16[256,256]{1,0:T(8,128)(2,1)S(1)}, bf16[256,256]{1,0:T(8,128)(2,1)}, u32[]{:S(2)}) copy-start(bf16[256,256]{1,0:T(8,128)(2,1)} %g_ref.3) | copy-start | bytes 393220
  0.6 11.2 %copy-start = (bf16[256,256]{1,0:T(8,128)(2,1)S(1)}, bf16[256,256]{1,0:T(8,128)(2,1)}, u32[]{:S(2)}) copy-start(bf16[256,256]{1,0:T(8,128)(2,1)} %q_ref.3) | copy-start | bytes 393220
  0.7 11.2 %copy-start.2 = (bf16[256,128]{1,0:T(8,128)(2,1)S(1)}, bf16[256,128]{1,0:T(8,128)(2,1)}, u32[]{:S(2)}) copy-start(bf16[256,128]{1,0:T(8,128)(2,1)} %k_ref.3) | copy-start | bytes 196612
  0.7 11.2 %copy-start.3 = (bf16[256,128]{1,0:T(8,128)(2,1)S(1)}, bf16[256,128]{1,0:T(8,128)(2,1)}, u32[]{:S(2)}) copy-start(bf16[256,128]{1,0:T(8,128)(2,1)} %v_ref.3) | copy-start | bytes 196612
  1.8 7.4 %collective-permute-start.2 = (bf16[256,128]{1,0:T(8,128)(2,1)S(1)}, bf16[256,128]{1,0:T(8,128)(2,1)S(1)}, u32[]{:S(2)}, u32[]{:S(2)}) collective-permute-start(bf16[256,128]{1,0:T(8,128)(2,1)S(1)} %get-tuple-element.23), channel_id=1, source_target_pairs={{0,2},{2,0},{4,6},{6,4},{8,10},{10,8},{12,14},{14,12},{1,3},{3,1},... | collective-permute-start | bytes 196616 | tf_op jit(solution)/shard_map/ppermute | solution.py:397
  3.9 6.0 %collective-permute-start = (bf16[256,256]{1,0:T(8,128)(2,1)S(1)}, bf16[256,256]{1,0:T(8,128)(2,1)S(1)}, u32[]{:S(2)}, u32[]{:S(2)}) collective-permute-start(bf16[256,256]{1,0:T(8,128)(2,1)S(1)} %get-tuple-element.22), channel_id=1, source_target_pairs={{0,4},{1,7},{2,6},{3,5},{4,8},{5,11},{6,10},{7,9},{8,12},{9,15},{1... | collective-permute-start | bytes 393224 | tf_op jit(solution)/shard_map/ppermute | solution.py:398
  7.1 7.6 %collective-permute-start.6 = (bf16[256,512]{1,0:T(8,128)(2,1)S(1)}, bf16[256,512]{1,0:T(8,128)(2,1)S(1)}, u32[]{:S(2)}, u32[]{:S(2)}) collective-permute-start(bf16[256,512]{1,0:T(8,128)(2,1)S(1)} %get-tuple-element.30), channel_id=1, source_target_pairs={{0,2},{2,0},{4,6},{6,4},{8,10},{10,8},{12,14},{14,12},{1,3},{3,1},... | collective-permute-start | bytes 786440 | tf_op jit(solution)/shard_map/ppermute | solution.py:396
  8.4 0.7 %copy-start.5 = (s32[16]{0:T(128)S(1)}, s32[16]{0:T(128)}, u32[]{:S(2)}) copy-start(s32[16]{0:T(128)} %param.10) | copy-start | bytes 196
  9.3 1.6 %collective-permute-start.3 = (bf16[256,128]{1,0:T(8,128)(2,1)S(1)}, bf16[256,128]{1,0:T(8,128)(2,1)S(1)}, u32[]{:S(2)}, u32[]{:S(2)}) collective-permute-start(bf16[256,128]{1,0:T(8,128)(2,1)S(1)} %collective-permute-done.2.half_ref), channel_id=1, source_target_pairs={{0,1},{1,0},{2,3},{3,2},{4,5},{5,4},{6,7},{7,6},{8,9},{9,8},{10,11... | collective-permute-start | bytes 196616 | tf_op jit(solution)/shard_map/ppermute | solution.py:401
  9.9 1.9 %collective-permute-start.1 = (bf16[1,256,256]{2,1,0:T(8,128)(2,1)S(1)}, bf16[1,256,256]{2,1,0:T(8,128)(2,1)S(1)}, u32[]{:S(2)}, u32[]{:S(2)}) collective-permute-start(bf16[1,256,256]{2,1,0:T(8,128)(2,1)S(1)} %bitcast.18), channel_id=1, source_target_pairs={{0,1},{1,0},{2,3},{3,2},{4,5},{5,4},{6,7},{7,6},{8,9},{9,8},{10,11... | collective-permute-start | bytes 393224 | tf_op jit(solution)/shard_map/ppermute | solution.py:400
  13.5 4.0 %collective-permute-start.4 = (s32[2]{0:T(128)S(1)}, s32[2]{0:T(128)S(1)}, u32[]{:S(2)}, u32[]{:S(2)}) collective-permute-start(s32[2]{0:T(128)S(1)} %get-tuple-element.26), channel_id=1, source_target_pairs={{0,4},{1,3},{2,6},{3,1},{4,0},{5,9},{6,2},{7,11},{8,12},{9,5},{10,... | collective-permute-start | bytes 32 | tf_op jit(solution)/shard_map/ppermute | solution.py:423
  16.1 8.7 %collective-permute-start.9 = (bf16[256,256]{1,0:T(8,128)(2,1)S(1)}, bf16[256,256]{1,0:T(8,128)(2,1)S(1)}, u32[]{:S(2)}, u32[]{:S(2)}) collective-permute-start(bf16[256,256]{1,0:T(8,128)(2,1)S(1)} %bitcast.22), channel_id=1, source_target_pairs={{4,0},{6,2},{8,4},{10,6},{12,8},{14,10},{5,1},{7,3},{9,5},{11,7},{... | collective-permute-start | bytes 393224 | tf_op jit(solution)/shard_map/ppermute | solution.py:452
  17.4 2.6 %collective-permute-start.5 = (s32[2]{0:T(128)S(1)}, s32[2]{0:T(128)S(1)}, u32[]{:S(2)}, u32[]{:S(2)}) collective-permute-start(s32[2]{0:T(128)S(1)} %collective-permute-done.4), channel_id=1, source_target_pairs={{0,1},{1,0},{2,3},{3,2},{4,5},{5,4},{6,7},{7,6},{8,9},{9,8},{10,11... | collective-permute-start | bytes 32 | tf_op jit(solution)/shard_map/ppermute | solution.py:424
  20.6 5.6 %collective-permute-start.7 = (bf16[256,512]{1,0:T(8,128)(2,1)S(1)}, bf16[256,512]{1,0:T(8,128)(2,1)S(1)}, u32[]{:S(2)}, u32[]{:S(2)}) collective-permute-start(bf16[256,512]{1,0:T(8,128)(2,1)S(1)} %get-tuple-element.36), channel_id=1, source_target_pairs={{0,4},{1,3},{2,6},{3,1},{4,0},{5,9},{6,2},{7,11},{8,12},{9,5},{10,... | collective-permute-start | bytes 786440 | tf_op jit(solution)/shard_map/ppermute | solution.py:448
  21.9 8.3 %collective-permute-start.8 = (bf16[256,512]{1,0:T(8,128)(2,1)S(1)}, bf16[256,512]{1,0:T(8,128)(2,1)S(1)}, u32[]{:S(2)}, u32[]{:S(2)}) collective-permute-start(bf16[256,512]{1,0:T(8,128)(2,1)S(1)} %get-tuple-element.37), channel_id=1, source_target_pairs={{0,2},{1,5},{2,0},{3,7},{4,8},{5,1},{6,10},{7,3},{8,4},{9,13},{10,... | collective-permute-start | bytes 786440 | tf_op jit(solution)/shard_map/ppermute | solution.py:449
  24.9 0.7 %copy-start.4 = (s32[2]{0:T(128)S(1)}, s32[2]{0:T(128)}, u32[]{:S(2)}) copy-start(s32[2]{0:T(128)} %plan_ref.1) | copy-start | bytes 28
  24.9 5.3 %collective-permute-start.10 = (f32[256,256]{1,0:T(8,128)S(1)}, f32[256,256]{1,0:T(8,128)S(1)}, u32[]{:S(2)}, u32[]{:S(2)}) collective-permute-start(f32[256,256]{1,0:T(8,128)S(1)} %convert_add_fusion.s_ref), channel_id=1, source_target_pairs={{0,1},{1,0},{2,3},{3,2},{4,5},{5,4},{6,7},{7,6},{8,9},{9,8},{10,11... | collective-permute-start | bytes 786440 | tf_op jit(solution)/shard_map/ppermute | solution.py:453

commit v4 on v3

--- a/solution.py
+++ b/solution.py
@@ -371,8 +371,8 @@
         for s in range(n):
             for h in range(2):
                 to = s // 2 + r + 1
-                if to < n // 2:
-                    pairs.append((2 * s + h, 2 * (2 * to + (s + h) % 2) + h))
+                column = (s + h) % 2 if to < n // 2 else s % 2
+                pairs.append((2 * s + h, 2 * (2 * (to % (n // 2)) + column) + h))
         return pairs
 
     def back_pairs(r):

time: 31.6 us -> 30.1 us (0.953)
  starting transfers between devices: 16.9 us -> 14 us
  waiting for transfers between devices: 6.47 us -> 8.29 us
    ppermute x1, starting transfers between devices: 3.17 us -> 1.27 us  [per_device(): mine = [lax.ppermute(own_kv, both, fetch_pairs(r)) for r in range(rounds)]]
    ppermute x1, waiting for transfers between devices: 0.01 us -> 1.66 us  [per_device(): mine = [lax.ppermute(own_kv, both, fetch_pairs(r)) for r in range(rounds)]]
    ppermute x1, starting transfers between devices: 0.94 us -> 2.09 us  [per_device(): other = lax.ppermute(mine, 'head', cross)]
    ppermute x1, starting transfers between devices: 1.76 us -> 0.87 us  [per_device(): plan_other = lax.ppermute(plan_mine, 'head', cross)]
    ppermute x1, starting transfers between devices: 1.19 us -> 0.32 us  [per_device(): plan_mine = lax.ppermute(stretch_here, both, tie_a)]
    ppermute x1, waiting for transfers between devices: 0.71 us -> 1.3 us  [per_device(): moved_a = lax.ppermute(send_a, both, tie_a)]
    ppermute x1, starting transfers between devices: 1.23 us -> 0.77 us  [per_device(): moved_a = lax.ppermute(send_a, both, tie_a)]
    ppermute x1, starting transfers between devices: 0.31 us -> 0.75 us  [per_device(): total_other = lax.ppermute(total, 'head', cross)]
  transfers between devices with their start and end apart: 11 -> 11, of which waited for: 4 -> 5; matrix products, arithmetic and copies ran while one was open for 1% -> 1% of each run, Pallas kernels for 12% -> 12%
where the time goes in v4:
time: 30.1 us; the launch traced here: 29.9 us
  starting transfers between devices  14 us (47%)
  waiting for transfers between devices  8.29 us (28%)
  Pallas kernels  5.8 us (19%)
  between operations  0.74 us (2%)
  local copies, waits for them, and re-layouts  0.7 us (2%)
  other arithmetic  0.31 us (1%)
    ppermute x1, waiting for transfers between devices, per_device(): moved_b = lax.ppermute(send_b, both, tie_b)  3.52 us
    ppermute x1, starting transfers between devices, per_device(): moved_b = lax.ppermute(send_b, both, tie_b)  2.72 us
    ppermute x1, starting transfers between devices, per_device(): half_next = lax.ppermute(half, 'ctx', near)  2.11 us
    ppermute x1, starting transfers between devices, per_device(): other = lax.ppermute(mine, 'head', cross)  2.09 us
    ppermute x1, waiting for transfers between devices, per_device(): mine = [lax.ppermute(own_kv, both, fetch_pairs(r)) for r in range(rounds)]  1.66 us
    pallas_call x1, Pallas kernels, per_device(): pl.pallas_call(own_kernel(sizes), out_shape=(attended, grads, key_sums, b...  1.59 us
    pallas_call x1, Pallas kernels, per_device(): pl.pallas_call(next_kernel(sizes), out_shape=(attended, grads, jax.ShapeD...  1.47 us
    ppermute x1, waiting for transfers between devices, per_device(): moved_a = lax.ppermute(send_a, both, tie_a)  1.3 us
  transfers between devices with their start and end apart: 11, of which 5 were waited for; matrix products, arithmetic and copies ran while one was open for 1% of the time, Pallas kernels for 12%

profile of v4, /device:TPU:1, one launch (start us, length us, event | category | flops | bytes accessed | tf_op | source)
XLA Modules:
  0.0 29.9 jit_solution(10146273736124570615)
XLA Ops:
  0.7 1.1 %pack.1 = (s32[2]{0:T(128)S(1)}, bf16[256,256]{1,0:T(8,128)(2,1)S(1)}, bf16[256,128]{1,0:T(8,128)(2,1)S(1)}, bf16[256,512]{1,0:T(8,128)(2,1)S(1)}) custom-call(s32[2]{0:T(128)} %plan_ref.1, bf16[256,128]{1,0:T(8,128)(2,1)} %k_ref.3, bf16[256,128]{1,0:T(8,128)(2,1)} %v_ref.3, bf16[256,256]{1,0:T(8,128)(2,1)} %q_ref.3, bf16[256,256]{1,0:T(8,128)(2,1)} %g_ref.3), custom_call_target="tpu_custom_call" | custom-call | tf_op jit(solution)/shard_map/pack/pallas_call | solution.py:381
  1.8 2.1 %collective-permute-start.2 = (bf16[256,128]{1,0:T(8,128)(2,1)S(1)}, bf16[256,128]{1,0:T(8,128)(2,1)S(1)}, u32[]{:S(2)}, u32[]{:S(2)}) collective-permute-start(bf16[256,128]{1,0:T(8,128)(2,1)S(1)} %get-tuple-element.23), channel_id=1, source_target_pairs={{0,2},{2,0},{4,6},{6,4},{8,10},{10,8},{12,14},{14,12},{1,3},{3,1},... | collective-permute-start | bytes 196616 | tf_op jit(solution)/shard_map/ppermute | solution.py:397
  3.9 1.3 %collective-permute-start = (bf16[256,256]{1,0:T(8,128)(2,1)S(1)}, bf16[256,256]{1,0:T(8,128)(2,1)S(1)}, u32[]{:S(2)}, u32[]{:S(2)}) collective-permute-start(bf16[256,256]{1,0:T(8,128)(2,1)S(1)} %get-tuple-element.22), channel_id=1, source_target_pairs={{0,4},{1,7},{2,6},{3,5},{4,8},{5,11},{6,10},{7,9},{8,12},{9,15},{1... | collective-permute-start | bytes 393224 | tf_op jit(solution)/shard_map/ppermute | solution.py:398
  5.2 1.2 %collective-permute-start.6 = (bf16[256,512]{1,0:T(8,128)(2,1)S(1)}, bf16[256,512]{1,0:T(8,128)(2,1)S(1)}, u32[]{:S(2)}, u32[]{:S(2)}) collective-permute-start(bf16[256,512]{1,0:T(8,128)(2,1)S(1)} %get-tuple-element.30), channel_id=1, source_target_pairs={{0,2},{2,0},{4,6},{6,4},{8,10},{10,8},{12,14},{14,12},{1,3},{3,1},... | collective-permute-start | bytes 786440 | tf_op jit(solution)/shard_map/ppermute | solution.py:396
  6.4 0.7 %copy-done.5 = s32[16]{0:T(128)S(1)} copy-done((s32[16]{0:T(128)S(1)}, s32[16]{0:T(128)}, u32[]{:S(2)}) %copy-start.5) | copy-done | bytes 88
  7.1 0.1 select_reduce_fusion.2
  7.2 0.1 select_reduce_fusion
  7.3 0.0 collective-permute-done.2.half_ref
  7.3 0.7 %collective-permute-start.3 = (bf16[256,128]{1,0:T(8,128)(2,1)S(1)}, bf16[256,128]{1,0:T(8,128)(2,1)S(1)}, u32[]{:S(2)}, u32[]{:S(2)}) collective-permute-start(bf16[256,128]{1,0:T(8,128)(2,1)S(1)} %collective-permute-done.2.half_ref), channel_id=1, source_target_pairs={{0,1},{1,0},{2,3},{3,2},{4,5},{5,4},{6,7},{7,6},{8,9},{9,8},{10,11... | collective-permute-start | bytes 196616 | tf_op jit(solution)/shard_map/ppermute | solution.py:401
  7.9 1.7 %collective-permute-done = bf16[256,256]{1,0:T(8,128)(2,1)S(1)} collective-permute-done((bf16[256,256]{1,0:T(8,128)(2,1)S(1)}, bf16[256,256]{1,0:T(8,128)(2,1)S(1)}, u32[]{:S(2)}, u32[]{:S(2)}) %collective-permute-start) | collective-permute-done | bytes 131104 | tf_op jit(solution)/shard_map/ppermute | solution.py:398
  9.6 2.1 %collective-permute-start.1 = (bf16[1,256,256]{2,1,0:T(8,128)(2,1)S(1)}, bf16[1,256,256]{2,1,0:T(8,128)(2,1)S(1)}, u32[]{:S(2)}, u32[]{:S(2)}) collective-permute-start(bf16[1,256,256]{2,1,0:T(8,128)(2,1)S(1)} %bitcast.18), channel_id=1, source_target_pairs={{0,1},{1,0},{2,3},{3,2},{4,5},{5,4},{6,7},{7,6},{8,9},{9,8},{10,11... | collective-permute-start | bytes 393224 | tf_op jit(solution)/shard_map/ppermute | solution.py:400
  11.7 0.0 collective-permute-done.3.cross_ref
  11.7 1.0 %collective-permute-done.1.other_ref = bf16[1,256,256]{2,1,0:T(8,128)(2,1)S(1)} collective-permute-done((bf16[1,256,256]{2,1,0:T(8,128)(2,1)S(1)}, bf16[1,256,256]{2,1,0:T(8,128)(2,1)S(1)}, u32[]{:S(2)}, u32[]{:S(2)}) %collective-permute-start.1) | collective-permute-done | bytes 131104 | tf_op jit(solution)/shard_map/ppermute | solution.py:400
  12.7 1.6 %attend_own.1 = (bf16[256,256]{1,0:T(8,128)(2,1)S(1)}, bf16[768,512]{1,0:T(8,128)(2,1)S(1)}, f32[2,256,256]{2,1,0:T(8,128)S(1)}, bf16[1024,128]{1,0:T(8,128)(2,1)S(1)}, bf16[1024,128]{1,0:T(8,128)(2,1)S(1)}) custom-call(s32[2,256]{1,0:T(2,128)S(1)} %bitcast.21, bf16[256,128]{1,0:T(8,128)(2,1)S(1)} %copy-done.2, bf16[256,128]{1,0:T(8,128)(2,1)S(1)} %copy-done.3, ...), custom_call_target="tpu_custom_call" | custom-call | tf_op jit(solution)/shard_map/attend_own/pallas_call | solution.py:412
  14.3 0.3 %collective-permute-start.4 = (s32[2]{0:T(128)S(1)}, s32[2]{0:T(128)S(1)}, u32[]{:S(2)}, u32[]{:S(2)}) collective-permute-start(s32[2]{0:T(128)S(1)} %get-tuple-element.26), channel_id=1, source_target_pairs={{0,4},{1,3},{2,6},{3,1},{4,0},{5,9},{6,2},{7,11},{8,12},{9,5},{10,... | collective-permute-start | bytes 32 | tf_op jit(solution)/shard_map/ppermute | solution.py:423
  14.6 0.0 collective-permute-done.6.qg_ref
  14.6 1.5 %attend_next.1 = (bf16[256,256]{1,0:T(8,128)(2,1)S(1)}, bf16[768,512]{1,0:T(8,128)(2,1)S(1)}, f32[256,256]{1,0:T(8,128)S(1)}, bf16[1,256,256]{2,1,0:T(8,128)(2,1)S(1)}) custom-call(s32[2,256]{1,0:T(2,128)S(1)} %bitcast.20, bf16[1024,128]{1,0:T(8,128)(2,1)S(1)} %get-tuple-element.27.kbuf, bf16[1024,128]{1,0:T(8,128)(2,1)S(1)} %get-tuple-element.29.vbuf, ...), custom_call_target="tpu_custom_call" | custom-call | tf_op jit(solution)/shard_map/attend_next/pallas_call | solution.py:427
  16.1 1.3 %collective-permute-start.9 = (bf16[256,256]{1,0:T(8,128)(2,1)S(1)}, bf16[256,256]{1,0:T(8,128)(2,1)S(1)}, u32[]{:S(2)}, u32[]{:S(2)}) collective-permute-start(bf16[256,256]{1,0:T(8,128)(2,1)S(1)} %bitcast.22), channel_id=1, source_target_pairs={{4,0},{6,2},{8,4},{10,6},{12,8},{14,10},{5,1},{7,3},{9,5},{11,7},{... | collective-permute-start | bytes 393224 | tf_op jit(solution)/shard_map/ppermute | solution.py:452
  17.4 0.0 collective-permute-done.4
  17.4 0.9 %collective-permute-start.5 = (s32[2]{0:T(128)S(1)}, s32[2]{0:T(128)S(1)}, u32[]{:S(2)}, u32[]{:S(2)}) collective-permute-start(s32[2]{0:T(128)S(1)} %collective-permute-done.4), channel_id=1, source_target_pairs={{0,1},{1,0},{2,3},{3,2},{4,5},{5,4},{6,7},{7,6},{8,9},{9,8},{10,11... | collective-permute-start | bytes 32 | tf_op jit(solution)/shard_map/ppermute | solution.py:424
  18.3 0.8 %collective-permute-done.5 = s32[2]{0:T(128)S(1)} collective-permute-done((s32[2]{0:T(128)S(1)}, s32[2]{0:T(128)S(1)}, u32[]{:S(2)}, u32[]{:S(2)}) %collective-permute-start.5) | collective-permute-done | bytes 40 | tf_op jit(solution)/shard_map/ppermute | solution.py:424
  19.1 0.1 broadcast_select_fusion
  19.2 0.5 %send_rows.1 = (bf16[512,512]{1,0:T(8,128)(2,1)S(1)}, bf16[256,512]{1,0:T(8,128)(2,1)S(1)}, bf16[256,512]{1,0:T(8,128)(2,1)S(1)}) custom-call(s32[1,128]{1,0:T(1,128)S(1)} %pad_bitcast_fusion.plan_ref, bf16[1024,128]{1,0:T(8,128)(2,1)S(1)} %get-tuple-element.27.kbuf, bf16[768,512]{1,0:T(8,128)(2,1)S(1)} %get-tuple-element.28.d_own, ...), custom_call_target="tpu_custom_call" | custom-call | tf_op jit(solution)/shard_map/send_rows/pallas_call | solution.py:439
  19.7 0.8 %collective-permute-start.7 = (bf16[256,512]{1,0:T(8,128)(2,1)S(1)}, bf16[256,512]{1,0:T(8,128)(2,1)S(1)}, u32[]{:S(2)}, u32[]{:S(2)}) collective-permute-start(bf16[256,512]{1,0:T(8,128)(2,1)S(1)} %get-tuple-element.36), channel_id=1, source_target_pairs={{0,4},{1,3},{2,6},{3,1},{4,0},{5,9},{6,2},{7,11},{8,12},{9,5},{10,... | collective-permute-start | bytes 786440 | tf_op jit(solution)/shard_map/ppermute | solution.py:448
  20.5 2.7 %collective-permute-start.8 = (bf16[256,512]{1,0:T(8,128)(2,1)S(1)}, bf16[256,512]{1,0:T(8,128)(2,1)S(1)}, u32[]{:S(2)}, u32[]{:S(2)}) collective-permute-start(bf16[256,512]{1,0:T(8,128)(2,1)S(1)} %get-tuple-element.37), channel_id=1, source_target_pairs={{0,2},{1,5},{2,0},{3,7},{4,8},{5,1},{6,10},{7,3},{8,4},{9,13},{10,... | collective-permute-start | bytes 786440 | tf_op jit(solution)/shard_map/ppermute | solution.py:449
  23.2 0.0 collective-permute-done.9
  23.2 0.8 %collective-permute-start.10 = (f32[256,256]{1,0:T(8,128)S(1)}, f32[256,256]{1,0:T(8,128)S(1)}, u32[]{:S(2)}, u32[]{:S(2)}) collective-permute-start(f32[256,256]{1,0:T(8,128)S(1)} %convert_add_fusion.s_ref), channel_id=1, source_target_pairs={{0,1},{1,0},{2,3},{3,2},{4,5},{5,4},{6,7},{7,6},{8,9},{9,8},{10,11... | collective-permute-start | bytes 786440 | tf_op jit(solution)/shard_map/ppermute | solution.py:453
  24.0 0.0 copy-done.4
  24.0 1.3 %collective-permute-done.7.a_ref = bf16[256,512]{1,0:T(8,128)(2,1)S(1)} collective-permute-done((bf16[256,512]{1,0:T(8,128)(2,1)S(1)}, bf16[256,512]{1,0:T(8,128)(2,1)S(1)}, u32[]{:S(2)}, u32[]{:S(2)}) %collective-permute-start.7) | collective-permute-done | bytes 262176 | tf_op jit(solution)/shard_map/ppermute | solution.py:448
  25.3 3.5 %collective-permute-done.8.b_ref = bf16[256,512]{1,0:T(8,128)(2,1)S(1)} collective-permute-done((bf16[256,512]{1,0:T(8,128)(2,1)S(1)}, bf16[256,512]{1,0:T(8,128)(2,1)S(1)}, u32[]{:S(2)}, u32[]{:S(2)}) %collective-permute-start.8) | collective-permute-done | bytes 262176 | tf_op jit(solution)/shard_map/ppermute | solution.py:449
  28.8 0.0 collective-permute-done.10.t_ref
  28.8 1.1 %place.1 = (bf16[256,256]{1,0:T(8,128)(2,1)}, f32[256,256]{1,0:T(8,128)}, f32[256,128]{1,0:T(8,128)}, f32[256,128]{1,0:T(8,128)}) custom-call(s32[1,128]{1,0:T(1,128)S(1)} %pad_bitcast_fusion.1.plan_ref, bf16[512,512]{1,0:T(8,128)(2,1)S(1)} %get-tuple-element.35.row_ref, bf16[256,512]{1,0:T(8,128)(2,1)S(1)} %collective-permute-done.7.a_ref, ...), custom_call_target="tpu_custom_call" | custom-call | tf_op jit(solution)/shard_map/place/pallas_call | solution.py:455
  (18 shorter events, 0.1 us)
Async XLA Ops:
  0.6 12.1 %copy-start.1 = (bf16[256,256]{1,0:T(8,128)(2,1)S(1)}, bf16[256,256]{1,0:T(8,128)(2,1)}, u32[]{:S(2)}) copy-start(bf16[256,256]{1,0:T(8,128)(2,1)} %g_ref.3) | copy-start | bytes 393220
  0.6 12.0 %copy-start = (bf16[256,256]{1,0:T(8,128)(2,1)S(1)}, bf16[256,256]{1,0:T(8,128)(2,1)}, u32[]{:S(2)}) copy-start(bf16[256,256]{1,0:T(8,128)(2,1)} %q_ref.3) | copy-start | bytes 393220
  0.7 12.0 %copy-start.2 = (bf16[256,128]{1,0:T(8,128)(2,1)S(1)}, bf16[256,128]{1,0:T(8,128)(2,1)}, u32[]{:S(2)}) copy-start(bf16[256,128]{1,0:T(8,128)(2,1)} %k_ref.3) | copy-start | bytes 196612
  0.7 12.0 %copy-start.3 = (bf16[256,128]{1,0:T(8,128)(2,1)S(1)}, bf16[256,128]{1,0:T(8,128)(2,1)}, u32[]{:S(2)}) copy-start(bf16[256,128]{1,0:T(8,128)(2,1)} %v_ref.3) | copy-start | bytes 196612
  1.8 5.5 %collective-permute-start.2 = (bf16[256,128]{1,0:T(8,128)(2,1)S(1)}, bf16[256,128]{1,0:T(8,128)(2,1)S(1)}, u32[]{:S(2)}, u32[]{:S(2)}) collective-permute-start(bf16[256,128]{1,0:T(8,128)(2,1)S(1)} %get-tuple-element.23), channel_id=1, source_target_pairs={{0,2},{2,0},{4,6},{6,4},{8,10},{10,8},{12,14},{14,12},{1,3},{3,1},... | collective-permute-start | bytes 196616 | tf_op jit(solution)/shard_map/ppermute | solution.py:397
  3.9 5.7 %collective-permute-start = (bf16[256,256]{1,0:T(8,128)(2,1)S(1)}, bf16[256,256]{1,0:T(8,128)(2,1)S(1)}, u32[]{:S(2)}, u32[]{:S(2)}) collective-permute-start(bf16[256,256]{1,0:T(8,128)(2,1)S(1)} %get-tuple-element.22), channel_id=1, source_target_pairs={{0,4},{1,7},{2,6},{3,5},{4,8},{5,11},{6,10},{7,9},{8,12},{9,15},{1... | collective-permute-start | bytes 393224 | tf_op jit(solution)/shard_map/ppermute | solution.py:398
  5.2 9.4 %collective-permute-start.6 = (bf16[256,512]{1,0:T(8,128)(2,1)S(1)}, bf16[256,512]{1,0:T(8,128)(2,1)S(1)}, u32[]{:S(2)}, u32[]{:S(2)}) collective-permute-start(bf16[256,512]{1,0:T(8,128)(2,1)S(1)} %get-tuple-element.30), channel_id=1, source_target_pairs={{0,2},{2,0},{4,6},{6,4},{8,10},{10,8},{12,14},{14,12},{1,3},{3,1},... | collective-permute-start | bytes 786440 | tf_op jit(solution)/shard_map/ppermute | solution.py:396
  6.4 0.7 %copy-start.5 = (s32[16]{0:T(128)S(1)}, s32[16]{0:T(128)}, u32[]{:S(2)}) copy-start(s32[16]{0:T(128)} %param.10) | copy-start | bytes 196
  7.3 4.4 %collective-permute-start.3 = (bf16[256,128]{1,0:T(8,128)(2,1)S(1)}, bf16[256,128]{1,0:T(8,128)(2,1)S(1)}, u32[]{:S(2)}, u32[]{:S(2)}) collective-permute-start(bf16[256,128]{1,0:T(8,128)(2,1)S(1)} %collective-permute-done.2.half_ref), channel_id=1, source_target_pairs={{0,1},{1,0},{2,3},{3,2},{4,5},{5,4},{6,7},{7,6},{8,9},{9,8},{10,11... | collective-permute-start | bytes 196616 | tf_op jit(solution)/shard_map/ppermute | solution.py:401
  9.6 3.1 %collective-permute-start.1 = (bf16[1,256,256]{2,1,0:T(8,128)(2,1)S(1)}, bf16[1,256,256]{2,1,0:T(8,128)(2,1)S(1)}, u32[]{:S(2)}, u32[]{:S(2)}) collective-permute-start(bf16[1,256,256]{2,1,0:T(8,128)(2,1)S(1)} %bitcast.18), channel_id=1, source_target_pairs={{0,1},{1,0},{2,3},{3,2},{4,5},{5,4},{6,7},{7,6},{8,9},{9,8},{10,11... | collective-permute-start | bytes 393224 | tf_op jit(solution)/shard_map/ppermute | solution.py:400
  14.3 3.1 %collective-permute-start.4 = (s32[2]{0:T(128)S(1)}, s32[2]{0:T(128)S(1)}, u32[]{:S(2)}, u32[]{:S(2)}) collective-permute-start(s32[2]{0:T(128)S(1)} %get-tuple-element.26), channel_id=1, source_target_pairs={{0,4},{1,3},{2,6},{3,1},{4,0},{5,9},{6,2},{7,11},{8,12},{9,5},{10,... | collective-permute-start | bytes 32 | tf_op jit(solution)/shard_map/ppermute | solution.py:423
  16.1 7.1 %collective-permute-start.9 = (bf16[256,256]{1,0:T(8,128)(2,1)S(1)}, bf16[256,256]{1,0:T(8,128)(2,1)S(1)}, u32[]{:S(2)}, u32[]{:S(2)}) collective-permute-start(bf16[256,256]{1,0:T(8,128)(2,1)S(1)} %bitcast.22), channel_id=1, source_target_pairs={{4,0},{6,2},{8,4},{10,6},{12,8},{14,10},{5,1},{7,3},{9,5},{11,7},{... | collective-permute-start | bytes 393224 | tf_op jit(solution)/shard_map/ppermute | solution.py:452
  17.4 1.7 %collective-permute-start.5 = (s32[2]{0:T(128)S(1)}, s32[2]{0:T(128)S(1)}, u32[]{:S(2)}, u32[]{:S(2)}) collective-permute-start(s32[2]{0:T(128)S(1)} %collective-permute-done.4), channel_id=1, source_target_pairs={{0,1},{1,0},{2,3},{3,2},{4,5},{5,4},{6,7},{7,6},{8,9},{9,8},{10,11... | collective-permute-start | bytes 32 | tf_op jit(solution)/shard_map/ppermute | solution.py:424
  19.7 5.6 %collective-permute-start.7 = (bf16[256,512]{1,0:T(8,128)(2,1)S(1)}, bf16[256,512]{1,0:T(8,128)(2,1)S(1)}, u32[]{:S(2)}, u32[]{:S(2)}) collective-permute-start(bf16[256,512]{1,0:T(8,128)(2,1)S(1)} %get-tuple-element.36), channel_id=1, source_target_pairs={{0,4},{1,3},{2,6},{3,1},{4,0},{5,9},{6,2},{7,11},{8,12},{9,5},{10,... | collective-permute-start | bytes 786440 | tf_op jit(solution)/shard_map/ppermute | solution.py:448
  20.5 8.3 %collective-permute-start.8 = (bf16[256,512]{1,0:T(8,128)(2,1)S(1)}, bf16[256,512]{1,0:T(8,128)(2,1)S(1)}, u32[]{:S(2)}, u32[]{:S(2)}) collective-permute-start(bf16[256,512]{1,0:T(8,128)(2,1)S(1)} %get-tuple-element.37), channel_id=1, source_target_pairs={{0,2},{1,5},{2,0},{3,7},{4,8},{5,1},{6,10},{7,3},{8,4},{9,13},{10,... | collective-permute-start | bytes 786440 | tf_op jit(solution)/shard_map/ppermute | solution.py:449
  23.2 0.8 %copy-start.4 = (s32[2]{0:T(128)S(1)}, s32[2]{0:T(128)}, u32[]{:S(2)}) copy-start(s32[2]{0:T(128)} %plan_ref.1) | copy-start | bytes 28
  23.2 5.6 %collective-permute-start.10 = (f32[256,256]{1,0:T(8,128)S(1)}, f32[256,256]{1,0:T(8,128)S(1)}, u32[]{:S(2)}, u32[]{:S(2)}) collective-permute-start(f32[256,256]{1,0:T(8,128)S(1)} %convert_add_fusion.s_ref), channel_id=1, source_target_pairs={{0,1},{1,0},{2,3},{3,2},{4,5},{5,4},{6,7},{7,6},{8,9},{9,8},{10,11... | collective-permute-start | bytes 786440 | tf_op jit(solution)/shard_map/ppermute | solution.py:453

commit v5 on v4

--- a/solution.py
+++ b/solution.py
@@ -173,12 +173,13 @@
     scale = [1.0 / jnp.sum(t, axis=0, keepdims=True) for t in totals]
     dots = []
     for i in range(2):
-        attended = (contract(sizes, low, vbuf, p_ref, i) * scale[i]).T.astype(jnp.bfloat16)
+        total = contract(sizes, low, vbuf, p_ref, i) * scale[i]
+        attended = total.T.astype(jnp.bfloat16)
         for h in range(heads):
             od_ref[i * CHUNK:(i + 1) * CHUNK, h * head_dim:(h + 1) * head_dim] = (
                 attended[h * CHUNK:(h + 1) * CHUNK])
-        product = g[i].astype(jnp.float32) * attended.astype(jnp.float32)
-        dots.append(jnp.sum(product.T, axis=0, keepdims=True))
+        rounded = total.astype(jnp.bfloat16).astype(jnp.float32)
+        dots.append(jnp.sum(g[i].astype(jnp.float32).T * rounded, axis=0, keepdims=True))
 
     def backward(j, carry):
         v = vbuf[rows_at(low + j), :]

time: 30.1 us -> 29.6 us (0.983)
  Pallas kernels: 5.8 us -> 5.32 us
    ppermute x1, waiting for transfers between devices: 1.3 us -> 1.79 us  [per_device(): moved_a = lax.ppermute(send_a, both, tie_a)]
    ppermute x1, waiting for transfers between devices: 3.52 us -> 3.04 us  [per_device(): moved_b = lax.ppermute(send_b, both, tie_b)]
  transfers between devices with their start and end apart: 11 -> 11, of which waited for: 5 -> 5; matrix products, arithmetic and copies ran while one was open for 1% -> 1% of each run, Pallas kernels for 12% -> 11%
where the time goes in v5:
time: 29.6 us; the launch traced here: 29.4 us
  starting transfers between devices  14 us (47%)
  waiting for transfers between devices  8.3 us (28%)
  Pallas kernels  5.32 us (18%)
  between operations  0.74 us (2%)
  local copies, waits for them, and re-layouts  0.7 us (2%)
  other arithmetic  0.31 us (1%)
    ppermute x1, waiting for transfers between devices, per_device(): moved_b = lax.ppermute(send_b, both, tie_b)  3.04 us
    ppermute x1, starting transfers between devices, per_device(): moved_b = lax.ppermute(send_b, both, tie_b)  2.71 us
    ppermute x1, starting transfers between devices, per_device(): half_next = lax.ppermute(half, 'ctx', near)  2.11 us
    ppermute x1, starting transfers between devices, per_device(): other = lax.ppermute(mine, 'head', cross)  2.09 us
    ppermute x1, waiting for transfers between devices, per_device(): moved_a = lax.ppermute(send_a, both, tie_a)  1.79 us
    ppermute x1, waiting for transfers between devices, per_device(): mine = [lax.ppermute(own_kv, both, fetch_pairs(r)) for r in range(rounds)]  1.66 us
    pallas_call x1, Pallas kernels, per_device(): pl.pallas_call(own_kernel(sizes), out_shape=(attended, grads, key_sums, b...  1.36 us
    ppermute x1, starting transfers between devices, per_device(): total = total + lax.ppermute(far[r], 'ctx', back_pairs(r + 1)).astype(f32)  1.29 us
  transfers between devices with their start and end apart: 11, of which 5 were waited for; matrix products, arithmetic and copies ran while one was open for 1% of the time, Pallas kernels for 11%

profile of v5, /device:TPU:1, one launch (start us, length us, event | category | flops | bytes accessed | tf_op | source)
XLA Modules:
  0.0 29.4 jit_solution(656327893761493170)
XLA Ops:
  0.7 1.1 %pack.1 = (s32[2]{0:T(128)S(1)}, bf16[256,256]{1,0:T(8,128)(2,1)S(1)}, bf16[256,128]{1,0:T(8,128)(2,1)S(1)}, bf16[256,512]{1,0:T(8,128)(2,1)S(1)}) custom-call(s32[2]{0:T(128)} %plan_ref.1, bf16[256,128]{1,0:T(8,128)(2,1)} %k_ref.3, bf16[256,128]{1,0:T(8,128)(2,1)} %v_ref.3, bf16[256,256]{1,0:T(8,128)(2,1)} %q_ref.3, bf16[256,256]{1,0:T(8,128)(2,1)} %g_ref.3), custom_call_target="tpu_custom_call" | custom-call | tf_op jit(solution)/shard_map/pack/pallas_call | solution.py:382
  1.8 2.1 %collective-permute-start.2 = (bf16[256,128]{1,0:T(8,128)(2,1)S(1)}, bf16[256,128]{1,0:T(8,128)(2,1)S(1)}, u32[]{:S(2)}, u32[]{:S(2)}) collective-permute-start(bf16[256,128]{1,0:T(8,128)(2,1)S(1)} %get-tuple-element.23), channel_id=1, source_target_pairs={{0,2},{2,0},{4,6},{6,4},{8,10},{10,8},{12,14},{14,12},{1,3},{3,1},... | collective-permute-start | bytes 196616 | tf_op jit(solution)/shard_map/ppermute | solution.py:398
  3.9 1.3 %collective-permute-start = (bf16[256,256]{1,0:T(8,128)(2,1)S(1)}, bf16[256,256]{1,0:T(8,128)(2,1)S(1)}, u32[]{:S(2)}, u32[]{:S(2)}) collective-permute-start(bf16[256,256]{1,0:T(8,128)(2,1)S(1)} %get-tuple-element.22), channel_id=1, source_target_pairs={{0,4},{1,7},{2,6},{3,5},{4,8},{5,11},{6,10},{7,9},{8,12},{9,15},{1... | collective-permute-start | bytes 393224 | tf_op jit(solution)/shard_map/ppermute | solution.py:399
  5.2 1.2 %collective-permute-start.6 = (bf16[256,512]{1,0:T(8,128)(2,1)S(1)}, bf16[256,512]{1,0:T(8,128)(2,1)S(1)}, u32[]{:S(2)}, u32[]{:S(2)}) collective-permute-start(bf16[256,512]{1,0:T(8,128)(2,1)S(1)} %get-tuple-element.30), channel_id=1, source_target_pairs={{0,2},{2,0},{4,6},{6,4},{8,10},{10,8},{12,14},{14,12},{1,3},{3,1},... | collective-permute-start | bytes 786440 | tf_op jit(solution)/shard_map/ppermute | solution.py:397
  6.4 0.7 %copy-done.5 = s32[16]{0:T(128)S(1)} copy-done((s32[16]{0:T(128)S(1)}, s32[16]{0:T(128)}, u32[]{:S(2)}) %copy-start.5) | copy-done | bytes 88
  7.1 0.1 select_reduce_fusion.2
  7.2 0.1 select_reduce_fusion
  7.3 0.0 collective-permute-done.2.half_ref
  7.3 0.7 %collective-permute-start.3 = (bf16[256,128]{1,0:T(8,128)(2,1)S(1)}, bf16[256,128]{1,0:T(8,128)(2,1)S(1)}, u32[]{:S(2)}, u32[]{:S(2)}) collective-permute-start(bf16[256,128]{1,0:T(8,128)(2,1)S(1)} %collective-permute-done.2.half_ref), channel_id=1, source_target_pairs={{0,1},{1,0},{2,3},{3,2},{4,5},{5,4},{6,7},{7,6},{8,9},{9,8},{10,11... | collective-permute-start | bytes 196616 | tf_op jit(solution)/shard_map/ppermute | solution.py:402
  7.9 1.7 %collective-permute-done = bf16[256,256]{1,0:T(8,128)(2,1)S(1)} collective-permute-done((bf16[256,256]{1,0:T(8,128)(2,1)S(1)}, bf16[256,256]{1,0:T(8,128)(2,1)S(1)}, u32[]{:S(2)}, u32[]{:S(2)}) %collective-permute-start) | collective-permute-done | bytes 131104 | tf_op jit(solution)/shard_map/ppermute | solution.py:399
  9.6 2.1 %collective-permute-start.1 = (bf16[1,256,256]{2,1,0:T(8,128)(2,1)S(1)}, bf16[1,256,256]{2,1,0:T(8,128)(2,1)S(1)}, u32[]{:S(2)}, u32[]{:S(2)}) collective-permute-start(bf16[1,256,256]{2,1,0:T(8,128)(2,1)S(1)} %bitcast.18), channel_id=1, source_target_pairs={{0,1},{1,0},{2,3},{3,2},{4,5},{5,4},{6,7},{7,6},{8,9},{9,8},{10,11... | collective-permute-start | bytes 393224 | tf_op jit(solution)/shard_map/ppermute | solution.py:401
  11.7 0.0 collective-permute-done.3.cross_ref
  11.7 1.0 %collective-permute-done.1.other_ref = bf16[1,256,256]{2,1,0:T(8,128)(2,1)S(1)} collective-permute-done((bf16[1,256,256]{2,1,0:T(8,128)(2,1)S(1)}, bf16[1,256,256]{2,1,0:T(8,128)(2,1)S(1)}, u32[]{:S(2)}, u32[]{:S(2)}) %collective-permute-start.1) | collective-permute-done | bytes 131104 | tf_op jit(solution)/shard_map/ppermute | solution.py:401
  12.7 0.0 copy-done.3
  12.7 1.4 %attend_own.1 = (bf16[256,256]{1,0:T(8,128)(2,1)S(1)}, bf16[768,512]{1,0:T(8,128)(2,1)S(1)}, f32[2,256,256]{2,1,0:T(8,128)S(1)}, bf16[1024,128]{1,0:T(8,128)(2,1)S(1)}, bf16[1024,128]{1,0:T(8,128)(2,1)S(1)}) custom-call(s32[2,256]{1,0:T(2,128)S(1)} %bitcast.21, bf16[256,128]{1,0:T(8,128)(2,1)S(1)} %copy-done.2, bf16[256,128]{1,0:T(8,128)(2,1)S(1)} %copy-done.3, ...), custom_call_target="tpu_custom_call" | custom-call | tf_op jit(solution)/shard_map/attend_own/pallas_call | solution.py:413
  14.1 0.3 %collective-permute-start.4 = (s32[2]{0:T(128)S(1)}, s32[2]{0:T(128)S(1)}, u32[]{:S(2)}, u32[]{:S(2)}) collective-permute-start(s32[2]{0:T(128)S(1)} %get-tuple-element.26), channel_id=1, source_target_pairs={{0,4},{1,3},{2,6},{3,1},{4,0},{5,9},{6,2},{7,11},{8,12},{9,5},{10,... | collective-permute-start | bytes 32 | tf_op jit(solution)/shard_map/ppermute | solution.py:424
  14.4 0.0 collective-permute-done.6.qg_ref
  14.4 1.2 %attend_next.1 = (bf16[256,256]{1,0:T(8,128)(2,1)S(1)}, bf16[768,512]{1,0:T(8,128)(2,1)S(1)}, f32[256,256]{1,0:T(8,128)S(1)}, bf16[1,256,256]{2,1,0:T(8,128)(2,1)S(1)}) custom-call(s32[2,256]{1,0:T(2,128)S(1)} %bitcast.20, bf16[1024,128]{1,0:T(8,128)(2,1)S(1)} %get-tuple-element.27.kbuf, bf16[1024,128]{1,0:T(8,128)(2,1)S(1)} %get-tuple-element.29.vbuf, ...), custom_call_target="tpu_custom_call" | custom-call | tf_op jit(solution)/shard_map/attend_next/pallas_call | solution.py:428
  15.6 1.3 %collective-permute-start.9 = (bf16[256,256]{1,0:T(8,128)(2,1)S(1)}, bf16[256,256]{1,0:T(8,128)(2,1)S(1)}, u32[]{:S(2)}, u32[]{:S(2)}) collective-permute-start(bf16[256,256]{1,0:T(8,128)(2,1)S(1)} %bitcast.22), channel_id=1, source_target_pairs={{4,0},{6,2},{8,4},{10,6},{12,8},{14,10},{5,1},{7,3},{9,5},{11,7},{... | collective-permute-start | bytes 393224 | tf_op jit(solution)/shard_map/ppermute | solution.py:453
  16.9 0.0 collective-permute-done.4
  16.9 1.1 %collective-permute-start.5 = (s32[2]{0:T(128)S(1)}, s32[2]{0:T(128)S(1)}, u32[]{:S(2)}, u32[]{:S(2)}) collective-permute-start(s32[2]{0:T(128)S(1)} %collective-permute-done.4), channel_id=1, source_target_pairs={{0,1},{1,0},{2,3},{3,2},{4,5},{5,4},{6,7},{7,6},{8,9},{9,8},{10,11... | collective-permute-start | bytes 32 | tf_op jit(solution)/shard_map/ppermute | solution.py:425
  18.0 0.8 %collective-permute-done.5 = s32[2]{0:T(128)S(1)} collective-permute-done((s32[2]{0:T(128)S(1)}, s32[2]{0:T(128)S(1)}, u32[]{:S(2)}, u32[]{:S(2)}) %collective-permute-start.5) | collective-permute-done | bytes 40 | tf_op jit(solution)/shard_map/ppermute | solution.py:425
  18.9 0.1 broadcast_select_fusion
  18.9 0.5 %send_rows.1 = (bf16[512,512]{1,0:T(8,128)(2,1)S(1)}, bf16[256,512]{1,0:T(8,128)(2,1)S(1)}, bf16[256,512]{1,0:T(8,128)(2,1)S(1)}) custom-call(s32[1,128]{1,0:T(1,128)S(1)} %pad_bitcast_fusion.plan_ref, bf16[1024,128]{1,0:T(8,128)(2,1)S(1)} %get-tuple-element.27.kbuf, bf16[768,512]{1,0:T(8,128)(2,1)S(1)} %get-tuple-element.28.d_own, ...), custom_call_target="tpu_custom_call" | custom-call | tf_op jit(solution)/shard_map/send_rows/pallas_call | solution.py:440
  19.5 0.5 %collective-permute-start.7 = (bf16[256,512]{1,0:T(8,128)(2,1)S(1)}, bf16[256,512]{1,0:T(8,128)(2,1)S(1)}, u32[]{:S(2)}, u32[]{:S(2)}) collective-permute-start(bf16[256,512]{1,0:T(8,128)(2,1)S(1)} %get-tuple-element.36), channel_id=1, source_target_pairs={{0,4},{1,3},{2,6},{3,1},{4,0},{5,9},{6,2},{7,11},{8,12},{9,5},{10,... | collective-permute-start | bytes 786440 | tf_op jit(solution)/shard_map/ppermute | solution.py:449
  20.0 2.7 %collective-permute-start.8 = (bf16[256,512]{1,0:T(8,128)(2,1)S(1)}, bf16[256,512]{1,0:T(8,128)(2,1)S(1)}, u32[]{:S(2)}, u32[]{:S(2)}) collective-permute-start(bf16[256,512]{1,0:T(8,128)(2,1)S(1)} %get-tuple-element.37), channel_id=1, source_target_pairs={{0,2},{1,5},{2,0},{3,7},{4,8},{5,1},{6,10},{7,3},{8,4},{9,13},{10,... | collective-permute-start | bytes 786440 | tf_op jit(solution)/shard_map/ppermute | solution.py:450
  22.7 0.0 collective-permute-done.9
  22.8 0.7 %collective-permute-start.10 = (f32[256,256]{1,0:T(8,128)S(1)}, f32[256,256]{1,0:T(8,128)S(1)}, u32[]{:S(2)}, u32[]{:S(2)}) collective-permute-start(f32[256,256]{1,0:T(8,128)S(1)} %convert_add_fusion.s_ref), channel_id=1, source_target_pairs={{0,1},{1,0},{2,3},{3,2},{4,5},{5,4},{6,7},{7,6},{8,9},{9,8},{10,11... | collective-permute-start | bytes 786440 | tf_op jit(solution)/shard_map/ppermute | solution.py:454
  23.5 1.8 %collective-permute-done.7.a_ref = bf16[256,512]{1,0:T(8,128)(2,1)S(1)} collective-permute-done((bf16[256,512]{1,0:T(8,128)(2,1)S(1)}, bf16[256,512]{1,0:T(8,128)(2,1)S(1)}, u32[]{:S(2)}, u32[]{:S(2)}) %collective-permute-start.7) | collective-permute-done | bytes 262176 | tf_op jit(solution)/shard_map/ppermute | solution.py:449
  25.3 3.0 %collective-permute-done.8.b_ref = bf16[256,512]{1,0:T(8,128)(2,1)S(1)} collective-permute-done((bf16[256,512]{1,0:T(8,128)(2,1)S(1)}, bf16[256,512]{1,0:T(8,128)(2,1)S(1)}, u32[]{:S(2)}, u32[]{:S(2)}) %collective-permute-start.8) | collective-permute-done | bytes 262176 | tf_op jit(solution)/shard_map/ppermute | solution.py:450
  28.4 0.0 collective-permute-done.10.t_ref
  28.4 1.1 %place.1 = (bf16[256,256]{1,0:T(8,128)(2,1)}, f32[256,256]{1,0:T(8,128)}, f32[256,128]{1,0:T(8,128)}, f32[256,128]{1,0:T(8,128)}) custom-call(s32[1,128]{1,0:T(1,128)S(1)} %pad_bitcast_fusion.1.plan_ref, bf16[512,512]{1,0:T(8,128)(2,1)S(1)} %get-tuple-element.35.row_ref, bf16[256,512]{1,0:T(8,128)(2,1)S(1)} %collective-permute-done.7.a_ref, ...), custom_call_target="tpu_custom_call" | custom-call | tf_op jit(solution)/shard_map/place/pallas_call | solution.py:456
  (18 shorter events, 0.1 us)
Async XLA Ops:
  0.6 12.1 %copy-start.1 = (bf16[256,256]{1,0:T(8,128)(2,1)S(1)}, bf16[256,256]{1,0:T(8,128)(2,1)}, u32[]{:S(2)}) copy-start(bf16[256,256]{1,0:T(8,128)(2,1)} %g_ref.3) | copy-start | bytes 393220
  0.6 12.0 %copy-start = (bf16[256,256]{1,0:T(8,128)(2,1)S(1)}, bf16[256,256]{1,0:T(8,128)(2,1)}, u32[]{:S(2)}) copy-start(bf16[256,256]{1,0:T(8,128)(2,1)} %q_ref.3) | copy-start | bytes 393220
  0.7 12.0 %copy-start.2 = (bf16[256,128]{1,0:T(8,128)(2,1)S(1)}, bf16[256,128]{1,0:T(8,128)(2,1)}, u32[]{:S(2)}) copy-start(bf16[256,128]{1,0:T(8,128)(2,1)} %k_ref.3) | copy-start | bytes 196612
  0.7 12.0 %copy-start.3 = (bf16[256,128]{1,0:T(8,128)(2,1)S(1)}, bf16[256,128]{1,0:T(8,128)(2,1)}, u32[]{:S(2)}) copy-start(bf16[256,128]{1,0:T(8,128)(2,1)} %v_ref.3) | copy-start | bytes 196612
  1.8 5.5 %collective-permute-start.2 = (bf16[256,128]{1,0:T(8,128)(2,1)S(1)}, bf16[256,128]{1,0:T(8,128)(2,1)S(1)}, u32[]{:S(2)}, u32[]{:S(2)}) collective-permute-start(bf16[256,128]{1,0:T(8,128)(2,1)S(1)} %get-tuple-element.23), channel_id=1, source_target_pairs={{0,2},{2,0},{4,6},{6,4},{8,10},{10,8},{12,14},{14,12},{1,3},{3,1},... | collective-permute-start | bytes 196616 | tf_op jit(solution)/shard_map/ppermute | solution.py:398
  3.9 5.7 %collective-permute-start = (bf16[256,256]{1,0:T(8,128)(2,1)S(1)}, bf16[256,256]{1,0:T(8,128)(2,1)S(1)}, u32[]{:S(2)}, u32[]{:S(2)}) collective-permute-start(bf16[256,256]{1,0:T(8,128)(2,1)S(1)} %get-tuple-element.22), channel_id=1, source_target_pairs={{0,4},{1,7},{2,6},{3,5},{4,8},{5,11},{6,10},{7,9},{8,12},{9,15},{1... | collective-permute-start | bytes 393224 | tf_op jit(solution)/shard_map/ppermute | solution.py:399
  5.2 9.2 %collective-permute-start.6 = (bf16[256,512]{1,0:T(8,128)(2,1)S(1)}, bf16[256,512]{1,0:T(8,128)(2,1)S(1)}, u32[]{:S(2)}, u32[]{:S(2)}) collective-permute-start(bf16[256,512]{1,0:T(8,128)(2,1)S(1)} %get-tuple-element.30), channel_id=1, source_target_pairs={{0,2},{2,0},{4,6},{6,4},{8,10},{10,8},{12,14},{14,12},{1,3},{3,1},... | collective-permute-start | bytes 786440 | tf_op jit(solution)/shard_map/ppermute | solution.py:397
  6.4 0.7 %copy-start.5 = (s32[16]{0:T(128)S(1)}, s32[16]{0:T(128)}, u32[]{:S(2)}) copy-start(s32[16]{0:T(128)} %param.10) | copy-start | bytes 196
  7.3 4.4 %collective-permute-start.3 = (bf16[256,128]{1,0:T(8,128)(2,1)S(1)}, bf16[256,128]{1,0:T(8,128)(2,1)S(1)}, u32[]{:S(2)}, u32[]{:S(2)}) collective-permute-start(bf16[256,128]{1,0:T(8,128)(2,1)S(1)} %collective-permute-done.2.half_ref), channel_id=1, source_target_pairs={{0,1},{1,0},{2,3},{3,2},{4,5},{5,4},{6,7},{7,6},{8,9},{9,8},{10,11... | collective-permute-start | bytes 196616 | tf_op jit(solution)/shard_map/ppermute | solution.py:402
  9.6 3.1 %collective-permute-start.1 = (bf16[1,256,256]{2,1,0:T(8,128)(2,1)S(1)}, bf16[1,256,256]{2,1,0:T(8,128)(2,1)S(1)}, u32[]{:S(2)}, u32[]{:S(2)}) collective-permute-start(bf16[1,256,256]{2,1,0:T(8,128)(2,1)S(1)} %bitcast.18), channel_id=1, source_target_pairs={{0,1},{1,0},{2,3},{3,2},{4,5},{5,4},{6,7},{7,6},{8,9},{9,8},{10,11... | collective-permute-start | bytes 393224 | tf_op jit(solution)/shard_map/ppermute | solution.py:401
  14.1 2.8 %collective-permute-start.4 = (s32[2]{0:T(128)S(1)}, s32[2]{0:T(128)S(1)}, u32[]{:S(2)}, u32[]{:S(2)}) collective-permute-start(s32[2]{0:T(128)S(1)} %get-tuple-element.26), channel_id=1, source_target_pairs={{0,4},{1,3},{2,6},{3,1},{4,0},{5,9},{6,2},{7,11},{8,12},{9,5},{10,... | collective-permute-start | bytes 32 | tf_op jit(solution)/shard_map/ppermute | solution.py:424
  15.6 7.1 %collective-permute-start.9 = (bf16[256,256]{1,0:T(8,128)(2,1)S(1)}, bf16[256,256]{1,0:T(8,128)(2,1)S(1)}, u32[]{:S(2)}, u32[]{:S(2)}) collective-permute-start(bf16[256,256]{1,0:T(8,128)(2,1)S(1)} %bitcast.22), channel_id=1, source_target_pairs={{4,0},{6,2},{8,4},{10,6},{12,8},{14,10},{5,1},{7,3},{9,5},{11,7},{... | collective-permute-start | bytes 393224 | tf_op jit(solution)/shard_map/ppermute | solution.py:453
  16.9 1.9 %collective-permute-start.5 = (s32[2]{0:T(128)S(1)}, s32[2]{0:T(128)S(1)}, u32[]{:S(2)}, u32[]{:S(2)}) collective-permute-start(s32[2]{0:T(128)S(1)} %collective-permute-done.4), channel_id=1, source_target_pairs={{0,1},{1,0},{2,3},{3,2},{4,5},{5,4},{6,7},{7,6},{8,9},{9,8},{10,11... | collective-permute-start | bytes 32 | tf_op jit(solution)/shard_map/ppermute | solution.py:425
  19.5 5.8 %collective-permute-start.7 = (bf16[256,512]{1,0:T(8,128)(2,1)S(1)}, bf16[256,512]{1,0:T(8,128)(2,1)S(1)}, u32[]{:S(2)}, u32[]{:S(2)}) collective-permute-start(bf16[256,512]{1,0:T(8,128)(2,1)S(1)} %get-tuple-element.36), channel_id=1, source_target_pairs={{0,4},{1,3},{2,6},{3,1},{4,0},{5,9},{6,2},{7,11},{8,12},{9,5},{10,... | collective-permute-start | bytes 786440 | tf_op jit(solution)/shard_map/ppermute | solution.py:449
  20.0 8.3 %collective-permute-start.8 = (bf16[256,512]{1,0:T(8,128)(2,1)S(1)}, bf16[256,512]{1,0:T(8,128)(2,1)S(1)}, u32[]{:S(2)}, u32[]{:S(2)}) collective-permute-start(bf16[256,512]{1,0:T(8,128)(2,1)S(1)} %get-tuple-element.37), channel_id=1, source_target_pairs={{0,2},{1,5},{2,0},{3,7},{4,8},{5,1},{6,10},{7,3},{8,4},{9,13},{10,... | collective-permute-start | bytes 786440 | tf_op jit(solution)/shard_map/ppermute | solution.py:450
  22.7 0.8 %copy-start.4 = (s32[2]{0:T(128)S(1)}, s32[2]{0:T(128)}, u32[]{:S(2)}) copy-start(s32[2]{0:T(128)} %plan_ref.1) | copy-start | bytes 28
  22.8 5.6 %collective-permute-start.10 = (f32[256,256]{1,0:T(8,128)S(1)}, f32[256,256]{1,0:T(8,128)S(1)}, u32[]{:S(2)}, u32[]{:S(2)}) collective-permute-start(f32[256,256]{1,0:T(8,128)S(1)} %convert_add_fusion.s_ref), channel_id=1, source_target_pairs={{0,1},{1,0},{2,3},{3,2},{4,5},{5,4},{6,7},{7,6},{8,9},{9,8},{10,11... | collective-permute-start | bytes 786440 | tf_op jit(solution)/shard_map/ppermute | solution.py:454

commit v6 on v5

--- a/solution.py
+++ b/solution.py
@@ -315,29 +315,43 @@
 
 
 def place_kernel(width):
-    def kernel(plan_ref, row_ref, a_ref, b_ref, s_ref, t_ref, out_ref, dq_ref, dk_ref, dv_ref):
+    def kernel(plan_ref, row_ref, a_ref, b_ref, s_ref, t_ref, out_ref, dq_ref, dk_ref, dv_ref,
+               rows_buf, dq_buf, dk_buf, dv_buf, sems):
         here = lax.axis_index("ctx")
         side = lax.axis_index("head")
         z = here // 2
         source_a = up_down(z, side)
         plan = scalars(plan_ref, 2)
+        half = dk_buf.shape[1]
+        copies = []
+
+        def send(buf, out, number):
+            copy = pltpu.make_async_copy(buf, out, sems.at[number])
+            copy.start()
+            copies.append(copy)
+
+        dk_buf[...] = s_ref[:, :half] + t_ref[:, :half]
+        send(dk_buf, dk_ref, 0)
+        dv_buf[...] = s_ref[:, half:] + t_ref[:, half:]
+        send(dv_buf, dv_ref, 1)
         for slot in range(2):
             wanted = plan[slot]
             to = pl.ds(slot * CHUNK, CHUNK)
             inside = row_of(wanted, here % 2)
 
             def put(rows):
-                out_ref[to, :] = rows[:, :width]
-                dq_ref[to, :] = rows[:, width:].astype(jnp.float32)
+                rows_buf[to, :] = rows[:, :width]
+                dq_buf[to, :] = rows[:, width:].astype(jnp.float32)
 
             home = wanted // 4 == z
             from_a = wanted // 4 == source_a
             pl.when(home)(lambda: put(row_ref[inside, :]))
             pl.when(from_a)(lambda: put(a_ref[to, :]))
             pl.when(jnp.logical_not(home | from_a))(lambda: put(b_ref[to, :]))
-        half = dk_ref.shape[1]
-        dk_ref[...] = s_ref[:, :half] + t_ref[:, :half]
-        dv_ref[...] = s_ref[:, half:] + t_ref[:, half:]
+            send(rows_buf.at[to, :], out_ref.at[to, :], 2 + 2 * slot)
+            send(dq_buf.at[to, :], dq_ref.at[to, :], 3 + 2 * slot)
+        for copy in copies:
+            copy.wait()
 
     return kernel
 
@@ -462,7 +476,12 @@
             jax.ShapeDtypeStruct((tok, head_dim), f32),
         ),
         in_specs=[VMEM] * 6,
-        out_specs=(VMEM,) * 4,
+        out_specs=(pl.BlockSpec(memory_space=pl.ANY),) * 4,
+        scratch_shapes=[
+            pltpu.VMEM((tok, width), bf16), pltpu.VMEM((tok, width), f32),
+            pltpu.VMEM((tok, head_dim), f32), pltpu.VMEM((tok, head_dim), f32),
+            pltpu.SemaphoreType.DMA((6,)),
+        ],
         compiler_params=pltpu.CompilerParams(vmem_limit_bytes=32 << 20),
         name="place",
     )(lanes_of(stretch_plan), od, moved_a, moved_b, total, total_other)

time: 29.6 us -> 29.5 us (level)
  no operation moved by 1% of the time
where the time goes in v6:
time: 29.5 us; the launch traced here: 29.3 us
  starting transfers between devices  14 us (47%)
  waiting for transfers between devices  8.3 us (28%)
  Pallas kernels  5.22 us (18%)
  between operations  0.74 us (3%)
  local copies, waits for them, and re-layouts  0.7 us (2%)
  other arithmetic  0.31 us (1%)
    ppermute x1, waiting for transfers between devices, per_device(): moved_b = lax.ppermute(send_b, both, tie_b)  3.04 us
    ppermute x1, starting transfers between devices, per_device(): moved_b = lax.ppermute(send_b, both, tie_b)  2.71 us
    ppermute x1, starting transfers between devices, per_device(): half_next = lax.ppermute(half, 'ctx', near)  2.11 us
    ppermute x1, starting transfers between devices, per_device(): other = lax.ppermute(mine, 'head', cross)  2.09 us
    ppermute x1, waiting for transfers between devices, per_device(): moved_a = lax.ppermute(send_a, both, tie_a)  1.79 us
    ppermute x1, waiting for transfers between devices, per_device(): mine = [lax.ppermute(own_kv, both, fetch_pairs(r)) for r in range(rounds)]  1.66 us
    pallas_call x1, Pallas kernels, per_device(): pl.pallas_call(own_kernel(sizes), out_shape=(attended, grads, key_sums, b...  1.36 us
    ppermute x1, starting transfers between devices, per_device(): total = total + lax.ppermute(far[r], 'ctx', back_pairs(r + 1)).astype(f32)  1.29 us
  transfers between devices with their start and end apart: 11, of which 5 were waited for; matrix products, arithmetic and copies ran while one was open for 1% of the time, Pallas kernels for 11%

profile of v6, /device:TPU:1, one launch (start us, length us, event | category | flops | bytes accessed | tf_op | source)
XLA Modules:
  0.0 29.3 jit_solution(9432273337989847426)
XLA Ops:
  0.6 0.0 copy-start.1
  0.7 1.1 %pack.1 = (s32[2]{0:T(128)S(1)}, bf16[256,256]{1,0:T(8,128)(2,1)S(1)}, bf16[256,128]{1,0:T(8,128)(2,1)S(1)}, bf16[256,512]{1,0:T(8,128)(2,1)S(1)}) custom-call(s32[2]{0:T(128)} %plan_ref.1, bf16[256,128]{1,0:T(8,128)(2,1)} %k_ref.3, bf16[256,128]{1,0:T(8,128)(2,1)} %v_ref.3, bf16[256,256]{1,0:T(8,128)(2,1)} %q_ref.3, bf16[256,256]{1,0:T(8,128)(2,1)} %g_ref.3), custom_call_target="tpu_custom_call" | custom-call | tf_op jit(solution)/shard_map/pack/pallas_call | solution.py:396
  1.8 2.1 %collective-permute-start.2 = (bf16[256,128]{1,0:T(8,128)(2,1)S(1)}, bf16[256,128]{1,0:T(8,128)(2,1)S(1)}, u32[]{:S(2)}, u32[]{:S(2)}) collective-permute-start(bf16[256,128]{1,0:T(8,128)(2,1)S(1)} %get-tuple-element.23), channel_id=1, source_target_pairs={{0,2},{2,0},{4,6},{6,4},{8,10},{10,8},{12,14},{14,12},{1,3},{3,1},... | collective-permute-start | bytes 196616 | tf_op jit(solution)/shard_map/ppermute | solution.py:412
  3.9 1.3 %collective-permute-start = (bf16[256,256]{1,0:T(8,128)(2,1)S(1)}, bf16[256,256]{1,0:T(8,128)(2,1)S(1)}, u32[]{:S(2)}, u32[]{:S(2)}) collective-permute-start(bf16[256,256]{1,0:T(8,128)(2,1)S(1)} %get-tuple-element.22), channel_id=1, source_target_pairs={{0,4},{1,7},{2,6},{3,5},{4,8},{5,11},{6,10},{7,9},{8,12},{9,15},{1... | collective-permute-start | bytes 393224 | tf_op jit(solution)/shard_map/ppermute | solution.py:413
  5.2 1.2 %collective-permute-start.6 = (bf16[256,512]{1,0:T(8,128)(2,1)S(1)}, bf16[256,512]{1,0:T(8,128)(2,1)S(1)}, u32[]{:S(2)}, u32[]{:S(2)}) collective-permute-start(bf16[256,512]{1,0:T(8,128)(2,1)S(1)} %get-tuple-element.30), channel_id=1, source_target_pairs={{0,2},{2,0},{4,6},{6,4},{8,10},{10,8},{12,14},{14,12},{1,3},{3,1},... | collective-permute-start | bytes 786440 | tf_op jit(solution)/shard_map/ppermute | solution.py:411
  6.4 0.7 %copy-done.5 = s32[16]{0:T(128)S(1)} copy-done((s32[16]{0:T(128)S(1)}, s32[16]{0:T(128)}, u32[]{:S(2)}) %copy-start.5) | copy-done | bytes 88
  7.1 0.1 select_reduce_fusion.2
  7.2 0.1 select_reduce_fusion
  7.3 0.0 collective-permute-done.2.half_ref
  7.3 0.7 %collective-permute-start.3 = (bf16[256,128]{1,0:T(8,128)(2,1)S(1)}, bf16[256,128]{1,0:T(8,128)(2,1)S(1)}, u32[]{:S(2)}, u32[]{:S(2)}) collective-permute-start(bf16[256,128]{1,0:T(8,128)(2,1)S(1)} %collective-permute-done.2.half_ref), channel_id=1, source_target_pairs={{0,1},{1,0},{2,3},{3,2},{4,5},{5,4},{6,7},{7,6},{8,9},{9,8},{10,11... | collective-permute-start | bytes 196616 | tf_op jit(solution)/shard_map/ppermute | solution.py:416
  7.9 1.7 %collective-permute-done = bf16[256,256]{1,0:T(8,128)(2,1)S(1)} collective-permute-done((bf16[256,256]{1,0:T(8,128)(2,1)S(1)}, bf16[256,256]{1,0:T(8,128)(2,1)S(1)}, u32[]{:S(2)}, u32[]{:S(2)}) %collective-permute-start) | collective-permute-done | bytes 131104 | tf_op jit(solution)/shard_map/ppermute | solution.py:413
  9.6 2.1 %collective-permute-start.1 = (bf16[1,256,256]{2,1,0:T(8,128)(2,1)S(1)}, bf16[1,256,256]{2,1,0:T(8,128)(2,1)S(1)}, u32[]{:S(2)}, u32[]{:S(2)}) collective-permute-start(bf16[1,256,256]{2,1,0:T(8,128)(2,1)S(1)} %bitcast.18), channel_id=1, source_target_pairs={{0,1},{1,0},{2,3},{3,2},{4,5},{5,4},{6,7},{7,6},{8,9},{9,8},{10,11... | collective-permute-start | bytes 393224 | tf_op jit(solution)/shard_map/ppermute | solution.py:415
  11.7 0.0 collective-permute-done.3.cross_ref
  11.7 1.0 %collective-permute-done.1.other_ref = bf16[1,256,256]{2,1,0:T(8,128)(2,1)S(1)} collective-permute-done((bf16[1,256,256]{2,1,0:T(8,128)(2,1)S(1)}, bf16[1,256,256]{2,1,0:T(8,128)(2,1)S(1)}, u32[]{:S(2)}, u32[]{:S(2)}) %collective-permute-start.1) | collective-permute-done | bytes 131104 | tf_op jit(solution)/shard_map/ppermute | solution.py:415
  12.7 1.4 %attend_own.1 = (bf16[256,256]{1,0:T(8,128)(2,1)S(1)}, bf16[768,512]{1,0:T(8,128)(2,1)S(1)}, f32[2,256,256]{2,1,0:T(8,128)S(1)}, bf16[1024,128]{1,0:T(8,128)(2,1)S(1)}, bf16[1024,128]{1,0:T(8,128)(2,1)S(1)}) custom-call(s32[2,256]{1,0:T(2,128)S(1)} %bitcast.21, bf16[256,128]{1,0:T(8,128)(2,1)S(1)} %copy-done.2, bf16[256,128]{1,0:T(8,128)(2,1)S(1)} %copy-done.3, ...), custom_call_target="tpu_custom_call" | custom-call | tf_op jit(solution)/shard_map/attend_own/pallas_call | solution.py:427
  14.1 0.3 %collective-permute-start.4 = (s32[2]{0:T(128)S(1)}, s32[2]{0:T(128)S(1)}, u32[]{:S(2)}, u32[]{:S(2)}) collective-permute-start(s32[2]{0:T(128)S(1)} %get-tuple-element.26), channel_id=1, source_target_pairs={{0,4},{1,3},{2,6},{3,1},{4,0},{5,9},{6,2},{7,11},{8,12},{9,5},{10,... | collective-permute-start | bytes 32 | tf_op jit(solution)/shard_map/ppermute | solution.py:438
  14.4 0.0 collective-permute-done.6.qg_ref
  14.4 1.2 %attend_next.1 = (bf16[256,256]{1,0:T(8,128)(2,1)S(1)}, bf16[768,512]{1,0:T(8,128)(2,1)S(1)}, f32[256,256]{1,0:T(8,128)S(1)}, bf16[1,256,256]{2,1,0:T(8,128)(2,1)S(1)}) custom-call(s32[2,256]{1,0:T(2,128)S(1)} %bitcast.20, bf16[1024,128]{1,0:T(8,128)(2,1)S(1)} %get-tuple-element.27.kbuf, bf16[1024,128]{1,0:T(8,128)(2,1)S(1)} %get-tuple-element.29.vbuf, ...), custom_call_target="tpu_custom_call" | custom-call | tf_op jit(solution)/shard_map/attend_next/pallas_call | solution.py:442
  15.6 1.3 %collective-permute-start.9 = (bf16[256,256]{1,0:T(8,128)(2,1)S(1)}, bf16[256,256]{1,0:T(8,128)(2,1)S(1)}, u32[]{:S(2)}, u32[]{:S(2)}) collective-permute-start(bf16[256,256]{1,0:T(8,128)(2,1)S(1)} %bitcast.22), channel_id=1, source_target_pairs={{4,0},{6,2},{8,4},{10,6},{12,8},{14,10},{5,1},{7,3},{9,5},{11,7},{... | collective-permute-start | bytes 393224 | tf_op jit(solution)/shard_map/ppermute | solution.py:467
  16.9 0.0 collective-permute-done.4
  16.9 1.1 %collective-permute-start.5 = (s32[2]{0:T(128)S(1)}, s32[2]{0:T(128)S(1)}, u32[]{:S(2)}, u32[]{:S(2)}) collective-permute-start(s32[2]{0:T(128)S(1)} %collective-permute-done.4), channel_id=1, source_target_pairs={{0,1},{1,0},{2,3},{3,2},{4,5},{5,4},{6,7},{7,6},{8,9},{9,8},{10,11... | collective-permute-start | bytes 32 | tf_op jit(solution)/shard_map/ppermute | solution.py:439
  18.0 0.8 %collective-permute-done.5 = s32[2]{0:T(128)S(1)} collective-permute-done((s32[2]{0:T(128)S(1)}, s32[2]{0:T(128)S(1)}, u32[]{:S(2)}, u32[]{:S(2)}) %collective-permute-start.5) | collective-permute-done | bytes 40 | tf_op jit(solution)/shard_map/ppermute | solution.py:439
  18.9 0.1 broadcast_select_fusion
  18.9 0.5 %send_rows.1 = (bf16[512,512]{1,0:T(8,128)(2,1)S(1)}, bf16[256,512]{1,0:T(8,128)(2,1)S(1)}, bf16[256,512]{1,0:T(8,128)(2,1)S(1)}) custom-call(s32[1,128]{1,0:T(1,128)S(1)} %pad_bitcast_fusion.plan_ref, bf16[1024,128]{1,0:T(8,128)(2,1)S(1)} %get-tuple-element.27.kbuf, bf16[768,512]{1,0:T(8,128)(2,1)S(1)} %get-tuple-element.28.d_own, ...), custom_call_target="tpu_custom_call" | custom-call | tf_op jit(solution)/shard_map/send_rows/pallas_call | solution.py:454
  19.5 0.5 %collective-permute-start.7 = (bf16[256,512]{1,0:T(8,128)(2,1)S(1)}, bf16[256,512]{1,0:T(8,128)(2,1)S(1)}, u32[]{:S(2)}, u32[]{:S(2)}) collective-permute-start(bf16[256,512]{1,0:T(8,128)(2,1)S(1)} %get-tuple-element.36), channel_id=1, source_target_pairs={{0,4},{1,3},{2,6},{3,1},{4,0},{5,9},{6,2},{7,11},{8,12},{9,5},{10,... | collective-permute-start | bytes 786440 | tf_op jit(solution)/shard_map/ppermute | solution.py:463
  20.0 2.7 %collective-permute-start.8 = (bf16[256,512]{1,0:T(8,128)(2,1)S(1)}, bf16[256,512]{1,0:T(8,128)(2,1)S(1)}, u32[]{:S(2)}, u32[]{:S(2)}) collective-permute-start(bf16[256,512]{1,0:T(8,128)(2,1)S(1)} %get-tuple-element.37), channel_id=1, source_target_pairs={{0,2},{1,5},{2,0},{3,7},{4,8},{5,1},{6,10},{7,3},{8,4},{9,13},{10,... | collective-permute-start | bytes 786440 | tf_op jit(solution)/shard_map/ppermute | solution.py:464
  22.7 0.0 collective-permute-done.9
  22.8 0.7 %collective-permute-start.10 = (f32[256,256]{1,0:T(8,128)S(1)}, f32[256,256]{1,0:T(8,128)S(1)}, u32[]{:S(2)}, u32[]{:S(2)}) collective-permute-start(f32[256,256]{1,0:T(8,128)S(1)} %convert_add_fusion.s_ref), channel_id=1, source_target_pairs={{0,1},{1,0},{2,3},{3,2},{4,5},{5,4},{6,7},{7,6},{8,9},{9,8},{10,11... | collective-permute-start | bytes 786440 | tf_op jit(solution)/shard_map/ppermute | solution.py:468
  23.5 1.8 %collective-permute-done.7.a_ref = bf16[256,512]{1,0:T(8,128)(2,1)S(1)} collective-permute-done((bf16[256,512]{1,0:T(8,128)(2,1)S(1)}, bf16[256,512]{1,0:T(8,128)(2,1)S(1)}, u32[]{:S(2)}, u32[]{:S(2)}) %collective-permute-start.7) | collective-permute-done | bytes 262176 | tf_op jit(solution)/shard_map/ppermute | solution.py:463
  25.3 3.0 %collective-permute-done.8.b_ref = bf16[256,512]{1,0:T(8,128)(2,1)S(1)} collective-permute-done((bf16[256,512]{1,0:T(8,128)(2,1)S(1)}, bf16[256,512]{1,0:T(8,128)(2,1)S(1)}, u32[]{:S(2)}, u32[]{:S(2)}) %collective-permute-start.8) | collective-permute-done | bytes 262176 | tf_op jit(solution)/shard_map/ppermute | solution.py:464
  28.4 0.0 collective-permute-done.10.t_ref
  28.4 1.0 %place.1 = (bf16[256,256]{1,0:T(8,128)(2,1)}, f32[256,256]{1,0:T(8,128)}, f32[256,128]{1,0:T(8,128)}, f32[256,128]{1,0:T(8,128)}) custom-call(s32[1,128]{1,0:T(1,128)S(1)} %pad_bitcast_fusion.1.plan_ref, bf16[512,512]{1,0:T(8,128)(2,1)S(1)} %get-tuple-element.35.row_ref, bf16[256,512]{1,0:T(8,128)(2,1)S(1)} %collective-permute-done.7.a_ref, ...), custom_call_target="tpu_custom_call" | custom-call | tf_op jit(solution)/shard_map/place/pallas_call | solution.py:470
  (18 shorter events, 0.1 us)
Async XLA Ops:
  0.6 12.1 %copy-start.1 = (bf16[256,256]{1,0:T(8,128)(2,1)S(1)}, bf16[256,256]{1,0:T(8,128)(2,1)}, u32[]{:S(2)}) copy-start(bf16[256,256]{1,0:T(8,128)(2,1)} %g_ref.3) | copy-start | bytes 393220
  0.6 12.0 %copy-start = (bf16[256,256]{1,0:T(8,128)(2,1)S(1)}, bf16[256,256]{1,0:T(8,128)(2,1)}, u32[]{:S(2)}) copy-start(bf16[256,256]{1,0:T(8,128)(2,1)} %q_ref.3) | copy-start | bytes 393220
  0.7 12.0 %copy-start.2 = (bf16[256,128]{1,0:T(8,128)(2,1)S(1)}, bf16[256,128]{1,0:T(8,128)(2,1)}, u32[]{:S(2)}) copy-start(bf16[256,128]{1,0:T(8,128)(2,1)} %k_ref.3) | copy-start | bytes 196612
  0.7 12.0 %copy-start.3 = (bf16[256,128]{1,0:T(8,128)(2,1)S(1)}, bf16[256,128]{1,0:T(8,128)(2,1)}, u32[]{:S(2)}) copy-start(bf16[256,128]{1,0:T(8,128)(2,1)} %v_ref.3) | copy-start | bytes 196612
  1.8 5.5 %collective-permute-start.2 = (bf16[256,128]{1,0:T(8,128)(2,1)S(1)}, bf16[256,128]{1,0:T(8,128)(2,1)S(1)}, u32[]{:S(2)}, u32[]{:S(2)}) collective-permute-start(bf16[256,128]{1,0:T(8,128)(2,1)S(1)} %get-tuple-element.23), channel_id=1, source_target_pairs={{0,2},{2,0},{4,6},{6,4},{8,10},{10,8},{12,14},{14,12},{1,3},{3,1},... | collective-permute-start | bytes 196616 | tf_op jit(solution)/shard_map/ppermute | solution.py:412
  3.9 5.7 %collective-permute-start = (bf16[256,256]{1,0:T(8,128)(2,1)S(1)}, bf16[256,256]{1,0:T(8,128)(2,1)S(1)}, u32[]{:S(2)}, u32[]{:S(2)}) collective-permute-start(bf16[256,256]{1,0:T(8,128)(2,1)S(1)} %get-tuple-element.22), channel_id=1, source_target_pairs={{0,4},{1,7},{2,6},{3,5},{4,8},{5,11},{6,10},{7,9},{8,12},{9,15},{1... | collective-permute-start | bytes 393224 | tf_op jit(solution)/shard_map/ppermute | solution.py:413
  5.2 9.2 %collective-permute-start.6 = (bf16[256,512]{1,0:T(8,128)(2,1)S(1)}, bf16[256,512]{1,0:T(8,128)(2,1)S(1)}, u32[]{:S(2)}, u32[]{:S(2)}) collective-permute-start(bf16[256,512]{1,0:T(8,128)(2,1)S(1)} %get-tuple-element.30), channel_id=1, source_target_pairs={{0,2},{2,0},{4,6},{6,4},{8,10},{10,8},{12,14},{14,12},{1,3},{3,1},... | collective-permute-start | bytes 786440 | tf_op jit(solution)/shard_map/ppermute | solution.py:411
  6.4 0.7 %copy-start.5 = (s32[16]{0:T(128)S(1)}, s32[16]{0:T(128)}, u32[]{:S(2)}) copy-start(s32[16]{0:T(128)} %param.10) | copy-start | bytes 196
  7.3 4.4 %collective-permute-start.3 = (bf16[256,128]{1,0:T(8,128)(2,1)S(1)}, bf16[256,128]{1,0:T(8,128)(2,1)S(1)}, u32[]{:S(2)}, u32[]{:S(2)}) collective-permute-start(bf16[256,128]{1,0:T(8,128)(2,1)S(1)} %collective-permute-done.2.half_ref), channel_id=1, source_target_pairs={{0,1},{1,0},{2,3},{3,2},{4,5},{5,4},{6,7},{7,6},{8,9},{9,8},{10,11... | collective-permute-start | bytes 196616 | tf_op jit(solution)/shard_map/ppermute | solution.py:416
  9.6 3.1 %collective-permute-start.1 = (bf16[1,256,256]{2,1,0:T(8,128)(2,1)S(1)}, bf16[1,256,256]{2,1,0:T(8,128)(2,1)S(1)}, u32[]{:S(2)}, u32[]{:S(2)}) collective-permute-start(bf16[1,256,256]{2,1,0:T(8,128)(2,1)S(1)} %bitcast.18), channel_id=1, source_target_pairs={{0,1},{1,0},{2,3},{3,2},{4,5},{5,4},{6,7},{7,6},{8,9},{9,8},{10,11... | collective-permute-start | bytes 393224 | tf_op jit(solution)/shard_map/ppermute | solution.py:415
  14.1 2.8 %collective-permute-start.4 = (s32[2]{0:T(128)S(1)}, s32[2]{0:T(128)S(1)}, u32[]{:S(2)}, u32[]{:S(2)}) collective-permute-start(s32[2]{0:T(128)S(1)} %get-tuple-element.26), channel_id=1, source_target_pairs={{0,4},{1,3},{2,6},{3,1},{4,0},{5,9},{6,2},{7,11},{8,12},{9,5},{10,... | collective-permute-start | bytes 32 | tf_op jit(solution)/shard_map/ppermute | solution.py:438
  15.6 7.1 %collective-permute-start.9 = (bf16[256,256]{1,0:T(8,128)(2,1)S(1)}, bf16[256,256]{1,0:T(8,128)(2,1)S(1)}, u32[]{:S(2)}, u32[]{:S(2)}) collective-permute-start(bf16[256,256]{1,0:T(8,128)(2,1)S(1)} %bitcast.22), channel_id=1, source_target_pairs={{4,0},{6,2},{8,4},{10,6},{12,8},{14,10},{5,1},{7,3},{9,5},{11,7},{... | collective-permute-start | bytes 393224 | tf_op jit(solution)/shard_map/ppermute | solution.py:467
  16.9 1.9 %collective-permute-start.5 = (s32[2]{0:T(128)S(1)}, s32[2]{0:T(128)S(1)}, u32[]{:S(2)}, u32[]{:S(2)}) collective-permute-start(s32[2]{0:T(128)S(1)} %collective-permute-done.4), channel_id=1, source_target_pairs={{0,1},{1,0},{2,3},{3,2},{4,5},{5,4},{6,7},{7,6},{8,9},{9,8},{10,11... | collective-permute-start | bytes 32 | tf_op jit(solution)/shard_map/ppermute | solution.py:439
  19.5 5.8 %collective-permute-start.7 = (bf16[256,512]{1,0:T(8,128)(2,1)S(1)}, bf16[256,512]{1,0:T(8,128)(2,1)S(1)}, u32[]{:S(2)}, u32[]{:S(2)}) collective-permute-start(bf16[256,512]{1,0:T(8,128)(2,1)S(1)} %get-tuple-element.36), channel_id=1, source_target_pairs={{0,4},{1,3},{2,6},{3,1},{4,0},{5,9},{6,2},{7,11},{8,12},{9,5},{10,... | collective-permute-start | bytes 786440 | tf_op jit(solution)/shard_map/ppermute | solution.py:463
  20.0 8.3 %collective-permute-start.8 = (bf16[256,512]{1,0:T(8,128)(2,1)S(1)}, bf16[256,512]{1,0:T(8,128)(2,1)S(1)}, u32[]{:S(2)}, u32[]{:S(2)}) collective-permute-start(bf16[256,512]{1,0:T(8,128)(2,1)S(1)} %get-tuple-element.37), channel_id=1, source_target_pairs={{0,2},{1,5},{2,0},{3,7},{4,8},{5,1},{6,10},{7,3},{8,4},{9,13},{10,... | collective-permute-start | bytes 786440 | tf_op jit(solution)/shard_map/ppermute | solution.py:464
  22.7 0.8 %copy-start.4 = (s32[2]{0:T(128)S(1)}, s32[2]{0:T(128)}, u32[]{:S(2)}) copy-start(s32[2]{0:T(128)} %plan_ref.1) | copy-start | bytes 28
  22.8 5.6 %collective-permute-start.10 = (f32[256,256]{1,0:T(8,128)S(1)}, f32[256,256]{1,0:T(8,128)S(1)}, u32[]{:S(2)}, u32[]{:S(2)}) collective-permute-start(f32[256,256]{1,0:T(8,128)S(1)} %convert_add_fusion.s_ref), channel_id=1, source_target_pairs={{0,1},{1,0},{2,3},{3,2},{4,5},{5,4},{6,7},{7,6},{8,9},{9,8},{10,11... | collective-permute-start | bytes 786440 | tf_op jit(solution)/shard_map/ppermute | solution.py:468

commit v7 on v6

--- a/solution.py
+++ b/solution.py
@@ -272,17 +272,17 @@
         here = lax.axis_index("ctx")
         z = here // 2
         x = here % 2
-        sums[...] = own_kv[...]
-
         def put(r, dk, dv):
-            at = r + x
-            sums[at, :, :head_dim] = sums[at, :, :head_dim] + dk
-            sums[at, :, head_dim:] = sums[at, :, head_dim:] + dv
+            sums[r, :, :head_dim] = dk
+            sums[r, :, head_dim:] = dv
 
         two_stretches(sizes, begin_ref, z, 1 - x, kbuf, vbuf, qg_ref.at[:, :width],
                       qg_ref.at[:, width:], w_ref, p_ref, d_ref, att_ref, (1, rounds), put)
-        kv_out[...] = sums[0]
-        far_out[...] = sums[1:].astype(far_out.dtype)
+        here_first = x == 0
+        kv_out[...] = own_kv[0] + jnp.where(here_first, sums[0], 0.0)
+        for r in range(rounds):
+            term = jnp.where(here_first, sums[r + 1] if r + 1 < rounds else 0.0, sums[r])
+            far_out[r] = (own_kv[r + 1] + term).astype(far_out.dtype)
 
     return kernel
 
@@ -447,7 +447,7 @@
         ),
         in_specs=[VMEM] * 5,
         out_specs=(VMEM,) * 4,
-        scratch_shapes=[scores, weights, pltpu.VMEM((rounds + 1, tok, 2 * head_dim), f32)],
+        scratch_shapes=[scores, weights, pltpu.VMEM((rounds, tok, 2 * head_dim), f32)],
         compiler_params=params,
         name="attend_next",
     )(begins(here ^ 1), kbuf, vbuf, part, kv_own)

time: 29.5 us -> 29.5 us (level)
  transfers between devices with their start and end apart: 11 -> 11, of which waited for: 5 -> 5; matrix products, arithmetic and copies ran while one was open for 1% -> 1% of each run, Pallas kernels for 11% -> 10%
where the time goes in v7:
time: 29.5 us; the launch traced here: 29.3 us
  starting transfers between devices  14 us (47%)
  waiting for transfers between devices  8.41 us (29%)
  Pallas kernels  5.1 us (17%)
  between operations  0.74 us (3%)
  local copies, waits for them, and re-layouts  0.7 us (2%)
  other arithmetic  0.31 us (1%)
    ppermute x1, waiting for transfers between devices, per_device(): moved_b = lax.ppermute(send_b, both, tie_b)  2.93 us
    ppermute x1, starting transfers between devices, per_device(): moved_b = lax.ppermute(send_b, both, tie_b)  2.71 us
    ppermute x1, starting transfers between devices, per_device(): half_next = lax.ppermute(half, 'ctx', near)  2.11 us
    ppermute x1, starting transfers between devices, per_device(): other = lax.ppermute(mine, 'head', cross)  2.09 us
    ppermute x1, waiting for transfers between devices, per_device(): moved_a = lax.ppermute(send_a, both, tie_a)  2.02 us
    ppermute x1, waiting for transfers between devices, per_device(): mine = [lax.ppermute(own_kv, both, fetch_pairs(r)) for r in range(rounds)]  1.66 us
    pallas_call x1, Pallas kernels, per_device(): pl.pallas_call(own_kernel(sizes), out_shape=(attended, grads, key_sums, b...  1.36 us
    ppermute x1, starting transfers between devices, per_device(): total = total + lax.ppermute(far[r], 'ctx', back_pairs(r + 1)).astype(f32)  1.29 us
  transfers between devices with their start and end apart: 11, of which 5 were waited for; matrix products, arithmetic and copies ran while one was open for 1% of the time, Pallas kernels for 10%

profile of v7, /device:TPU:1, one launch (start us, length us, event | category | flops | bytes accessed | tf_op | source)
XLA Modules:
  0.0 29.3 jit_solution(10663705302537300195)
XLA Ops:
  0.7 1.1 %pack.1 = (s32[2]{0:T(128)S(1)}, bf16[256,256]{1,0:T(8,128)(2,1)S(1)}, bf16[256,128]{1,0:T(8,128)(2,1)S(1)}, bf16[256,512]{1,0:T(8,128)(2,1)S(1)}) custom-call(s32[2]{0:T(128)} %plan_ref.1, bf16[256,128]{1,0:T(8,128)(2,1)} %k_ref.3, bf16[256,128]{1,0:T(8,128)(2,1)} %v_ref.3, bf16[256,256]{1,0:T(8,128)(2,1)} %q_ref.3, bf16[256,256]{1,0:T(8,128)(2,1)} %g_ref.3), custom_call_target="tpu_custom_call" | custom-call | tf_op jit(solution)/shard_map/pack/pallas_call | solution.py:396
  1.8 2.1 %collective-permute-start.2 = (bf16[256,128]{1,0:T(8,128)(2,1)S(1)}, bf16[256,128]{1,0:T(8,128)(2,1)S(1)}, u32[]{:S(2)}, u32[]{:S(2)}) collective-permute-start(bf16[256,128]{1,0:T(8,128)(2,1)S(1)} %get-tuple-element.23), channel_id=1, source_target_pairs={{0,2},{2,0},{4,6},{6,4},{8,10},{10,8},{12,14},{14,12},{1,3},{3,1},... | collective-permute-start | bytes 196616 | tf_op jit(solution)/shard_map/ppermute | solution.py:412
  3.9 1.3 %collective-permute-start = (bf16[256,256]{1,0:T(8,128)(2,1)S(1)}, bf16[256,256]{1,0:T(8,128)(2,1)S(1)}, u32[]{:S(2)}, u32[]{:S(2)}) collective-permute-start(bf16[256,256]{1,0:T(8,128)(2,1)S(1)} %get-tuple-element.22), channel_id=1, source_target_pairs={{0,4},{1,7},{2,6},{3,5},{4,8},{5,11},{6,10},{7,9},{8,12},{9,15},{1... | collective-permute-start | bytes 393224 | tf_op jit(solution)/shard_map/ppermute | solution.py:413
  5.2 1.2 %collective-permute-start.6 = (bf16[256,512]{1,0:T(8,128)(2,1)S(1)}, bf16[256,512]{1,0:T(8,128)(2,1)S(1)}, u32[]{:S(2)}, u32[]{:S(2)}) collective-permute-start(bf16[256,512]{1,0:T(8,128)(2,1)S(1)} %get-tuple-element.30), channel_id=1, source_target_pairs={{0,2},{2,0},{4,6},{6,4},{8,10},{10,8},{12,14},{14,12},{1,3},{3,1},... | collective-permute-start | bytes 786440 | tf_op jit(solution)/shard_map/ppermute | solution.py:411
  6.4 0.7 %copy-done.5 = s32[16]{0:T(128)S(1)} copy-done((s32[16]{0:T(128)S(1)}, s32[16]{0:T(128)}, u32[]{:S(2)}) %copy-start.5) | copy-done | bytes 88
  7.1 0.1 select_reduce_fusion.2
  7.2 0.1 select_reduce_fusion
  7.3 0.0 collective-permute-done.2.half_ref
  7.3 0.7 %collective-permute-start.3 = (bf16[256,128]{1,0:T(8,128)(2,1)S(1)}, bf16[256,128]{1,0:T(8,128)(2,1)S(1)}, u32[]{:S(2)}, u32[]{:S(2)}) collective-permute-start(bf16[256,128]{1,0:T(8,128)(2,1)S(1)} %collective-permute-done.2.half_ref), channel_id=1, source_target_pairs={{0,1},{1,0},{2,3},{3,2},{4,5},{5,4},{6,7},{7,6},{8,9},{9,8},{10,11... | collective-permute-start | bytes 196616 | tf_op jit(solution)/shard_map/ppermute | solution.py:416
  7.9 1.7 %collective-permute-done = bf16[256,256]{1,0:T(8,128)(2,1)S(1)} collective-permute-done((bf16[256,256]{1,0:T(8,128)(2,1)S(1)}, bf16[256,256]{1,0:T(8,128)(2,1)S(1)}, u32[]{:S(2)}, u32[]{:S(2)}) %collective-permute-start) | collective-permute-done | bytes 131104 | tf_op jit(solution)/shard_map/ppermute | solution.py:413
  9.6 2.1 %collective-permute-start.1 = (bf16[1,256,256]{2,1,0:T(8,128)(2,1)S(1)}, bf16[1,256,256]{2,1,0:T(8,128)(2,1)S(1)}, u32[]{:S(2)}, u32[]{:S(2)}) collective-permute-start(bf16[1,256,256]{2,1,0:T(8,128)(2,1)S(1)} %bitcast.18), channel_id=1, source_target_pairs={{0,1},{1,0},{2,3},{3,2},{4,5},{5,4},{6,7},{7,6},{8,9},{9,8},{10,11... | collective-permute-start | bytes 393224 | tf_op jit(solution)/shard_map/ppermute | solution.py:415
  11.7 0.0 collective-permute-done.3.cross_ref
  11.7 1.0 %collective-permute-done.1.other_ref = bf16[1,256,256]{2,1,0:T(8,128)(2,1)S(1)} collective-permute-done((bf16[1,256,256]{2,1,0:T(8,128)(2,1)S(1)}, bf16[1,256,256]{2,1,0:T(8,128)(2,1)S(1)}, u32[]{:S(2)}, u32[]{:S(2)}) %collective-permute-start.1) | collective-permute-done | bytes 131104 | tf_op jit(solution)/shard_map/ppermute | solution.py:415
  12.7 0.0 copy-done.1
  12.7 1.4 %attend_own.1 = (bf16[256,256]{1,0:T(8,128)(2,1)S(1)}, bf16[768,512]{1,0:T(8,128)(2,1)S(1)}, f32[2,256,256]{2,1,0:T(8,128)S(1)}, bf16[1024,128]{1,0:T(8,128)(2,1)S(1)}, bf16[1024,128]{1,0:T(8,128)(2,1)S(1)}) custom-call(s32[2,256]{1,0:T(2,128)S(1)} %bitcast.21, bf16[256,128]{1,0:T(8,128)(2,1)S(1)} %copy-done.2, bf16[256,128]{1,0:T(8,128)(2,1)S(1)} %copy-done.3, ...), custom_call_target="tpu_custom_call" | custom-call | tf_op jit(solution)/shard_map/attend_own/pallas_call | solution.py:427
  14.1 0.3 %collective-permute-start.4 = (s32[2]{0:T(128)S(1)}, s32[2]{0:T(128)S(1)}, u32[]{:S(2)}, u32[]{:S(2)}) collective-permute-start(s32[2]{0:T(128)S(1)} %get-tuple-element.26), channel_id=1, source_target_pairs={{0,4},{1,3},{2,6},{3,1},{4,0},{5,9},{6,2},{7,11},{8,12},{9,5},{10,... | collective-permute-start | bytes 32 | tf_op jit(solution)/shard_map/ppermute | solution.py:438
  14.4 0.0 collective-permute-done.6.qg_ref
  14.4 1.1 %attend_next.1 = (bf16[256,256]{1,0:T(8,128)(2,1)S(1)}, bf16[768,512]{1,0:T(8,128)(2,1)S(1)}, f32[256,256]{1,0:T(8,128)S(1)}, bf16[1,256,256]{2,1,0:T(8,128)(2,1)S(1)}) custom-call(s32[2,256]{1,0:T(2,128)S(1)} %bitcast.20, bf16[1024,128]{1,0:T(8,128)(2,1)S(1)} %get-tuple-element.27.kbuf, bf16[1024,128]{1,0:T(8,128)(2,1)S(1)} %get-tuple-element.29.vbuf, ...), custom_call_target="tpu_custom_call" | custom-call | tf_op jit(solution)/shard_map/attend_next/pallas_call | solution.py:442
  15.5 1.3 %collective-permute-start.9 = (bf16[256,256]{1,0:T(8,128)(2,1)S(1)}, bf16[256,256]{1,0:T(8,128)(2,1)S(1)}, u32[]{:S(2)}, u32[]{:S(2)}) collective-permute-start(bf16[256,256]{1,0:T(8,128)(2,1)S(1)} %bitcast.22), channel_id=1, source_target_pairs={{4,0},{6,2},{8,4},{10,6},{12,8},{14,10},{5,1},{7,3},{9,5},{11,7},{... | collective-permute-start | bytes 393224 | tf_op jit(solution)/shard_map/ppermute | solution.py:467
  16.8 0.0 collective-permute-done.4
  16.8 1.2 %collective-permute-start.5 = (s32[2]{0:T(128)S(1)}, s32[2]{0:T(128)S(1)}, u32[]{:S(2)}, u32[]{:S(2)}) collective-permute-start(s32[2]{0:T(128)S(1)} %collective-permute-done.4), channel_id=1, source_target_pairs={{0,1},{1,0},{2,3},{3,2},{4,5},{5,4},{6,7},{7,6},{8,9},{9,8},{10,11... | collective-permute-start | bytes 32 | tf_op jit(solution)/shard_map/ppermute | solution.py:439
  18.0 0.8 %collective-permute-done.5 = s32[2]{0:T(128)S(1)} collective-permute-done((s32[2]{0:T(128)S(1)}, s32[2]{0:T(128)S(1)}, u32[]{:S(2)}, u32[]{:S(2)}) %collective-permute-start.5) | collective-permute-done | bytes 40 | tf_op jit(solution)/shard_map/ppermute | solution.py:439
  18.9 0.1 broadcast_select_fusion
  18.9 0.5 %send_rows.1 = (bf16[512,512]{1,0:T(8,128)(2,1)S(1)}, bf16[256,512]{1,0:T(8,128)(2,1)S(1)}, bf16[256,512]{1,0:T(8,128)(2,1)S(1)}) custom-call(s32[1,128]{1,0:T(1,128)S(1)} %pad_bitcast_fusion.plan_ref, bf16[1024,128]{1,0:T(8,128)(2,1)S(1)} %get-tuple-element.27.kbuf, bf16[768,512]{1,0:T(8,128)(2,1)S(1)} %get-tuple-element.28.d_own, ...), custom_call_target="tpu_custom_call" | custom-call | tf_op jit(solution)/shard_map/send_rows/pallas_call | solution.py:454
  19.5 0.4 %collective-permute-start.7 = (bf16[256,512]{1,0:T(8,128)(2,1)S(1)}, bf16[256,512]{1,0:T(8,128)(2,1)S(1)}, u32[]{:S(2)}, u32[]{:S(2)}) collective-permute-start(bf16[256,512]{1,0:T(8,128)(2,1)S(1)} %get-tuple-element.36), channel_id=1, source_target_pairs={{0,4},{1,3},{2,6},{3,1},{4,0},{5,9},{6,2},{7,11},{8,12},{9,5},{10,... | collective-permute-start | bytes 786440 | tf_op jit(solution)/shard_map/ppermute | solution.py:463
  19.9 2.7 %collective-permute-start.8 = (bf16[256,512]{1,0:T(8,128)(2,1)S(1)}, bf16[256,512]{1,0:T(8,128)(2,1)S(1)}, u32[]{:S(2)}, u32[]{:S(2)}) collective-permute-start(bf16[256,512]{1,0:T(8,128)(2,1)S(1)} %get-tuple-element.37), channel_id=1, source_target_pairs={{0,2},{1,5},{2,0},{3,7},{4,8},{5,1},{6,10},{7,3},{8,4},{9,13},{10,... | collective-permute-start | bytes 786440 | tf_op jit(solution)/shard_map/ppermute | solution.py:464
  22.6 0.0 collective-permute-done.9
  22.7 0.7 %collective-permute-start.10 = (f32[256,256]{1,0:T(8,128)S(1)}, f32[256,256]{1,0:T(8,128)S(1)}, u32[]{:S(2)}, u32[]{:S(2)}) collective-permute-start(f32[256,256]{1,0:T(8,128)S(1)} %convert_add_fusion.s_ref), channel_id=1, source_target_pairs={{0,1},{1,0},{2,3},{3,2},{4,5},{5,4},{6,7},{7,6},{8,9},{9,8},{10,11... | collective-permute-start | bytes 786440 | tf_op jit(solution)/shard_map/ppermute | solution.py:468
  23.4 2.0 %collective-permute-done.7.a_ref = bf16[256,512]{1,0:T(8,128)(2,1)S(1)} collective-permute-done((bf16[256,512]{1,0:T(8,128)(2,1)S(1)}, bf16[256,512]{1,0:T(8,128)(2,1)S(1)}, u32[]{:S(2)}, u32[]{:S(2)}) %collective-permute-start.7) | collective-permute-done | bytes 262176 | tf_op jit(solution)/shard_map/ppermute | solution.py:463
  25.4 2.9 %collective-permute-done.8.b_ref = bf16[256,512]{1,0:T(8,128)(2,1)S(1)} collective-permute-done((bf16[256,512]{1,0:T(8,128)(2,1)S(1)}, bf16[256,512]{1,0:T(8,128)(2,1)S(1)}, u32[]{:S(2)}, u32[]{:S(2)}) %collective-permute-start.8) | collective-permute-done | bytes 262176 | tf_op jit(solution)/shard_map/ppermute | solution.py:464
  28.4 0.0 collective-permute-done.10.t_ref
  28.4 1.0 %place.1 = (bf16[256,256]{1,0:T(8,128)(2,1)}, f32[256,256]{1,0:T(8,128)}, f32[256,128]{1,0:T(8,128)}, f32[256,128]{1,0:T(8,128)}) custom-call(s32[1,128]{1,0:T(1,128)S(1)} %pad_bitcast_fusion.1.plan_ref, bf16[512,512]{1,0:T(8,128)(2,1)S(1)} %get-tuple-element.35.row_ref, bf16[256,512]{1,0:T(8,128)(2,1)S(1)} %collective-permute-done.7.a_ref, ...), custom_call_target="tpu_custom_call" | custom-call | tf_op jit(solution)/shard_map/place/pallas_call | solution.py:470
  (18 shorter events, 0.1 us)
Async XLA Ops:
  0.6 12.1 %copy-start.1 = (bf16[256,256]{1,0:T(8,128)(2,1)S(1)}, bf16[256,256]{1,0:T(8,128)(2,1)}, u32[]{:S(2)}) copy-start(bf16[256,256]{1,0:T(8,128)(2,1)} %g_ref.3) | copy-start | bytes 393220
  0.6 12.0 %copy-start = (bf16[256,256]{1,0:T(8,128)(2,1)S(1)}, bf16[256,256]{1,0:T(8,128)(2,1)}, u32[]{:S(2)}) copy-start(bf16[256,256]{1,0:T(8,128)(2,1)} %q_ref.3) | copy-start | bytes 393220
  0.7 12.0 %copy-start.2 = (bf16[256,128]{1,0:T(8,128)(2,1)S(1)}, bf16[256,128]{1,0:T(8,128)(2,1)}, u32[]{:S(2)}) copy-start(bf16[256,128]{1,0:T(8,128)(2,1)} %k_ref.3) | copy-start | bytes 196612
  0.7 12.0 %copy-start.3 = (bf16[256,128]{1,0:T(8,128)(2,1)S(1)}, bf16[256,128]{1,0:T(8,128)(2,1)}, u32[]{:S(2)}) copy-start(bf16[256,128]{1,0:T(8,128)(2,1)} %v_ref.3) | copy-start | bytes 196612
  1.8 5.5 %collective-permute-start.2 = (bf16[256,128]{1,0:T(8,128)(2,1)S(1)}, bf16[256,128]{1,0:T(8,128)(2,1)S(1)}, u32[]{:S(2)}, u32[]{:S(2)}) collective-permute-start(bf16[256,128]{1,0:T(8,128)(2,1)S(1)} %get-tuple-element.23), channel_id=1, source_target_pairs={{0,2},{2,0},{4,6},{6,4},{8,10},{10,8},{12,14},{14,12},{1,3},{3,1},... | collective-permute-start | bytes 196616 | tf_op jit(solution)/shard_map/ppermute | solution.py:412
  3.9 5.7 %collective-permute-start = (bf16[256,256]{1,0:T(8,128)(2,1)S(1)}, bf16[256,256]{1,0:T(8,128)(2,1)S(1)}, u32[]{:S(2)}, u32[]{:S(2)}) collective-permute-start(bf16[256,256]{1,0:T(8,128)(2,1)S(1)} %get-tuple-element.22), channel_id=1, source_target_pairs={{0,4},{1,7},{2,6},{3,5},{4,8},{5,11},{6,10},{7,9},{8,12},{9,15},{1... | collective-permute-start | bytes 393224 | tf_op jit(solution)/shard_map/ppermute | solution.py:413
  5.2 9.2 %collective-permute-start.6 = (bf16[256,512]{1,0:T(8,128)(2,1)S(1)}, bf16[256,512]{1,0:T(8,128)(2,1)S(1)}, u32[]{:S(2)}, u32[]{:S(2)}) collective-permute-start(bf16[256,512]{1,0:T(8,128)(2,1)S(1)} %get-tuple-element.30), channel_id=1, source_target_pairs={{0,2},{2,0},{4,6},{6,4},{8,10},{10,8},{12,14},{14,12},{1,3},{3,1},... | collective-permute-start | bytes 786440 | tf_op jit(solution)/shard_map/ppermute | solution.py:411
  6.4 0.7 %copy-start.5 = (s32[16]{0:T(128)S(1)}, s32[16]{0:T(128)}, u32[]{:S(2)}) copy-start(s32[16]{0:T(128)} %param.10) | copy-start | bytes 196
  7.3 4.4 %collective-permute-start.3 = (bf16[256,128]{1,0:T(8,128)(2,1)S(1)}, bf16[256,128]{1,0:T(8,128)(2,1)S(1)}, u32[]{:S(2)}, u32[]{:S(2)}) collective-permute-start(bf16[256,128]{1,0:T(8,128)(2,1)S(1)} %collective-permute-done.2.half_ref), channel_id=1, source_target_pairs={{0,1},{1,0},{2,3},{3,2},{4,5},{5,4},{6,7},{7,6},{8,9},{9,8},{10,11... | collective-permute-start | bytes 196616 | tf_op jit(solution)/shard_map/ppermute | solution.py:416
  9.6 3.1 %collective-permute-start.1 = (bf16[1,256,256]{2,1,0:T(8,128)(2,1)S(1)}, bf16[1,256,256]{2,1,0:T(8,128)(2,1)S(1)}, u32[]{:S(2)}, u32[]{:S(2)}) collective-permute-start(bf16[1,256,256]{2,1,0:T(8,128)(2,1)S(1)} %bitcast.18), channel_id=1, source_target_pairs={{0,1},{1,0},{2,3},{3,2},{4,5},{5,4},{6,7},{7,6},{8,9},{9,8},{10,11... | collective-permute-start | bytes 393224 | tf_op jit(solution)/shard_map/ppermute | solution.py:415
  14.1 2.7 %collective-permute-start.4 = (s32[2]{0:T(128)S(1)}, s32[2]{0:T(128)S(1)}, u32[]{:S(2)}, u32[]{:S(2)}) collective-permute-start(s32[2]{0:T(128)S(1)} %get-tuple-element.26), channel_id=1, source_target_pairs={{0,4},{1,3},{2,6},{3,1},{4,0},{5,9},{6,2},{7,11},{8,12},{9,5},{10,... | collective-permute-start | bytes 32 | tf_op jit(solution)/shard_map/ppermute | solution.py:438
  15.5 7.1 %collective-permute-start.9 = (bf16[256,256]{1,0:T(8,128)(2,1)S(1)}, bf16[256,256]{1,0:T(8,128)(2,1)S(1)}, u32[]{:S(2)}, u32[]{:S(2)}) collective-permute-start(bf16[256,256]{1,0:T(8,128)(2,1)S(1)} %bitcast.22), channel_id=1, source_target_pairs={{4,0},{6,2},{8,4},{10,6},{12,8},{14,10},{5,1},{7,3},{9,5},{11,7},{... | collective-permute-start | bytes 393224 | tf_op jit(solution)/shard_map/ppermute | solution.py:467
  16.8 2.1 %collective-permute-start.5 = (s32[2]{0:T(128)S(1)}, s32[2]{0:T(128)S(1)}, u32[]{:S(2)}, u32[]{:S(2)}) collective-permute-start(s32[2]{0:T(128)S(1)} %collective-permute-done.4), channel_id=1, source_target_pairs={{0,1},{1,0},{2,3},{3,2},{4,5},{5,4},{6,7},{7,6},{8,9},{9,8},{10,11... | collective-permute-start | bytes 32 | tf_op jit(solution)/shard_map/ppermute | solution.py:439
  19.5 5.9 %collective-permute-start.7 = (bf16[256,512]{1,0:T(8,128)(2,1)S(1)}, bf16[256,512]{1,0:T(8,128)(2,1)S(1)}, u32[]{:S(2)}, u32[]{:S(2)}) collective-permute-start(bf16[256,512]{1,0:T(8,128)(2,1)S(1)} %get-tuple-element.36), channel_id=1, source_target_pairs={{0,4},{1,3},{2,6},{3,1},{4,0},{5,9},{6,2},{7,11},{8,12},{9,5},{10,... | collective-permute-start | bytes 786440 | tf_op jit(solution)/shard_map/ppermute | solution.py:463
  19.9 8.4 %collective-permute-start.8 = (bf16[256,512]{1,0:T(8,128)(2,1)S(1)}, bf16[256,512]{1,0:T(8,128)(2,1)S(1)}, u32[]{:S(2)}, u32[]{:S(2)}) collective-permute-start(bf16[256,512]{1,0:T(8,128)(2,1)S(1)} %get-tuple-element.37), channel_id=1, source_target_pairs={{0,2},{1,5},{2,0},{3,7},{4,8},{5,1},{6,10},{7,3},{8,4},{9,13},{10,... | collective-permute-start | bytes 786440 | tf_op jit(solution)/shard_map/ppermute | solution.py:464
  22.6 0.8 %copy-start.4 = (s32[2]{0:T(128)S(1)}, s32[2]{0:T(128)}, u32[]{:S(2)}) copy-start(s32[2]{0:T(128)} %plan_ref.1) | copy-start | bytes 28
  22.7 5.7 %collective-permute-start.10 = (f32[256,256]{1,0:T(8,128)S(1)}, f32[256,256]{1,0:T(8,128)S(1)}, u32[]{:S(2)}, u32[]{:S(2)}) collective-permute-start(f32[256,256]{1,0:T(8,128)S(1)} %convert_add_fusion.s_ref), channel_id=1, source_target_pairs={{0,1},{1,0},{2,3},{3,2},{4,5},{5,4},{6,7},{7,6},{8,9},{9,8},{10,11... | collective-permute-start | bytes 786440 | tf_op jit(solution)/shard_map/ppermute | solution.py:468

commit v8 on v7

--- a/solution.py
+++ b/solution.py
@@ -174,11 +174,9 @@
     dots = []
     for i in range(2):
         total = contract(sizes, low, vbuf, p_ref, i) * scale[i]
-        attended = total.T.astype(jnp.bfloat16)
-        for h in range(heads):
-            od_ref[i * CHUNK:(i + 1) * CHUNK, h * head_dim:(h + 1) * head_dim] = (
-                attended[h * CHUNK:(h + 1) * CHUNK])
-        rounded = total.astype(jnp.bfloat16).astype(jnp.float32)
+        attended = total.astype(jnp.bfloat16)
+        od_ref[i * head_dim:(i + 1) * head_dim, :] = attended
+        rounded = attended.astype(jnp.float32)
         dots.append(jnp.sum(g[i].astype(jnp.float32).T * rounded, axis=0, keepdims=True))
 
     def backward(j, carry):
@@ -298,7 +296,11 @@
         plan = scalars(plan_ref, 4)
         for at, column, att, d_ref in ((0, x, att_own, d_own), (tok, 1 - x, att_next, d_next)):
             rows = od_ref.at[at:at + tok, :]
-            rows[:, :width] = att[...]
+            for i in range(2):
+                turned = att[i * head_dim:(i + 1) * head_dim, :].astype(jnp.float32).T
+                for h in range(heads):
+                    rows[i * CHUNK:(i + 1) * CHUNK, h * head_dim:(h + 1) * head_dim] = (
+                        turned[h * CHUNK:(h + 1) * CHUNK].astype(jnp.bfloat16))
             query_grads(sizes, column, kbuf, d_ref, rows)
         for way, out in enumerate((send_a, send_b)):
             flip = (side + way) % 2
@@ -421,7 +423,7 @@
     scores = pltpu.VMEM((2, span, CHUNK, heads * CHUNK), f32)
     buffer = jax.ShapeDtypeStruct(((2 * rounds + 2) * tok, head_dim), bf16)
     rows = jax.ShapeDtypeStruct((tok, 2 * width), bf16)
-    attended = jax.ShapeDtypeStruct((tok, width), bf16)
+    attended = jax.ShapeDtypeStruct((2 * head_dim, heads * CHUNK), bf16)
     grads = jax.ShapeDtypeStruct((span * CHUNK, 2 * heads * CHUNK), bf16)
     key_sums = jax.ShapeDtypeStruct((rounds + 1, tok, 2 * head_dim), f32)
     att_own, d_own, kv_own, kbuf, vbuf = pl.pallas_call(

time: 29.5 us -> 29.6 us (level)
  transfers between devices with their start and end apart: 11 -> 11, of which waited for: 5 -> 5; matrix products, arithmetic and copies ran while one was open for 1% -> 1% of each run, Pallas kernels for 10% -> 11%
where the time goes in v8:
time: 29.6 us; the launch traced here: 29.4 us
  starting transfers between devices  14 us (47%)
  waiting for transfers between devices  8.49 us (29%)
  Pallas kernels  5.18 us (18%)
  between operations  0.75 us (3%)
  local copies, waits for them, and re-layouts  0.7 us (2%)
  other arithmetic  0.31 us (1%)
    ppermute x1, waiting for transfers between devices, per_device(): moved_b = lax.ppermute(send_b, both, tie_b)  2.93 us
    ppermute x1, starting transfers between devices, per_device(): moved_b = lax.ppermute(send_b, both, tie_b)  2.71 us
    ppermute x1, starting transfers between devices, per_device(): half_next = lax.ppermute(half, 'ctx', near)  2.11 us
    ppermute x1, waiting for transfers between devices, per_device(): moved_a = lax.ppermute(send_a, both, tie_a)  2.1 us
    ppermute x1, starting transfers between devices, per_device(): other = lax.ppermute(mine, 'head', cross)  2.09 us
    ppermute x1, waiting for transfers between devices, per_device(): mine = [lax.ppermute(own_kv, both, fetch_pairs(r)) for r in range(rounds)]  1.66 us
    pallas_call x1, Pallas kernels, per_device(): pl.pallas_call(own_kernel(sizes), out_shape=(attended, grads, key_sums, b...  1.37 us
    ppermute x1, starting transfers between devices, per_device(): total = total + lax.ppermute(far[r], 'ctx', back_pairs(r + 1)).astype(f32)  1.29 us
  transfers between devices with their start and end apart: 11, of which 5 were waited for; matrix products, arithmetic and copies ran while one was open for 1% of the time, Pallas kernels for 11%

profile of v8, /device:TPU:1, one launch (start us, length us, event | category | flops | bytes accessed | tf_op | source)
XLA Modules:
  0.0 29.4 jit_solution(10423573449111303620)
XLA Ops:
  0.7 1.1 %pack.1 = (s32[2]{0:T(128)S(1)}, bf16[256,256]{1,0:T(8,128)(2,1)S(1)}, bf16[256,128]{1,0:T(8,128)(2,1)S(1)}, bf16[256,512]{1,0:T(8,128)(2,1)S(1)}) custom-call(s32[2]{0:T(128)} %plan_ref.1, bf16[256,128]{1,0:T(8,128)(2,1)} %k_ref.3, bf16[256,128]{1,0:T(8,128)(2,1)} %v_ref.3, bf16[256,256]{1,0:T(8,128)(2,1)} %q_ref.3, bf16[256,256]{1,0:T(8,128)(2,1)} %g_ref.3), custom_call_target="tpu_custom_call" | custom-call | tf_op jit(solution)/shard_map/pack/pallas_call | solution.py:398
  1.8 2.1 %collective-permute-start.2 = (bf16[256,128]{1,0:T(8,128)(2,1)S(1)}, bf16[256,128]{1,0:T(8,128)(2,1)S(1)}, u32[]{:S(2)}, u32[]{:S(2)}) collective-permute-start(bf16[256,128]{1,0:T(8,128)(2,1)S(1)} %get-tuple-element.23), channel_id=1, source_target_pairs={{0,2},{2,0},{4,6},{6,4},{8,10},{10,8},{12,14},{14,12},{1,3},{3,1},... | collective-permute-start | bytes 196616 | tf_op jit(solution)/shard_map/ppermute | solution.py:414
  3.9 1.3 %collective-permute-start = (bf16[256,256]{1,0:T(8,128)(2,1)S(1)}, bf16[256,256]{1,0:T(8,128)(2,1)S(1)}, u32[]{:S(2)}, u32[]{:S(2)}) collective-permute-start(bf16[256,256]{1,0:T(8,128)(2,1)S(1)} %get-tuple-element.22), channel_id=1, source_target_pairs={{0,4},{1,7},{2,6},{3,5},{4,8},{5,11},{6,10},{7,9},{8,12},{9,15},{1... | collective-permute-start | bytes 393224 | tf_op jit(solution)/shard_map/ppermute | solution.py:415
  5.2 1.2 %collective-permute-start.6 = (bf16[256,512]{1,0:T(8,128)(2,1)S(1)}, bf16[256,512]{1,0:T(8,128)(2,1)S(1)}, u32[]{:S(2)}, u32[]{:S(2)}) collective-permute-start(bf16[256,512]{1,0:T(8,128)(2,1)S(1)} %get-tuple-element.30), channel_id=1, source_target_pairs={{0,2},{2,0},{4,6},{6,4},{8,10},{10,8},{12,14},{14,12},{1,3},{3,1},... | collective-permute-start | bytes 786440 | tf_op jit(solution)/shard_map/ppermute | solution.py:413
  6.4 0.7 %copy-done.5 = s32[16]{0:T(128)S(1)} copy-done((s32[16]{0:T(128)S(1)}, s32[16]{0:T(128)}, u32[]{:S(2)}) %copy-start.5) | copy-done | bytes 88
  7.1 0.1 select_reduce_fusion.2
  7.2 0.1 select_reduce_fusion
  7.3 0.0 collective-permute-done.2.half_ref
  7.3 0.7 %collective-permute-start.3 = (bf16[256,128]{1,0:T(8,128)(2,1)S(1)}, bf16[256,128]{1,0:T(8,128)(2,1)S(1)}, u32[]{:S(2)}, u32[]{:S(2)}) collective-permute-start(bf16[256,128]{1,0:T(8,128)(2,1)S(1)} %collective-permute-done.2.half_ref), channel_id=1, source_target_pairs={{0,1},{1,0},{2,3},{3,2},{4,5},{5,4},{6,7},{7,6},{8,9},{9,8},{10,11... | collective-permute-start | bytes 196616 | tf_op jit(solution)/shard_map/ppermute | solution.py:418
  7.9 1.7 %collective-permute-done = bf16[256,256]{1,0:T(8,128)(2,1)S(1)} collective-permute-done((bf16[256,256]{1,0:T(8,128)(2,1)S(1)}, bf16[256,256]{1,0:T(8,128)(2,1)S(1)}, u32[]{:S(2)}, u32[]{:S(2)}) %collective-permute-start) | collective-permute-done | bytes 131104 | tf_op jit(solution)/shard_map/ppermute | solution.py:415
  9.6 2.1 %collective-permute-start.1 = (bf16[1,256,256]{2,1,0:T(8,128)(2,1)S(1)}, bf16[1,256,256]{2,1,0:T(8,128)(2,1)S(1)}, u32[]{:S(2)}, u32[]{:S(2)}) collective-permute-start(bf16[1,256,256]{2,1,0:T(8,128)(2,1)S(1)} %bitcast.18), channel_id=1, source_target_pairs={{0,1},{1,0},{2,3},{3,2},{4,5},{5,4},{6,7},{7,6},{8,9},{9,8},{10,11... | collective-permute-start | bytes 393224 | tf_op jit(solution)/shard_map/ppermute | solution.py:417
  11.7 0.0 collective-permute-done.3.cross_ref
  11.7 1.0 %collective-permute-done.1.other_ref = bf16[1,256,256]{2,1,0:T(8,128)(2,1)S(1)} collective-permute-done((bf16[1,256,256]{2,1,0:T(8,128)(2,1)S(1)}, bf16[1,256,256]{2,1,0:T(8,128)(2,1)S(1)}, u32[]{:S(2)}, u32[]{:S(2)}) %collective-permute-start.1) | collective-permute-done | bytes 131104 | tf_op jit(solution)/shard_map/ppermute | solution.py:417
  12.7 0.0 copy-done.1
  12.7 1.4 %attend_own.1 = (bf16[256,256]{1,0:T(8,128)(2,1)S(1)}, bf16[768,512]{1,0:T(8,128)(2,1)S(1)}, f32[2,256,256]{2,1,0:T(8,128)S(1)}, bf16[1024,128]{1,0:T(8,128)(2,1)S(1)}, bf16[1024,128]{1,0:T(8,128)(2,1)S(1)}) custom-call(s32[2,256]{1,0:T(2,128)S(1)} %bitcast.21, bf16[256,128]{1,0:T(8,128)(2,1)S(1)} %copy-done.2, bf16[256,128]{1,0:T(8,128)(2,1)S(1)} %copy-done.3, ...), custom_call_target="tpu_custom_call" | custom-call | tf_op jit(solution)/shard_map/attend_own/pallas_call | solution.py:429
  14.1 0.3 %collective-permute-start.4 = (s32[2]{0:T(128)S(1)}, s32[2]{0:T(128)S(1)}, u32[]{:S(2)}, u32[]{:S(2)}) collective-permute-start(s32[2]{0:T(128)S(1)} %get-tuple-element.26), channel_id=1, source_target_pairs={{0,4},{1,3},{2,6},{3,1},{4,0},{5,9},{6,2},{7,11},{8,12},{9,5},{10,... | collective-permute-start | bytes 32 | tf_op jit(solution)/shard_map/ppermute | solution.py:440
  14.4 0.0 collective-permute-done.6.qg_ref
  14.4 1.1 %attend_next.1 = (bf16[256,256]{1,0:T(8,128)(2,1)S(1)}, bf16[768,512]{1,0:T(8,128)(2,1)S(1)}, f32[256,256]{1,0:T(8,128)S(1)}, bf16[1,256,256]{2,1,0:T(8,128)(2,1)S(1)}) custom-call(s32[2,256]{1,0:T(2,128)S(1)} %bitcast.20, bf16[1024,128]{1,0:T(8,128)(2,1)S(1)} %get-tuple-element.27.kbuf, bf16[1024,128]{1,0:T(8,128)(2,1)S(1)} %get-tuple-element.29.vbuf, ...), custom_call_target="tpu_custom_call" | custom-call | tf_op jit(solution)/shard_map/attend_next/pallas_call | solution.py:444
  15.5 1.3 %collective-permute-start.9 = (bf16[256,256]{1,0:T(8,128)(2,1)S(1)}, bf16[256,256]{1,0:T(8,128)(2,1)S(1)}, u32[]{:S(2)}, u32[]{:S(2)}) collective-permute-start(bf16[256,256]{1,0:T(8,128)(2,1)S(1)} %bitcast.22), channel_id=1, source_target_pairs={{4,0},{6,2},{8,4},{10,6},{12,8},{14,10},{5,1},{7,3},{9,5},{11,7},{... | collective-permute-start | bytes 393224 | tf_op jit(solution)/shard_map/ppermute | solution.py:469
  16.8 0.0 collective-permute-done.4
  16.8 1.2 %collective-permute-start.5 = (s32[2]{0:T(128)S(1)}, s32[2]{0:T(128)S(1)}, u32[]{:S(2)}, u32[]{:S(2)}) collective-permute-start(s32[2]{0:T(128)S(1)} %collective-permute-done.4), channel_id=1, source_target_pairs={{0,1},{1,0},{2,3},{3,2},{4,5},{5,4},{6,7},{7,6},{8,9},{9,8},{10,11... | collective-permute-start | bytes 32 | tf_op jit(solution)/shard_map/ppermute | solution.py:441
  18.0 0.8 %collective-permute-done.5 = s32[2]{0:T(128)S(1)} collective-permute-done((s32[2]{0:T(128)S(1)}, s32[2]{0:T(128)S(1)}, u32[]{:S(2)}, u32[]{:S(2)}) %collective-permute-start.5) | collective-permute-done | bytes 40 | tf_op jit(solution)/shard_map/ppermute | solution.py:441
  18.9 0.1 broadcast_select_fusion
  18.9 0.6 %send_rows.1 = (bf16[512,512]{1,0:T(8,128)(2,1)S(1)}, bf16[256,512]{1,0:T(8,128)(2,1)S(1)}, bf16[256,512]{1,0:T(8,128)(2,1)S(1)}) custom-call(s32[1,128]{1,0:T(1,128)S(1)} %pad_bitcast_fusion.plan_ref, bf16[1024,128]{1,0:T(8,128)(2,1)S(1)} %get-tuple-element.27.kbuf, bf16[768,512]{1,0:T(8,128)(2,1)S(1)} %get-tuple-element.28.d_own, ...), custom_call_target="tpu_custom_call" | custom-call | tf_op jit(solution)/shard_map/send_rows/pallas_call | solution.py:456
  19.6 0.4 %collective-permute-start.7 = (bf16[256,512]{1,0:T(8,128)(2,1)S(1)}, bf16[256,512]{1,0:T(8,128)(2,1)S(1)}, u32[]{:S(2)}, u32[]{:S(2)}) collective-permute-start(bf16[256,512]{1,0:T(8,128)(2,1)S(1)} %get-tuple-element.36), channel_id=1, source_target_pairs={{0,4},{1,3},{2,6},{3,1},{4,0},{5,9},{6,2},{7,11},{8,12},{9,5},{10,... | collective-permute-start | bytes 786440 | tf_op jit(solution)/shard_map/ppermute | solution.py:465
  20.0 2.7 %collective-permute-start.8 = (bf16[256,512]{1,0:T(8,128)(2,1)S(1)}, bf16[256,512]{1,0:T(8,128)(2,1)S(1)}, u32[]{:S(2)}, u32[]{:S(2)}) collective-permute-start(bf16[256,512]{1,0:T(8,128)(2,1)S(1)} %get-tuple-element.37), channel_id=1, source_target_pairs={{0,2},{1,5},{2,0},{3,7},{4,8},{5,1},{6,10},{7,3},{8,4},{9,13},{10,... | collective-permute-start | bytes 786440 | tf_op jit(solution)/shard_map/ppermute | solution.py:466
  22.7 0.0 collective-permute-done.9
  22.7 0.7 %collective-permute-start.10 = (f32[256,256]{1,0:T(8,128)S(1)}, f32[256,256]{1,0:T(8,128)S(1)}, u32[]{:S(2)}, u32[]{:S(2)}) collective-permute-start(f32[256,256]{1,0:T(8,128)S(1)} %convert_add_fusion.s_ref), channel_id=1, source_target_pairs={{0,1},{1,0},{2,3},{3,2},{4,5},{5,4},{6,7},{7,6},{8,9},{9,8},{10,11... | collective-permute-start | bytes 786440 | tf_op jit(solution)/shard_map/ppermute | solution.py:470
  23.4 2.1 %collective-permute-done.7.a_ref = bf16[256,512]{1,0:T(8,128)(2,1)S(1)} collective-permute-done((bf16[256,512]{1,0:T(8,128)(2,1)S(1)}, bf16[256,512]{1,0:T(8,128)(2,1)S(1)}, u32[]{:S(2)}, u32[]{:S(2)}) %collective-permute-start.7) | collective-permute-done | bytes 262176 | tf_op jit(solution)/shard_map/ppermute | solution.py:465
  25.5 2.9 %collective-permute-done.8.b_ref = bf16[256,512]{1,0:T(8,128)(2,1)S(1)} collective-permute-done((bf16[256,512]{1,0:T(8,128)(2,1)S(1)}, bf16[256,512]{1,0:T(8,128)(2,1)S(1)}, u32[]{:S(2)}, u32[]{:S(2)}) %collective-permute-start.8) | collective-permute-done | bytes 262176 | tf_op jit(solution)/shard_map/ppermute | solution.py:466
  28.4 0.0 collective-permute-done.10.t_ref
  28.4 1.0 %place.1 = (bf16[256,256]{1,0:T(8,128)(2,1)}, f32[256,256]{1,0:T(8,128)}, f32[256,128]{1,0:T(8,128)}, f32[256,128]{1,0:T(8,128)}) custom-call(s32[1,128]{1,0:T(1,128)S(1)} %pad_bitcast_fusion.1.plan_ref, bf16[512,512]{1,0:T(8,128)(2,1)S(1)} %get-tuple-element.35.row_ref, bf16[256,512]{1,0:T(8,128)(2,1)S(1)} %collective-permute-done.7.a_ref, ...), custom_call_target="tpu_custom_call" | custom-call | tf_op jit(solution)/shard_map/place/pallas_call | solution.py:472
  (18 shorter events, 0.1 us)
Async XLA Ops:
  0.6 12.1 %copy-start.1 = (bf16[256,256]{1,0:T(8,128)(2,1)S(1)}, bf16[256,256]{1,0:T(8,128)(2,1)}, u32[]{:S(2)}) copy-start(bf16[256,256]{1,0:T(8,128)(2,1)} %g_ref.3) | copy-start | bytes 393220
  0.6 12.0 %copy-start = (bf16[256,256]{1,0:T(8,128)(2,1)S(1)}, bf16[256,256]{1,0:T(8,128)(2,1)}, u32[]{:S(2)}) copy-start(bf16[256,256]{1,0:T(8,128)(2,1)} %q_ref.3) | copy-start | bytes 393220
  0.7 12.0 %copy-start.2 = (bf16[256,128]{1,0:T(8,128)(2,1)S(1)}, bf16[256,128]{1,0:T(8,128)(2,1)}, u32[]{:S(2)}) copy-start(bf16[256,128]{1,0:T(8,128)(2,1)} %k_ref.3) | copy-start | bytes 196612
  0.7 12.0 %copy-start.3 = (bf16[256,128]{1,0:T(8,128)(2,1)S(1)}, bf16[256,128]{1,0:T(8,128)(2,1)}, u32[]{:S(2)}) copy-start(bf16[256,128]{1,0:T(8,128)(2,1)} %v_ref.3) | copy-start | bytes 196612
  1.8 5.5 %collective-permute-start.2 = (bf16[256,128]{1,0:T(8,128)(2,1)S(1)}, bf16[256,128]{1,0:T(8,128)(2,1)S(1)}, u32[]{:S(2)}, u32[]{:S(2)}) collective-permute-start(bf16[256,128]{1,0:T(8,128)(2,1)S(1)} %get-tuple-element.23), channel_id=1, source_target_pairs={{0,2},{2,0},{4,6},{6,4},{8,10},{10,8},{12,14},{14,12},{1,3},{3,1},... | collective-permute-start | bytes 196616 | tf_op jit(solution)/shard_map/ppermute | solution.py:414
  3.9 5.7 %collective-permute-start = (bf16[256,256]{1,0:T(8,128)(2,1)S(1)}, bf16[256,256]{1,0:T(8,128)(2,1)S(1)}, u32[]{:S(2)}, u32[]{:S(2)}) collective-permute-start(bf16[256,256]{1,0:T(8,128)(2,1)S(1)} %get-tuple-element.22), channel_id=1, source_target_pairs={{0,4},{1,7},{2,6},{3,5},{4,8},{5,11},{6,10},{7,9},{8,12},{9,15},{1... | collective-permute-start | bytes 393224 | tf_op jit(solution)/shard_map/ppermute | solution.py:415
  5.2 9.2 %collective-permute-start.6 = (bf16[256,512]{1,0:T(8,128)(2,1)S(1)}, bf16[256,512]{1,0:T(8,128)(2,1)S(1)}, u32[]{:S(2)}, u32[]{:S(2)}) collective-permute-start(bf16[256,512]{1,0:T(8,128)(2,1)S(1)} %get-tuple-element.30), channel_id=1, source_target_pairs={{0,2},{2,0},{4,6},{6,4},{8,10},{10,8},{12,14},{14,12},{1,3},{3,1},... | collective-permute-start | bytes 786440 | tf_op jit(solution)/shard_map/ppermute | solution.py:413
  6.4 0.7 %copy-start.5 = (s32[16]{0:T(128)S(1)}, s32[16]{0:T(128)}, u32[]{:S(2)}) copy-start(s32[16]{0:T(128)} %param.10) | copy-start | bytes 196
  7.3 4.4 %collective-permute-start.3 = (bf16[256,128]{1,0:T(8,128)(2,1)S(1)}, bf16[256,128]{1,0:T(8,128)(2,1)S(1)}, u32[]{:S(2)}, u32[]{:S(2)}) collective-permute-start(bf16[256,128]{1,0:T(8,128)(2,1)S(1)} %collective-permute-done.2.half_ref), channel_id=1, source_target_pairs={{0,1},{1,0},{2,3},{3,2},{4,5},{5,4},{6,7},{7,6},{8,9},{9,8},{10,11... | collective-permute-start | bytes 196616 | tf_op jit(solution)/shard_map/ppermute | solution.py:418
  9.6 3.1 %collective-permute-start.1 = (bf16[1,256,256]{2,1,0:T(8,128)(2,1)S(1)}, bf16[1,256,256]{2,1,0:T(8,128)(2,1)S(1)}, u32[]{:S(2)}, u32[]{:S(2)}) collective-permute-start(bf16[1,256,256]{2,1,0:T(8,128)(2,1)S(1)} %bitcast.18), channel_id=1, source_target_pairs={{0,1},{1,0},{2,3},{3,2},{4,5},{5,4},{6,7},{7,6},{8,9},{9,8},{10,11... | collective-permute-start | bytes 393224 | tf_op jit(solution)/shard_map/ppermute | solution.py:417
  14.1 2.7 %collective-permute-start.4 = (s32[2]{0:T(128)S(1)}, s32[2]{0:T(128)S(1)}, u32[]{:S(2)}, u32[]{:S(2)}) collective-permute-start(s32[2]{0:T(128)S(1)} %get-tuple-element.26), channel_id=1, source_target_pairs={{0,4},{1,3},{2,6},{3,1},{4,0},{5,9},{6,2},{7,11},{8,12},{9,5},{10,... | collective-permute-start | bytes 32 | tf_op jit(solution)/shard_map/ppermute | solution.py:440
  15.5 7.2 %collective-permute-start.9 = (bf16[256,256]{1,0:T(8,128)(2,1)S(1)}, bf16[256,256]{1,0:T(8,128)(2,1)S(1)}, u32[]{:S(2)}, u32[]{:S(2)}) collective-permute-start(bf16[256,256]{1,0:T(8,128)(2,1)S(1)} %bitcast.22), channel_id=1, source_target_pairs={{4,0},{6,2},{8,4},{10,6},{12,8},{14,10},{5,1},{7,3},{9,5},{11,7},{... | collective-permute-start | bytes 393224 | tf_op jit(solution)/shard_map/ppermute | solution.py:469
  16.8 2.1 %collective-permute-start.5 = (s32[2]{0:T(128)S(1)}, s32[2]{0:T(128)S(1)}, u32[]{:S(2)}, u32[]{:S(2)}) collective-permute-start(s32[2]{0:T(128)S(1)} %collective-permute-done.4), channel_id=1, source_target_pairs={{0,1},{1,0},{2,3},{3,2},{4,5},{5,4},{6,7},{7,6},{8,9},{9,8},{10,11... | collective-permute-start | bytes 32 | tf_op jit(solution)/shard_map/ppermute | solution.py:441
  19.6 5.9 %collective-permute-start.7 = (bf16[256,512]{1,0:T(8,128)(2,1)S(1)}, bf16[256,512]{1,0:T(8,128)(2,1)S(1)}, u32[]{:S(2)}, u32[]{:S(2)}) collective-permute-start(bf16[256,512]{1,0:T(8,128)(2,1)S(1)} %get-tuple-element.36), channel_id=1, source_target_pairs={{0,4},{1,3},{2,6},{3,1},{4,0},{5,9},{6,2},{7,11},{8,12},{9,5},{10,... | collective-permute-start | bytes 786440 | tf_op jit(solution)/shard_map/ppermute | solution.py:465
  20.0 8.4 %collective-permute-start.8 = (bf16[256,512]{1,0:T(8,128)(2,1)S(1)}, bf16[256,512]{1,0:T(8,128)(2,1)S(1)}, u32[]{:S(2)}, u32[]{:S(2)}) collective-permute-start(bf16[256,512]{1,0:T(8,128)(2,1)S(1)} %get-tuple-element.37), channel_id=1, source_target_pairs={{0,2},{1,5},{2,0},{3,7},{4,8},{5,1},{6,10},{7,3},{8,4},{9,13},{10,... | collective-permute-start | bytes 786440 | tf_op jit(solution)/shard_map/ppermute | solution.py:466
  22.7 0.7 %copy-start.4 = (s32[2]{0:T(128)S(1)}, s32[2]{0:T(128)}, u32[]{:S(2)}) copy-start(s32[2]{0:T(128)} %plan_ref.1) | copy-start | bytes 28
  22.7 5.7 %collective-permute-start.10 = (f32[256,256]{1,0:T(8,128)S(1)}, f32[256,256]{1,0:T(8,128)S(1)}, u32[]{:S(2)}, u32[]{:S(2)}) collective-permute-start(f32[256,256]{1,0:T(8,128)S(1)} %convert_add_fusion.s_ref), channel_id=1, source_target_pairs={{0,1},{1,0},{2,3},{3,2},{4,5},{5,4},{6,7},{7,6},{8,9},{9,8},{10,11... | collective-permute-start | bytes 786440 | tf_op jit(solution)/shard_map/ppermute | solution.py:470
